TPU v7x, 128 devices: a whole 4x4x4 slice. The times are simulated.
128 devices in a mesh: gx: 8 (over z_hi, y), gy: 8 (over z_lo, x), gz: 2 (over core).
Axes of the slice: x: 4, y: 4, z: 4 (z_hi: 2, z_lo: 2; z = z_hi * 2 + z_lo), core: 2. Of those that a mesh axis runs over, the one named last changes fastest.
Arguments:
- state: bfloat16 [32, 128, 128, 256], P('gx', ('gy', 'gz')), may hold values from -6 to 6
- cotangent: bfloat16 [32, 128, 128, 256], P('gx', ('gy', 'gz')), may hold values from -6 to 6
- factors: bfloat16 [262144, 256], P(('gx', 'gy', 'gz')), may hold values from -0.25 to 0.25
- speeds: float32 [3, 262144], P(None, ('gx', 'gy', 'gz')), may hold values from 0.25 to 4
- signs: int32 [3, 262144], P(None, ('gx', 'gy', 'gz')), may hold values from 0 to 1, as said below
- mask: int32 [32, 128, 128], P('gx', ('gy', 'gz')), may hold values 0 or 1
Outputs:
- grad_state: bfloat16 [32, 128, 128, 256], P('gx', ('gy', 'gz'))
- grad_factors: float32 [262144, 256], P(('gx', 'gy', 'gz'))
Inputs may be any that keep to these rules, and one draw needn't show every extreme that they name: `signs`: 1 where the velocity component points towards higher indices, else 0. `mask`: 1 where a cell is updated, 0 where it is held fixed.
All inputs are finite; a program needn't handle non-finite values. No bound on the sum of `mask` on one device may be relied on, other than what follows from the above.
Results may differ from a plain program's by a relative error of at most 0.0068.
Values may be sent and summed in bfloat16 or wider, within the bound.
No kernel may reach another device: no remote copies, remote signals or barrier semaphores. Data moves between devices by JAX's collectives and lax.ppermute only.
A program may use at most 128 MiB of HBM per device.

v0:
```python
import jax
import jax.numpy as jnp
from jax import lax
from jax.sharding import PartitionSpec as P

courant = 0.2


def with_halo(block, sides, width):
    for axis, dim in sides:
        count = lax.axis_size(axis)
        forward = [(i, i + 1) for i in range(count - 1)]
        backward = [(target, source) for source, target in forward]
        low = lax.ppermute(
            lax.slice_in_dim(block, block.shape[dim] - width, None, axis=dim), axis, forward
        )
        high = lax.ppermute(lax.slice_in_dim(block, 0, width, axis=dim), axis, backward)
        block = jnp.concatenate([low, block, high], axis=dim)
    return block


def build_rates(speeds, signs):
    chosen = signs.astype(jnp.float32)
    rate_rows = []
    for direction in range(3):
        rate_rows.append(speeds[direction] * chosen[direction])
        rate_rows.append(speeds[direction] * (1.0 - chosen[direction]))
    return jnp.stack(rate_rows)


def neighbour_pairs(padded):
    centre = padded[1:-1, 1:-1].astype(jnp.float32)
    rank_size = centre.shape[-1]
    zero_face = jnp.zeros_like(centre[:, :, :1])
    sides = (
        (padded[:-2, 1:-1], padded[2:, 1:-1]),
        (padded[1:-1, :-2], padded[1:-1, 2:]),
        (
            jnp.concatenate([zero_face, centre[:, :, :-1]], axis=2),
            jnp.concatenate([centre[:, :, 1:], zero_face], axis=2),
        ),
    )
    diff_pairs = []
    for lower_side, upper_side in sides:
        lower_diff = (centre - lower_side.astype(jnp.float32)).astype(jnp.bfloat16)
        upper_diff = (upper_side.astype(jnp.float32) - centre).astype(jnp.bfloat16)
        diff_pairs.append(
            jnp.concatenate([lower_diff, upper_diff], axis=-1).reshape(-1, 2 * rank_size)
        )
    return diff_pairs


def backward_terms(diff_pairs, partner, back_mats):
    grid_shape = partner.shape
    flat_partner = partner.reshape(-1, grid_shape[-1])
    running = None
    flux_grads = []
    for direction in range(3):
        term = jnp.dot(
            diff_pairs[direction], back_mats[direction], preferred_element_type=jnp.float32
        )
        running = term if direction == 0 else running + term
        flux_grads.append(
            lax.dot_general(
                flat_partner,
                diff_pairs[direction],
                (((0,), (0,)), ((), ())),
                preferred_element_type=jnp.float32,
            )
        )
    return (courant * running.reshape(grid_shape), flux_grads)


def on_device(state, cotangent, factors, speeds, signs, mask):
    grid_shape = state.shape
    rank_size = grid_shape[-1]
    rate_table = build_rates(speeds, signs)
    weighted = (rate_table[:, :, None] * factors.astype(jnp.float32)[None]).astype(jnp.bfloat16)
    gram_local = jnp.einsum("vj,kvl->kjl", factors, weighted, preferred_element_type=jnp.float32)
    flux_sum = lax.psum(gram_local, ("gx", "gy", "gz"))
    flux_bf = flux_sum.astype(jnp.bfloat16)
    cell_gate = mask.astype(jnp.float32)[..., None]
    held_back = cotangent * mask.astype(jnp.bfloat16)[..., None]
    padded_state = with_halo(state, (("gx", 0), (("gy", "gz"), 1)), 1)
    padded_held = with_halo(held_back, (("gx", 0), (("gy", "gz"), 1)), 1)
    forward_mats = [
        jnp.concatenate([flux_bf[2 * direction], -flux_bf[2 * direction + 1]], axis=0)
        for direction in range(3)
    ]
    back_mats = [
        jnp.concatenate([-flux_bf[2 * direction + 1].T, flux_bf[2 * direction].T], axis=0)
        for direction in range(3)
    ]
    state_pairs = neighbour_pairs(padded_state)
    flow_term = None
    for direction in range(3):
        term = jnp.dot(
            state_pairs[direction], forward_mats[direction], preferred_element_type=jnp.float32
        )
        flow_term = term if direction == 0 else flow_term + term
    flow_term = -courant * flow_term.reshape(grid_shape)
    middle = (state.astype(jnp.float32) + cell_gate * flow_term).astype(jnp.bfloat16)
    back_held, grads_held = backward_terms(neighbour_pairs(padded_held), middle, back_mats)
    inner_grad = 0.5 * cotangent.astype(jnp.float32) + 0.5 * back_held
    held_inner = (cell_gate * inner_grad).astype(jnp.bfloat16)
    padded_inner = with_halo(held_inner, (("gx", 0), (("gy", "gz"), 1)), 1)
    back_inner, grads_inner = backward_terms(neighbour_pairs(padded_inner), state, back_mats)
    grad_state = (0.5 * cotangent.astype(jnp.float32) + inner_grad + back_inner).astype(
        jnp.bfloat16
    )
    flux_grad = []
    for direction in range(3):
        flux_grad.append(
            courant
            * (grads_inner[direction][:, rank_size:] + 0.5 * grads_held[direction][:, rank_size:])
        )
        flux_grad.append(
            -courant
            * (grads_inner[direction][:, :rank_size] + 0.5 * grads_held[direction][:, :rank_size])
        )
    local_grad = jnp.stack(flux_grad)
    total_grad = lax.psum(local_grad, ("gx", "gy", "gz"))
    symmetric = (total_grad + jnp.swapaxes(total_grad, 1, 2)).astype(jnp.bfloat16)
    grad_factors = jnp.einsum(
        "kvj,kjl->vl", weighted, symmetric, preferred_element_type=jnp.float32
    )
    return (grad_state, grad_factors)


def solution(mesh):
    placed = (
        P("gx", ("gy", "gz"), None, None),
        P("gx", ("gy", "gz"), None, None),
        P(("gx", "gy", "gz"), None),
        P(None, ("gx", "gy", "gz")),
        P(None, ("gx", "gy", "gz")),
        P("gx", ("gy", "gz"), None),
    )
    return jax.shard_map(
        on_device,
        mesh=mesh,
        in_specs=placed,
        out_specs=(P("gx", ("gy", "gz"), None, None), P(("gx", "gy", "gz"), None)),
        check_vma=False,
    )
```

profile of v0, /device:TPU:1, one launch (start us, length us, event | category | flops | bytes accessed | tf_op | source)
XLA Modules:
  0.0 413.2 jit_solution(12088359582028968462)
XLA Ops:
  7.2 2.4 fusion.86
  9.6 4.8 %collective-permute-start.8 = (bf16[1,8,128,256]{3,2,1,0:T(8,128)(2,1)}, bf16[1,8,128,256]{3,2,1,0:T(8,128)(2,1)}, u32[]{:S(2)}, u32[]{:S(2)}) collective-permute-start(bf16[1,8,128,256]{3,2,1,0:T(8,128)(2,1)} %get-tuple-element.28), channel_id=1, source_target_pairs={{0,16},{16,32},{32,48},{48,64},{64,80},{80,96},{96,112},{1,17},{17... | collective-permute-start | bytes 1572872 | tf_op jit(solution)/shard_map/ppermute | solution.py:14
  16.5 1.9 broadcast_multiply_fusion
  19.5 4.0 collective-permute-start
  25.0 4.1 %fusion.85 = (f32[4,8,127,256]{3,2,1,0:T(8,128)}, f32[4,8,127,256]{3,2,1,0:T(8,128)}) fusion(bf16[4,8,128,256]{3,2,1,0:T(8,128)(2,1)S(1)} %copy-done), kind=kLoop, calls=%fused_computation.184 | loop fusion | bytes 16646144 | tf_op jit(solution)/shard_map/slice | solution.py:39
  29.2 1.5 convert_element_type.142
  31.4 6.5 %fusion.30 = f32[6,256,256]{1,2,0:T(8,128)} fusion(f32[2048,256]{1,0:T(8,128)} %convert_element_type.142, f32[6,2048]{1,0:T(8,128)S(1)} %stack.30, bf16[2048,256]{1,0:T(8,128)(2,1)} %param.8), kind=kOutput, calls=%fused_computation.89 | convolution fusion | flops 1616904192 | bytes 4767744 | tf_op jit(solution)/shard_map/vj,kvl->kjl/dot_general | solution.py:79
  38.0 78.6 %all-reduce.10 = bf16[6,256,256]{1,2,0:T(8,128)(2,1)S(1)} all-reduce(f32[6,256,256]{1,2,0:T(8,128)} %fusion.30), channel_id=1, replica_groups=mesh['gx'=8,'gy'=8,'gz'=2] {'gx','gy','gz'}, use_global_device_ids=true, to_apply=%region_0.0 | all-reduce | flops 393216 | bytes 2359296 | tf_op jit(solution)/shard_map/psum | solution.py:80
  116.6 4.2 %fusion.89 = (f32[4,8,127,256]{3,2,1,0:T(8,128)}, f32[4,8,127,256]{3,2,1,0:T(8,128)}) fusion(bf16[4,8,128,256]{3,2,1,0:T(8,128)(2,1)S(1)} %broadcast_multiply_fusion), kind=kLoop, calls=%fused_computation.188 | loop fusion | bytes 16646144 | tf_op jit(solution)/shard_map/slice | solution.py:39
  120.8 3.9 copy.24
  125.9 1.9 constant_dynamic-update-slice_fusion.1
  128.9 2.7 collective-permute-start.10
  131.6 2.2 collective-permute-start.11
  135.0 1.9 pad_maximum_fusion.34
  136.9 3.5 collective-permute-start.2
  140.4 2.4 collective-permute-start.3
  143.7 6.8 %fusion.22 = (bf16[4,8,128,256]{3,2,1,0:T(8,128)(2,1)S(1)}, bf16[4,8,128,256]{3,2,1,0:T(8,128)(2,1)S(1)}, bf16[4,8,128,256]{3,2,1,0:T(8,128)(2,1)S(1)}, bf16[4,8...) fusion(bf16[4,8,128,256]{3,2,1,0:T(8,128)(2,1)S(1)} %copy-done.1, ...), kind=kLoop, calls=%fused_computation.48 | loop fusion | flops 22020096 | bytes 27983872 | tf_op jit(solution)/shard_map/convert_element_type | solution.py:45
  157.9 1.7 fusion.26
  162.4 5.9 %fusion.12 = (bf16[4,8,128,256]{3,2,1,0:T(8,128)(2,1)S(1)}, bf16[4,8,128,256]{3,2,1,0:T(8,128)(2,1)S(1)}, bf16[4,8,128,256]{3,2,1,0:T(8,128)(2,1)S(1)}, bf16[4,8...) fusion(bf16[4,8,128,256]{3,2,1,0:T(8,128)(2,1)S(1)} %broadcast_multiply_fusion, ...), kind=kLoop, calls=%fused_computation.38 | loop fusion | flops 26214400 | bytes 24838144 | tf_op jit(solution)/shard_map/convert_element_type | solution.py:45
  168.8 2.7 copy-done.27
  171.5 2.6 convolution_bitcast_fusion
  177.7 3.4 fusion.7
  181.1 5.3 %copy.26 = f32[4,8,128,256]{2,3,1,0:T(8,128)} copy(f32[4,8,128,256]{3,2,1,0:T(8,128)} %bitcast.129) | data formatting | bytes 8388608 | tf_op jit(solution)/shard_map/mul | solution.py:104
  186.4 3.9 multiply_convert_fusion.3
  190.4 2.4 collective-permute-start.4
  194.2 2.6 convolution_bitcast_fusion.2
  197.9 5.6 %collective-permute-done.4 = bf16[1,8,128,256]{2,3,1,0:T(8,128)(2,1)S(1)} collective-permute-done((bf16[1,8,128,256]{2,3,1,0:T(8,128)(2,1)S(1)}, bf16[1,8,128,256]{2,3,1,0:T(8,128)(2,1)S(1)}, u32[]{:S(2)}, u32[]{:S(2)}) %collective-permute-start.4) | collective-permute-done | bytes 524320 | tf_op jit(solution)/shard_map/ppermute | solution.py:14
  203.5 4.1 collective-permute-done.5
  207.8 3.5 collective-permute-start.6
  211.3 1.9 collective-permute-start.7
  213.2 2.6 convolution_bitcast_fusion.4
  216.0 4.4 %collective-permute-done.7 = bf16[6,1,128,256]{2,3,1,0:T(8,128)(2,1)S(1)} collective-permute-done((bf16[6,1,128,256]{2,3,1,0:T(8,128)(2,1)S(1)}, bf16[6,1,128,256]{2,3,1,0:T(8,128)(2,1)S(1)}, u32[]{:S(2)}, u32[]{:S(2)}) %collective-permute-start.7) | collective-permute-done | bytes 393248 | tf_op jit(solution)/shard_map/ppermute | solution.py:17
  221.1 6.2 %fusion.18 = (bf16[4,8,128,256]{2,3,1,0:T(8,128)(2,1)}, bf16[4,8,128,256]{2,3,1,0:T(8,128)(2,1)}, bf16[4,8,128,256]{2,3,1,0:T(8,128)(2,1)S(1)}, bf16[4,8,128,256...) fusion(bf16[4,8,128,256]{2,3,1,0:T(8,128)(2,1)S(1)} %multiply_convert_fusion.3, ...), kind=kLoop, calls=%fused_computation.44 | loop fusion | flops 26214400 | bytes 24838144 | tf_op jit(solution)/shard_map/convert_element_type | solution.py:45
  227.4 3.6 convolution_bitcast_fusion.1
  231.1 2.5 pad_maximum_fusion.5
  234.8 2.2 pad_maximum_fusion.4
  238.3 2.4 pad_maximum_fusion.3
  242.2 6.2 %copy.29 = bf16[4,8,128,512]{3,2,1,0:T(8,128)(2,1)} copy(bf16[4,8,128,512]{2,3,1,0:T(8,128)(2,1)} %pad_maximum_fusion.5) | data formatting | bytes 8388608 | tf_op jit(solution)/shard_map/concatenate | solution.py:48
  248.4 6.2 %copy.28 = bf16[4,8,128,512]{3,2,1,0:T(8,128)(2,1)} copy(bf16[4,8,128,512]{2,3,1,0:T(8,128)(2,1)} %pad_maximum_fusion.4) | data formatting | bytes 8388608 | tf_op jit(solution)/shard_map/concatenate | solution.py:48
  254.6 6.3 %copy.27 = bf16[4,8,128,512]{3,2,1,0:T(8,128)(2,1)} copy(bf16[4,8,128,512]{2,3,1,0:T(8,128)(2,1)} %pad_maximum_fusion.3) | data formatting | bytes 8388608 | tf_op jit(solution)/shard_map/concatenate | solution.py:48
  260.9 3.6 fusion.67
  266.8 3.4 fusion.6
  270.2 5.5 %copy.30 = f32[4,8,128,256]{2,3,1,0:T(8,128)} copy(f32[4,8,128,256]{3,2,1,0:T(8,128)} %bitcast.128) | data formatting | bytes 8388608 | tf_op jit(solution)/shard_map/mul | solution.py:71
  275.7 5.9 %add_convert_fusion = bf16[4,8,128,256]{2,3,1,0:T(8,128)(2,1)} fusion(f32[4,8,128,256]{2,3,1,0:T(8,128)} %copy.30, bf16[4,8,128,256]{2,3,1,0:T(8,128)(2,1)S(1)} %copy-done.5, f32[4,8,128,256]{2,3,1,0:T(8,128)} %copy.26), kind=kLoop, calls=%fused_computation.62 | loop fusion | flops 6291456 | bytes 12582912 | tf_op jit(solution)/shard_map/convert_element_type | solution.py:108
  281.6 4.1 copy.42
  285.7 112.4 %all-reduce.9.cloned.1.call-done = f32[6,256,256]{1,2,0:T(8,128)} async-done(((f32[6,256,256]{1,2,0:T(8,128)}), f32[6,256,256]{1,2,0:T(8,128)}) %all-reduce.9.cloned.1.call-update) | async-done | bytes 1572880 | tf_op jit(solution)/shard_map/psum | solution.py:122
  398.1 3.1 copy.40
  401.2 4.9 %fusion.28 = f32[2048,256]{1,0:T(8,128)} fusion(f32[2048,256]{1,0:T(8,128)S(1)} %copy-done.26, f32[6,2048]{1,0:T(8,128)S(1)} %copy-done.57, f32[6,256,256]{1,2,0:T(8,128)} %all-reduce.9.cloned.1.call-done, f32[6,256,256]{2,1,0:T(8,128)} %copy.40), kind=kOutput, calls=%fused_computation.66 | convolution fusion | flops 1617690624 | bytes 7389184 | tf_op jit(solution)/shard_map/kvj,kjl->vl/dot_general | solution.py:124
  (166 shorter events, 33.4 us)
Async XLA Ops:
  7.2 391.0 %all-reduce.9.cloned.1.call-start = ((), (), s32[]{:S(2)}) async-start(), calls=%async_computation | async-start | bytes 3145728 | tf_op jit(solution)/shard_map/psum | solution.py:122
  7.2 17.8 %copy-start = (bf16[4,8,128,256]{3,2,1,0:T(8,128)(2,1)S(1)}, bf16[4,8,128,256]{3,2,1,0:T(8,128)(2,1)}, u32[]{:S(2)}) copy-start(bf16[4,8,128,256]{3,2,1,0:T(8,128)(2,1)} %param.6) | copy-start | bytes 6291460
  9.6 115.1 %collective-permute-start.8 = (bf16[1,8,128,256]{3,2,1,0:T(8,128)(2,1)}, bf16[1,8,128,256]{3,2,1,0:T(8,128)(2,1)}, u32[]{:S(2)}, u32[]{:S(2)}) collective-permute-start(bf16[1,8,128,256]{3,2,1,0:T(8,128)(2,1)} %get-tuple-element.28), channel_id=1, source_target_pairs={{0,16},{16,32},{32,48},{48,64},{64,80},{80,96},{96,112},{1,17},{17... | collective-permute-start | bytes 1572872 | tf_op jit(solution)/shard_map/ppermute | solution.py:14
  14.4 113.3 %collective-permute-start.9 = (bf16[1,8,128,256]{3,2,1,0:T(8,128)(2,1)}, bf16[1,8,128,256]{3,2,1,0:T(8,128)(2,1)}, u32[]{:S(2)}, u32[]{:S(2)}) collective-permute-start(bf16[1,8,128,256]{3,2,1,0:T(8,128)(2,1)} %get-tuple-element.29), channel_id=1, source_target_pairs={{16,0},{32,16},{48,32},{64,48},{80,64},{96,80},{112,96},{17,1},{33... | collective-permute-start | bytes 1572872 | tf_op jit(solution)/shard_map/ppermute | solution.py:17
  19.5 115.5 %collective-permute-start = (bf16[1,8,128,256]{3,2,1,0:T(8,128)(2,1)}, bf16[1,8,128,256]{3,2,1,0:T(8,128)(2,1)S(1)}, u32[]{:S(2)}, u32[]{:S(2)}) collective-permute-start(bf16[1,8,128,256]{3,2,1,0:T(8,128)(2,1)} %get-tuple-element.48), channel_id=1, source_target_pairs={{0,16},{16,32},{32,48},{48,64},{64,80},{80,96},{96,112},{1,17},{17... | collective-permute-start | bytes 1572872 | tf_op jit(solution)/shard_map/ppermute | solution.py:14
  23.6 5.6 %copy-start.59 = (s32[3,2048]{1,0:T(4,128)S(1)}, s32[3,2048]{1,0:T(4,128)}, u32[]{:S(2)}) copy-start(s32[3,2048]{1,0:T(4,128)} %param.10) | copy-start | bytes 73732
  23.6 5.6 %copy-start.41 = (bf16[2048,256]{1,0:T(8,128)(2,1)S(1)}, bf16[2048,256]{1,0:T(8,128)(2,1)}, u32[]{:S(2)}) copy-start(bf16[2048,256]{1,0:T(8,128)(2,1)} %param.8) | copy-start | bytes 3145732
  23.6 7.1 %copy-start.60 = (f32[3,2048]{1,0:T(4,128)S(1)}, f32[3,2048]{1,0:T(4,128)}, u32[]{:S(2)}) copy-start(f32[3,2048]{1,0:T(4,128)} %param.9) | copy-start | bytes 73732
  23.6 111.4 %collective-permute-start.1 = (bf16[1,8,128,256]{3,2,1,0:T(8,128)(2,1)}, bf16[1,8,128,256]{3,2,1,0:T(8,128)(2,1)}, u32[]{:S(2)}, u32[]{:S(2)}) collective-permute-start(bf16[1,8,128,256]{3,2,1,0:T(8,128)(2,1)} %get-tuple-element.49), channel_id=1, source_target_pairs={{16,0},{32,16},{48,32},{64,48},{80,64},{96,80},{112,96},{17,1},{33... | collective-permute-start | bytes 1572872 | tf_op jit(solution)/shard_map/ppermute | solution.py:17
  120.8 3.9 copy-start.58
  125.8 17.8 %copy-start.9 = (f32[4,8,127,256]{3,2,1,0:T(8,128)S(1)}, f32[4,8,127,256]{3,2,1,0:T(8,128)}, u32[]{:S(2)}) copy-start(f32[4,8,127,256]{3,2,1,0:T(8,128)} %get-tuple-element.24) | copy-start | bytes 12484612
  128.8 14.0 %copy-start.22 = (bf16[6,8,128,256]{3,2,1,0:T(8,128)(2,1)}, bf16[6,8,128,256]{3,2,1,0:T(8,128)(2,1)S(1)}, u32[]{:S(2)}) copy-start(bf16[6,8,128,256]{3,2,1,0:T(8,128)(2,1)S(1)} %constant_dynamic-update-slice_fusion) | copy-start | bytes 9437188
  128.9 14.8 %copy-start.1 = (bf16[4,8,128,256]{3,2,1,0:T(8,128)(2,1)S(1)}, bf16[4,8,128,256]{3,2,1,0:T(8,128)(2,1)}, u32[]{:S(2)}) copy-start(bf16[4,8,128,256]{3,2,1,0:T(8,128)(2,1)} %param.6) | copy-start | bytes 6291460
  128.9 14.8 %copy-start.8 = (f32[4,8,127,256]{3,2,1,0:T(8,128)S(1)}, f32[4,8,127,256]{3,2,1,0:T(8,128)}, u32[]{:S(2)}) copy-start(f32[4,8,127,256]{3,2,1,0:T(8,128)} %get-tuple-element.23) | copy-start | bytes 12484612
  128.9 13.8 %collective-permute-start.10 = (bf16[6,1,128,256]{3,2,1,0:T(8,128)(2,1)S(1)}, bf16[6,1,128,256]{3,2,1,0:T(8,128)(2,1)S(1)}, u32[]{:S(2)}, u32[]{:S(2)}) collective-permute-start(bf16[6,1,128,256]{3,2,1,0:T(8,128)(2,1)S(1)} %get-tuple-element.8), channel_id=1, source_target_pairs={{0,1},{1,2},{2,3},{3,4},{4,5},{5,6},{6,7},{7,8},{8,9},{9,10},{10,1... | collective-permute-start | bytes 1179656 | tf_op jit(solution)/shard_map/ppermute | solution.py:14
  131.6 11.2 %collective-permute-start.11 = (bf16[6,1,128,256]{3,2,1,0:T(8,128)(2,1)S(1)}, bf16[6,1,128,256]{3,2,1,0:T(8,128)(2,1)S(1)}, u32[]{:S(2)}, u32[]{:S(2)}) collective-permute-start(bf16[6,1,128,256]{3,2,1,0:T(8,128)(2,1)S(1)} %get-tuple-element.9), channel_id=1, source_target_pairs={{1,0},{2,1},{3,2},{4,3},{5,4},{6,5},{7,6},{8,7},{9,8},{10,9},{11,1... | collective-permute-start | bytes 1179656 | tf_op jit(solution)/shard_map/ppermute | solution.py:17
  136.9 22.8 %collective-permute-start.2 = (bf16[6,1,128,256]{3,2,1,0:T(8,128)(2,1)}, bf16[6,1,128,256]{3,2,1,0:T(8,128)(2,1)S(1)}, u32[]{:S(2)}, u32[]{:S(2)}) collective-permute-start(bf16[6,1,128,256]{3,2,1,0:T(8,128)(2,1)} %get-tuple-element.16), channel_id=1, source_target_pairs={{0,1},{1,2},{2,3},{3,4},{4,5},{5,6},{6,7},{7,8},{8,9},{9,10},{10,1... | collective-permute-start | bytes 1179656 | tf_op jit(solution)/shard_map/ppermute | solution.py:14
  140.4 19.3 %collective-permute-start.3 = (bf16[6,1,128,256]{3,2,1,0:T(8,128)(2,1)}, bf16[6,1,128,256]{3,2,1,0:T(8,128)(2,1)S(1)}, u32[]{:S(2)}, u32[]{:S(2)}) collective-permute-start(bf16[6,1,128,256]{3,2,1,0:T(8,128)(2,1)} %get-tuple-element.17), channel_id=1, source_target_pairs={{1,0},{2,1},{3,2},{4,3},{5,4},{6,5},{7,6},{8,7},{9,8},{10,9},{11,1... | collective-permute-start | bytes 1179656 | tf_op jit(solution)/shard_map/ppermute | solution.py:17
  157.9 3.2 copy-start.6
  157.9 4.5 %copy-start.7 = (f32[4,8,127,256]{3,2,1,0:T(8,128)S(1)}, f32[4,8,127,256]{3,2,1,0:T(8,128)}, u32[]{:S(2)}) copy-start(f32[4,8,127,256]{3,2,1,0:T(8,128)} %get-tuple-element.47) | copy-start | bytes 12484612
  168.3 5.7 %copy-start.12 = (bf16[4,8,128,256]{3,2,1,0:T(8,128)(2,1)}, bf16[4,8,128,256]{3,2,1,0:T(8,128)(2,1)S(1)}, u32[]{:S(2)}) copy-start(bf16[4,8,128,256]{3,2,1,0:T(8,128)(2,1)S(1)} %get-tuple-element.42) | copy-start | bytes 6291460
  168.3 5.7 %copy-start.14 = (bf16[4,8,128,256]{3,2,1,0:T(8,128)(2,1)}, bf16[4,8,128,256]{3,2,1,0:T(8,128)(2,1)S(1)}, u32[]{:S(2)}) copy-start(bf16[4,8,128,256]{3,2,1,0:T(8,128)(2,1)S(1)} %get-tuple-element.43) | copy-start | bytes 6291460
  168.4 3.1 copy-start.27
  171.5 2.6 copy-start.16
  171.5 2.6 copy-start.18
  186.4 7.7 %copy-start.17 = (bf16[4,8,128,256]{3,2,1,0:T(8,128)(2,1)S(1)}, bf16[4,8,128,256]{3,2,1,0:T(8,128)(2,1)}, u32[]{:S(2)}) copy-start(bf16[4,8,128,256]{3,2,1,0:T(8,128)(2,1)} %get-tuple-element.44) | copy-start | bytes 6291460
  186.4 7.7 %copy-start.19 = (bf16[4,8,128,256]{3,2,1,0:T(8,128)(2,1)S(1)}, bf16[4,8,128,256]{3,2,1,0:T(8,128)(2,1)}, u32[]{:S(2)}) copy-start(bf16[4,8,128,256]{3,2,1,0:T(8,128)(2,1)} %get-tuple-element.45) | copy-start | bytes 6291460
  186.4 7.7 %copy-start.28 = (bf16[4,8,128,256]{3,2,1,0:T(8,128)(2,1)S(1)}, bf16[4,8,128,256]{3,2,1,0:T(8,128)(2,1)}, u32[]{:S(2)}) copy-start(bf16[4,8,128,256]{3,2,1,0:T(8,128)(2,1)} %fusion.26) | copy-start | bytes 6291460
  190.4 13.1 %collective-permute-start.4 = (bf16[1,8,128,256]{2,3,1,0:T(8,128)(2,1)S(1)}, bf16[1,8,128,256]{2,3,1,0:T(8,128)(2,1)S(1)}, u32[]{:S(2)}, u32[]{:S(2)}) collective-permute-start(bf16[1,8,128,256]{2,3,1,0:T(8,128)(2,1)S(1)} %get-tuple-element.38), channel_id=1, source_target_pairs={{0,16},{16,32},{32,48},{48,64},{64,80},{80,96},{96,112},{1,17},{17... | collective-permute-start | bytes 1572872 | tf_op jit(solution)/shard_map/ppermute | solution.py:14
  192.8 14.8 %collective-permute-start.5 = (bf16[1,8,128,256]{2,3,1,0:T(8,128)(2,1)S(1)}, bf16[1,8,128,256]{2,3,1,0:T(8,128)(2,1)S(1)}, u32[]{:S(2)}, u32[]{:S(2)}) collective-permute-start(bf16[1,8,128,256]{2,3,1,0:T(8,128)(2,1)S(1)} %get-tuple-element.39), channel_id=1, source_target_pairs={{16,0},{32,16},{48,32},{64,48},{80,64},{96,80},{112,96},{17,1},{33... | collective-permute-start | bytes 1572872 | tf_op jit(solution)/shard_map/ppermute | solution.py:17
  196.8 16.5 %copy-start.13 = (bf16[4,8,128,256]{3,2,1,0:T(8,128)(2,1)S(1)}, bf16[4,8,128,256]{3,2,1,0:T(8,128)(2,1)}, u32[]{:S(2)}) copy-start(bf16[4,8,128,256]{3,2,1,0:T(8,128)(2,1)} %copy-done.12) | copy-start | bytes 6291460
  196.8 16.5 %copy-start.15 = (bf16[4,8,128,256]{3,2,1,0:T(8,128)(2,1)S(1)}, bf16[4,8,128,256]{3,2,1,0:T(8,128)(2,1)}, u32[]{:S(2)}) copy-start(bf16[4,8,128,256]{3,2,1,0:T(8,128)(2,1)} %copy-done.14) | copy-start | bytes 6291460
  203.5 12.3 %copy-start.24 = (bf16[1,8,128,256]{2,3,1,0:T(8,128)(2,1)}, bf16[1,8,128,256]{2,3,1,0:T(8,128)(2,1)S(1)}, u32[]{:S(2)}) copy-start(bf16[1,8,128,256]{2,3,1,0:T(8,128)(2,1)S(1)} %collective-permute-done.4) | copy-start | bytes 1572868
  207.7 8.2 %copy-start.25 = (bf16[1,8,128,256]{2,3,1,0:T(8,128)(2,1)}, bf16[1,8,128,256]{2,3,1,0:T(8,128)(2,1)S(1)}, u32[]{:S(2)}) copy-start(bf16[1,8,128,256]{2,3,1,0:T(8,128)(2,1)S(1)} %collective-permute-done.5) | copy-start | bytes 1572868
  207.8 8.2 %collective-permute-start.6 = (bf16[6,1,128,256]{2,3,1,0:T(8,128)(2,1)S(1)}, bf16[6,1,128,256]{2,3,1,0:T(8,128)(2,1)S(1)}, u32[]{:S(2)}, u32[]{:S(2)}) collective-permute-start(bf16[6,1,128,256]{2,3,1,0:T(8,128)(2,1)S(1)} %get-tuple-element.12), channel_id=1, source_target_pairs={{0,1},{1,2},{2,3},{3,4},{4,5},{5,6},{6,7},{7,8},{8,9},{9,10},{10,1... | collective-permute-start | bytes 1179656 | tf_op jit(solution)/shard_map/ppermute | solution.py:14
  211.3 9.1 %collective-permute-start.7 = (bf16[6,1,128,256]{2,3,1,0:T(8,128)(2,1)S(1)}, bf16[6,1,128,256]{2,3,1,0:T(8,128)(2,1)S(1)}, u32[]{:S(2)}, u32[]{:S(2)}) collective-permute-start(bf16[6,1,128,256]{2,3,1,0:T(8,128)(2,1)S(1)} %get-tuple-element.13), channel_id=1, source_target_pairs={{1,0},{2,1},{3,2},{4,3},{5,4},{6,5},{7,6},{8,7},{9,8},{10,9},{11,1... | collective-permute-start | bytes 1179656 | tf_op jit(solution)/shard_map/ppermute | solution.py:17
  216.0 4.4 %copy-start.54 = (bf16[6,1,128,256]{2,3,1,0:T(8,128)(2,1)}, bf16[6,1,128,256]{2,3,1,0:T(8,128)(2,1)S(1)}, u32[]{:S(2)}) copy-start(bf16[6,1,128,256]{2,3,1,0:T(8,128)(2,1)S(1)} %collective-permute-done.6) | copy-start | bytes 1179652
  221.1 6.2 %copy-start.2 = (bf16[4,8,128,256]{3,2,1,0:T(8,128)(2,1)S(1)}, bf16[4,8,128,256]{3,2,1,0:T(8,128)(2,1)}, u32[]{:S(2)}) copy-start(bf16[4,8,128,256]{3,2,1,0:T(8,128)(2,1)} %param.6) | copy-start | bytes 6291460
  227.4 3.7 copy-start.10
  227.4 3.7 copy-start.11
  254.6 6.3 %copy-start.38 = (bf16[256,256]{1,0:T(8,128)(2,1)S(1)}, bf16[256,256]{1,0:T(8,128)(2,1)}, u32[]{:S(2)}) copy-start(bf16[256,256]{1,0:T(8,128)(2,1)} %get-tuple-element.52) | copy-start | bytes 393220
  254.6 6.3 %copy-start.40 = (bf16[256,256]{1,0:T(8,128)(2,1)S(1)}, bf16[256,256]{1,0:T(8,128)(2,1)}, u32[]{:S(2)}) copy-start(bf16[256,256]{1,0:T(8,128)(2,1)} %get-tuple-element.53) | copy-start | bytes 393220
  260.9 3.6 copy-start.4
  260.9 3.6 copy-start.34
  260.9 3.6 copy-start.36
  270.2 5.5 %copy-start.5 = (bf16[4,8,128,256]{2,3,1,0:T(8,128)(2,1)S(1)}, bf16[4,8,128,256]{2,3,1,0:T(8,128)(2,1)}, u32[]{:S(2)}) copy-start(bf16[4,8,128,256]{2,3,1,0:T(8,128)(2,1)} %copy.24) | copy-start | bytes 6291460
  281.6 119.6 %copy-start.26 = (f32[2048,256]{1,0:T(8,128)S(1)}, f32[2048,256]{1,0:T(8,128)}, u32[]{:S(2)}) copy-start(f32[2048,256]{1,0:T(8,128)} %convert_element_type.142) | copy-start | bytes 6291460
  281.6 119.6 %copy-start.57 = (f32[6,2048]{1,0:T(8,128)S(1)}, f32[6,2048]{1,0:T(8,128)}, u32[]{:S(2)}) copy-start(f32[6,2048]{1,0:T(8,128)} %copy-done.56) | copy-start | bytes 147460
  (26 other events, 36.9 us)
Sparse Core Ops, SparseCore 0:
  242.3 155.7 all-reduce.8
where the time goes:
time: 421 us; the launch traced here: 413 us
  waiting for transfers between devices  127 us (30%)
  blocking collectives  78.6 us (19%)
  local copies, waits for them, and re-layouts  70 us (17%)
  other arithmetic  47.5 us (11%)
  matrix products  43.8 us (10%)
  starting transfers between devices  31.4 us (7%)
  between operations  15.1 us (4%)
    psum x1, waiting for transfers between devices, on_device(): total_grad = lax.psum(local_grad, ('gx', 'gy', 'gz'))  112 us
    psum x1, blocking collectives, on_device(): flux_sum = lax.psum(gram_local, ('gx', 'gy', 'gz'))  78.6 us
    unnamed x126, local copies, waits for them, and re-layouts  23.1 us
    ppermute x6, starting transfers between devices, with_halo(): lax.ppermute(lax.slice_in_dim(block, block.shape[dim] - width, None, axis...  20.9 us
    convert_element_type x3, other arithmetic, neighbour_pairs(): lower_diff = (centre - lower_side.astype(jnp.float32)).astype(jnp.bfloat16)  18.9 us
    concatenate x3, local copies, waits for them, and re-layouts, neighbour_pairs(): jnp.concatenate([lower_diff, upper_diff], axis=-1)  18.7 us
    dot_general x6, matrix products, backward_terms(): jnp.dot(diff_pairs[direction], back_mats[direction], preferred_element_ty...  14.2 us
    dot_general x6, matrix products, backward_terms(): lax.dot_general(flat_partner, diff_pairs[direction], (((0,), (0,)), ((),...  14 us
  transfers between devices with their start and end apart: 13, of which 5 were waited for; matrix products, arithmetic and copies ran while one was open for 23% of the time, Pallas kernels for 0%

commit v1 on v0

v1 whole, which is shorter than its diff:
```python
import jax
import jax.numpy as jnp
from jax import lax
from jax.experimental import pallas as pl
from jax.experimental.pallas import tpu as pltpu
from jax.sharding import PartitionSpec as P

courant = 0.2
ALL = ("gx", "gy", "gz")
BF = jnp.bfloat16
F32 = jnp.float32
NX, NY, NZ, R = 4, 8, 128, 256
ROWS = NY * NZ
VMEM_LIMIT = 56 * 1024 * 1024
whole = pl.BlockSpec(memory_space=pltpu.VMEM)
raw = pl.BlockSpec(memory_space=pl.ANY)


def params(**kw):
    return pltpu.CompilerParams(vmem_limit_bytes=VMEM_LIMIT, **kw)


def cost(flops, bytes_accessed):
    return pl.CostEstimate(flops=flops, bytes_accessed=bytes_accessed, transcendentals=0)


def tri_masks():
    row = lax.broadcasted_iota(jnp.int32, (128, 128), 0)
    col = lax.broadcasted_iota(jnp.int32, (128, 128), 1)
    return row, col


def store_packed(out_ref, k, a, b, d):
    row, col = tri_masks()
    out_ref[k * 256 : k * 256 + 128, :] = jnp.where(row <= col, a, d).astype(BF)
    out_ref[k * 256 + 128 : k * 256 + 256, :] = b.astype(BF)
    return jnp.sum(jnp.where(row == col, d, 0.0), axis=0, keepdims=True)


def store_diagonals(out_ref, diagonals):
    zeros = jnp.zeros((10, 128), F32)
    out_ref[1536:1552, :] = jnp.concatenate(diagonals + [zeros], axis=0).astype(BF)
    out_ref[1552:2048, :] = jnp.zeros((496, 128), BF)


def load_packed(packed_ref, k):
    row, col = tri_masks()
    t = packed_ref[k * 256 : k * 256 + 128, :].astype(F32)
    b = packed_ref[k * 256 + 128 : k * 256 + 256, :].astype(F32)
    diag = packed_ref[1536:1552, :].astype(F32)[k : k + 1, :]
    tt = t.T
    a = jnp.where(row <= col, t, tt)
    d = jnp.where(row > col, t, jnp.where(row < col, tt, jnp.broadcast_to(diag, (128, 128))))
    return a, b, b.T, d


def rate_rows(speeds_ref, signs_ref):
    rows = []
    for d in range(3):
        chosen = signs_ref[d : d + 1, :].astype(F32)
        speed = speeds_ref[d : d + 1, :]
        rows.append(speed * chosen)
        rows.append(speed * (1.0 - chosen))
    return rows


def gram_kernel(factors_ref, speeds_ref, signs_ref, out_ref, turned_ref, acc_ref):
    rows = rate_rows(speeds_ref, signs_ref)
    turned = factors_ref[...].astype(F32).T
    for k in range(6):
        turned_ref[k * 256 : k * 256 + 256, :] = (turned * rows[k]).astype(BF)
    acc_ref[...] = jnp.dot(turned_ref[...], factors_ref[...], preferred_element_type=F32)
    diagonals = []
    for k in range(6):
        g = acc_ref.at[pl.ds(k * 256, 256), :]
        diagonals.append(
            store_packed(out_ref, k, g[:128, :128], g[:128, 128:], g[128:, 128:])
        )
    store_diagonals(out_ref, diagonals)


def gram(factors, speeds, signs):
    return pl.pallas_call(
        gram_kernel,
        out_shape=jax.ShapeDtypeStruct((2048, 128), BF),
        in_specs=[whole] * 3,
        out_specs=whole,
        scratch_shapes=[pltpu.VMEM((1536, 2048), BF), pltpu.VMEM((1536, 256), F32)],
        compiler_params=params(),
        cost_estimate=cost(2 * 2048 * 256 * 1536, 2 << 20),
        name="gram",
    )(factors, speeds, signs)


def total_kernel(parts_ref, out_ref):
    total = jnp.sum(parts_ref[...].astype(F32), axis=0).astype(BF)
    out_ref[...] = jnp.broadcast_to(total[None], (128, 16, 128))


def sum_everywhere(packed):
    pieces = packed.reshape(128, 16, 128)
    mine = lax.all_to_all(pieces, ALL, split_axis=0, concat_axis=0, tiled=True)
    copies = pl.pallas_call(
        total_kernel,
        out_shape=jax.ShapeDtypeStruct((128, 16, 128), BF),
        in_specs=[whole],
        out_specs=whole,
        compiler_params=params(),
        cost_estimate=cost(1 << 18, 1 << 20),
        name="total",
    )(mine)
    everything = lax.all_to_all(copies, ALL, split_axis=0, concat_axis=0, tiled=True)
    return everything.reshape(2048, 128)


def mask_columns(mask_plane):
    return mask_plane.astype(F32).T


def faces_kernel(state_ref, cot_ref, mask_ref, held_ref, xlo_ref, xhi_ref, ylo_ref, yhi_ref):
    p = pl.program_id(0)
    columns = mask_columns(mask_ref[0])
    for y in range(NY):
        gate = jnp.broadcast_to(columns[:, y : y + 1], (NZ, R)).astype(BF)
        held_ref[0, y] = cot_ref[0, y] * gate
    ylo_ref[0, 0] = state_ref[0, 0]
    ylo_ref[1, 0] = held_ref[0, 0]
    yhi_ref[0, 0] = state_ref[0, NY - 1]
    yhi_ref[1, 0] = held_ref[0, NY - 1]

    @pl.when(p == 0)
    def _():
        xlo_ref[0] = state_ref[0]
        xlo_ref[1] = held_ref[0]

    @pl.when(p == NX - 1)
    def _():
        xhi_ref[0] = state_ref[0]
        xhi_ref[1] = held_ref[0]


plane = pl.BlockSpec((1, NY, NZ, R), lambda p: (p, 0, 0, 0))
mask_block = pl.BlockSpec((1, NY, NZ), lambda p: (p, 0, 0))


def faces(state, cotangent, mask):
    x_face = pl.BlockSpec((2, NY, NZ, R), lambda p: (0, 0, 0, 0))
    y_face = pl.BlockSpec((2, 1, NZ, R), lambda p: (0, p, 0, 0))
    x_shape = jax.ShapeDtypeStruct((2, NY, NZ, R), BF)
    y_shape = jax.ShapeDtypeStruct((2, NX, NZ, R), BF)
    return pl.pallas_call(
        faces_kernel,
        grid=(NX,),
        out_shape=(jax.ShapeDtypeStruct((NX, NY, NZ, R), BF), x_shape, x_shape, y_shape, y_shape),
        in_specs=[plane, plane, mask_block],
        out_specs=(plane, x_face, x_face, y_face, y_face),
        compiler_params=params(),
        cost_estimate=cost(1 << 20, 9 << 20),
        name="faces",
    )(state, cotangent, mask)


def load_padded(padded, sem, centre, xlo, xhi, ylo, yhi):
    copies = [
        pltpu.make_async_copy(centre, padded.at[pl.ds(1, NX), pl.ds(1, NY)], sem.at[0]),
        pltpu.make_async_copy(xlo, padded.at[0, pl.ds(1, NY)], sem.at[1]),
        pltpu.make_async_copy(xhi, padded.at[NX + 1, pl.ds(1, NY)], sem.at[2]),
        pltpu.make_async_copy(ylo, padded.at[pl.ds(1, NX), 0], sem.at[3]),
        pltpu.make_async_copy(yhi, padded.at[pl.ds(1, NX), NY + 1], sem.at[4]),
    ]
    for copy in copies:
        copy.start()
    return copies


def build_pairs(padded, p, pairs):
    place = lax.broadcasted_iota(jnp.int32, (NZ, R), 0)

    def one_row(y, carry):
        at = pl.ds(pl.multiple_of(y * NZ, NZ), NZ)
        centre = padded[p + 1, y + 1]
        pairs[at, 0:256] = padded[p + 2, y + 1] - centre
        pairs[at, 256:512] = centre - padded[p, y + 1]
        pairs[at, 512:768] = padded[p + 1, y + 2] - centre
        pairs[at, 768:1024] = centre - padded[p + 1, y]
        wide = centre.astype(F32)
        after = jnp.where(place < NZ - 1, pltpu.roll(wide, NZ - 1, 0), 0.0)
        before = jnp.where(place > 0, pltpu.roll(wide, 1, 0), 0.0)
        pairs[at, 1024:1280] = (after - wide).astype(BF)
        pairs[at, 1280:1536] = (wide - before).astype(BF)
        return carry

    lax.fori_loop(0, NY, one_row, 0)


def inner_kernel(
    packed_ref, cot_ref, mask_ref, held_hbm, xlo_hbm, xhi_hbm, ylo_hbm, yhi_hbm,
    hi_ref, base_ref, hxlo_ref, hxhi_ref, hylo_ref, hyhi_ref, back_ref, flow_ref,
    padded, pairs, acc, sem,
):
    p = pl.program_id(0)

    @pl.when(p == 0)
    def _():
        copies = load_padded(
            padded, sem, held_hbm, xlo_hbm.at[1], xhi_hbm.at[1], ylo_hbm.at[1], yhi_hbm.at[1]
        )
        for d in range(3):
            for side in range(2):
                a, b, c, e = load_packed(packed_ref, 2 * d + side)
                sign = 1.0 - 2.0 * side
                at = (2 * d + side) * 256
                back_ref[at : at + 128, :128] = (sign * a).astype(BF)
                back_ref[at : at + 128, 128:] = (sign * b).astype(BF)
                back_ref[at + 128 : at + 256, :128] = (sign * c).astype(BF)
                back_ref[at + 128 : at + 256, 128:] = (sign * e).astype(BF)
                at = (2 * d + 1 - side) * 256
                flow_ref[at : at + 128, :128] = (-sign * a).astype(BF)
                flow_ref[at : at + 128, 128:] = (-sign * b).astype(BF)
                flow_ref[at + 128 : at + 256, :128] = (-sign * c).astype(BF)
                flow_ref[at + 128 : at + 256, 128:] = (-sign * e).astype(BF)
        for copy in copies:
            copy.wait()

    build_pairs(padded, p, pairs)
    acc[...] = jnp.dot(pairs[...], back_ref[...], preferred_element_type=F32)
    columns = mask_columns(mask_ref[0])
    for y in range(NY):
        gate = jnp.broadcast_to(columns[:, y : y + 1], (NZ, R))
        half = 0.5 * cot_ref[0, y].astype(F32)
        inner = half + (0.5 * courant) * acc[y * NZ : (y + 1) * NZ, :]
        hi_ref[0, y] = (gate * inner).astype(BF)
        base_ref[0, y] = half + inner
    hylo_ref[0] = hi_ref[0, 0]
    hyhi_ref[0] = hi_ref[0, NY - 1]

    @pl.when(p == 0)
    def _():
        hxlo_ref[...] = hi_ref[0]

    @pl.when(p == NX - 1)
    def _():
        hxhi_ref[...] = hi_ref[0]


def constant(shape):
    return pl.BlockSpec(shape, lambda p: (0,) * len(shape), pipeline_mode=pl.Buffered(1))


def kept(shape):
    return pl.BlockSpec(shape, lambda p: (0,) * len(shape))


def inner_step(packed, cotangent, mask, held, xlo, xhi, ylo, yhi):
    grid_shape = (NX, NY, NZ, R)
    x_shape = jax.ShapeDtypeStruct((NY, NZ, R), BF)
    y_shape = jax.ShapeDtypeStruct((NX, NZ, R), BF)
    y_face = pl.BlockSpec((1, NZ, R), lambda p: (p, 0, 0))
    mats = jax.ShapeDtypeStruct((1536, 256), BF)
    return pl.pallas_call(
        inner_kernel,
        grid=(NX,),
        out_shape=(
            jax.ShapeDtypeStruct(grid_shape, BF),
            jax.ShapeDtypeStruct(grid_shape, F32),
            x_shape, x_shape, y_shape, y_shape, mats, mats,
        ),
        in_specs=[constant((2048, 128)), plane, mask_block] + [raw] * 5,
        out_specs=(
            plane, plane, kept((NY, NZ, R)), kept((NY, NZ, R)), y_face, y_face,
            kept((1536, 256)), kept((1536, 256)),
        ),
        scratch_shapes=[
            pltpu.VMEM((NX + 2, NY + 2, NZ, R), BF),
            pltpu.VMEM((ROWS, 1536), BF),
            pltpu.VMEM((ROWS, R), F32),
            pltpu.SemaphoreType.DMA((5,)),
        ],
        compiler_params=params(),
        cost_estimate=cost(2 * 4096 * 256 * 1536, 14 << 20),
        name="inner",
    )(packed, cotangent, mask, held, xlo, xhi, ylo, yhi)


def middle_kernel(
    flow_ref, mask_ref, state_hbm, held_hbm, xlo_hbm, xhi_hbm, ylo_hbm, yhi_hbm,
    grads_ref, state_pad, held_pad, pairs, held_pairs, middle, acc, sem_s, sem_h,
):
    p = pl.program_id(0)

    @pl.when(p == 0)
    def _():
        first = load_padded(
            state_pad, sem_s, state_hbm, xlo_hbm.at[0], xhi_hbm.at[0], ylo_hbm.at[0], yhi_hbm.at[0]
        )
        second = load_padded(
            held_pad, sem_h, held_hbm, xlo_hbm.at[1], xhi_hbm.at[1], ylo_hbm.at[1], yhi_hbm.at[1]
        )
        grads_ref[...] = jnp.zeros_like(grads_ref)
        for copy in first + second:
            copy.wait()

    build_pairs(state_pad, p, pairs)
    acc[...] = jnp.dot(pairs[...], flow_ref[...], preferred_element_type=F32)
    columns = mask_columns(mask_ref[0])
    for y in range(NY):
        gate = jnp.broadcast_to(columns[:, y : y + 1], (NZ, R))
        flow = courant * acc[y * NZ : (y + 1) * NZ, :]
        own = state_pad[p + 1, y + 1].astype(F32)
        middle[y * NZ : (y + 1) * NZ, :] = (own + gate * flow).astype(BF)
    build_pairs(held_pad, p, held_pairs)
    grads_ref[...] += lax.dot_general(
        middle[...], held_pairs[...], (((0,), (0,)), ((), ())), preferred_element_type=F32
    )


def middle_step(flow_mats, mask, state, held, xlo, xhi, ylo, yhi):
    padded = pltpu.VMEM((NX + 2, NY + 2, NZ, R), BF)
    return pl.pallas_call(
        middle_kernel,
        grid=(NX,),
        out_shape=jax.ShapeDtypeStruct((256, 1536), F32),
        in_specs=[constant((1536, 256)), mask_block] + [raw] * 6,
        out_specs=kept((256, 1536)),
        scratch_shapes=[
            padded, padded,
            pltpu.VMEM((ROWS, 1536), BF),
            pltpu.VMEM((ROWS, 1536), BF),
            pltpu.VMEM((ROWS, R), BF),
            pltpu.VMEM((ROWS, R), F32),
            pltpu.SemaphoreType.DMA((5,)),
            pltpu.SemaphoreType.DMA((5,)),
        ],
        compiler_params=params(),
        cost_estimate=cost(4 * 4096 * 256 * 1536, 8 << 20),
        name="middle",
    )(flow_mats, mask, state, held, xlo, xhi, ylo, yhi)


def grads_kernel(
    held_grads_ref, state_ref, hi_hbm, xlo_hbm, xhi_hbm, ylo_hbm, yhi_hbm,
    out_ref, padded, pairs, acc, sem,
):
    p = pl.program_id(0)

    @pl.when(p == 0)
    def _():
        copies = load_padded(padded, sem, hi_hbm, xlo_hbm, xhi_hbm, ylo_hbm, yhi_hbm)
        acc[...] = 0.5 * held_grads_ref[...]
        for copy in copies:
            copy.wait()

    build_pairs(padded, p, pairs)
    acc[...] += lax.dot_general(
        state_ref[0].reshape(ROWS, R), pairs[...], (((0,), (0,)), ((), ())),
        preferred_element_type=F32,
    )

    @pl.when(p == NX - 1)
    def _():
        diagonals = []
        for k in range(6):
            scale = courant if k % 2 == 0 else -courant
            g = acc.at[:, pl.ds(k * 256, 256)]
            a, b, c, d = g[:128, :128], g[:128, 128:], g[128:, :128], g[128:, 128:]
            diagonals.append(
                store_packed(
                    out_ref, k, scale * (a + a.T), scale * (b + c.T), scale * (d + d.T)
                )
            )
        store_diagonals(out_ref, diagonals)


def grads_step(held_grads, state, hi, xlo, xhi, ylo, yhi):
    return pl.pallas_call(
        grads_kernel,
        grid=(NX,),
        out_shape=jax.ShapeDtypeStruct((2048, 128), BF),
        in_specs=[constant((256, 1536)), plane] + [raw] * 5,
        out_specs=kept((2048, 128)),
        scratch_shapes=[
            pltpu.VMEM((NX + 2, NY + 2, NZ, R), BF),
            pltpu.VMEM((ROWS, 1536), BF),
            pltpu.VMEM((256, 1536), F32),
            pltpu.SemaphoreType.DMA((5,)),
        ],
        compiler_params=params(),
        cost_estimate=cost(2 * 4096 * 256 * 1536, 7 << 20),
        name="grads",
    )(held_grads, state, hi, xlo, xhi, ylo, yhi)


def outer_kernel(
    back_ref, base_ref, hi_hbm, xlo_hbm, xhi_hbm, ylo_hbm, yhi_hbm,
    out_ref, padded, pairs, acc, sem,
):
    p = pl.program_id(0)

    @pl.when(p == 0)
    def _():
        copies = load_padded(padded, sem, hi_hbm, xlo_hbm, xhi_hbm, ylo_hbm, yhi_hbm)
        for copy in copies:
            copy.wait()

    build_pairs(padded, p, pairs)
    acc[...] = jnp.dot(pairs[...], back_ref[...], preferred_element_type=F32)
    for y in range(NY):
        out_ref[0, y] = (base_ref[0, y] + courant * acc[y * NZ : (y + 1) * NZ, :]).astype(BF)


def outer_step(back_mats, base, hi, xlo, xhi, ylo, yhi):
    return pl.pallas_call(
        outer_kernel,
        grid=(NX,),
        out_shape=jax.ShapeDtypeStruct((NX, NY, NZ, R), BF),
        in_specs=[constant((1536, 256)), plane] + [raw] * 5,
        out_specs=plane,
        scratch_shapes=[
            pltpu.VMEM((NX + 2, NY + 2, NZ, R), BF),
            pltpu.VMEM((ROWS, 1536), BF),
            pltpu.VMEM((ROWS, R), F32),
            pltpu.SemaphoreType.DMA((5,)),
        ],
        compiler_params=params(),
        cost_estimate=cost(2 * 4096 * 256 * 1536, 11 << 20),
        name="outer",
    )(back_mats, base, hi, xlo, xhi, ylo, yhi)


CHUNK = 512


def final_kernel(packed_ref, factors_ref, speeds_ref, signs_ref, out_ref, mats, weighted):
    @pl.when(pl.program_id(0) == 0)
    def _():
        for k in range(6):
            a, b, c, d = load_packed(packed_ref, k)
            at = k * 256
            mats[at : at + 128, :128] = a.astype(BF)
            mats[at : at + 128, 128:] = b.astype(BF)
            mats[at + 128 : at + 256, :128] = c.astype(BF)
            mats[at + 128 : at + 256, 128:] = d.astype(BF)

    rows = rate_rows(speeds_ref, signs_ref)
    columns = jnp.concatenate(rows + rows[:2], axis=0).T
    values = factors_ref[...].astype(F32)
    for k in range(6):
        rate = jnp.broadcast_to(columns[:, k : k + 1], (CHUNK, R))
        weighted[:, k * 256 : k * 256 + 256] = (rate * values).astype(BF)
    out_ref[...] = jnp.dot(weighted[...], mats[...], preferred_element_type=F32)


def final_step(packed, factors, speeds, signs):
    rows = factors.shape[0]
    return pl.pallas_call(
        final_kernel,
        grid=(rows // CHUNK,),
        out_shape=jax.ShapeDtypeStruct((rows, R), F32),
        in_specs=[
            constant((2048, 128)),
            pl.BlockSpec((CHUNK, R), lambda i: (i, 0)),
            pl.BlockSpec((3, CHUNK), lambda i: (0, i)),
            pl.BlockSpec((3, CHUNK), lambda i: (0, i)),
        ],
        out_specs=pl.BlockSpec((CHUNK, R), lambda i: (i, 0)),
        scratch_shapes=[pltpu.VMEM((1536, 256), BF), pltpu.VMEM((CHUNK, 1536), BF)],
        compiler_params=params(),
        cost_estimate=cost(2 * 2048 * 256 * 1536, 4 << 20),
        name="final",
    )(packed, factors, speeds, signs)


def exchange(lo_x, hi_x, lo_y, hi_y):
    results = []
    for axis, lo, hi in (("gx", lo_x, hi_x), (("gy", "gz"), lo_y, hi_y)):
        count = lax.axis_size(axis)
        forward = [(i, i + 1) for i in range(count - 1)]
        backward = [(i + 1, i) for i in range(count - 1)]
        results.append(lax.ppermute(hi, axis, forward))
        results.append(lax.ppermute(lo, axis, backward))
    return results


def on_device(state, cotangent, factors, speeds, signs, mask):
    packed = sum_everywhere(gram(factors, speeds, signs))
    held, xlo, xhi, ylo, yhi = faces(state, cotangent, mask)
    halos = exchange(xlo, xhi, ylo, yhi)
    hi, base, hxlo, hxhi, hylo, hyhi, back_mats, flow_mats = inner_step(
        packed, cotangent, mask, held, *halos
    )
    hi_halos = exchange(hxlo, hxhi, hylo, hyhi)
    held_grads = middle_step(flow_mats, mask, state, held, *halos)
    symmetric = sum_everywhere(grads_step(held_grads, state, hi, *hi_halos))
    grad_state = outer_step(back_mats, base, hi, *hi_halos)
    grad_factors = final_step(symmetric, factors, speeds, signs)
    return (grad_state, grad_factors)


def solution(mesh):
    placed = (
        P("gx", ("gy", "gz"), None, None),
        P("gx", ("gy", "gz"), None, None),
        P(ALL, None),
        P(None, ALL),
        P(None, ALL),
        P("gx", ("gy", "gz"), None),
    )
    return jax.shard_map(
        on_device,
        mesh=mesh,
        in_specs=placed,
        out_specs=(P("gx", ("gy", "gz"), None, None), P(ALL, None)),
        check_vma=False,
    )
```

time: 421 us -> 188 us (0.45); the launches traced: 413 us -> 187 us
  waiting for transfers between devices: 127 us -> 32.4 us
  Pallas kernels: 0 us -> 74.2 us
  local copies, waits for them, and re-layouts: 70 us -> 4.2 us
  blocking collectives: 78.6 us -> 25.5 us
  other arithmetic: 47.5 us -> 0 us
  matrix products: 43.8 us -> 0 us
  starting transfers between devices: 31.4 us -> 49.5 us
  between operations: 15.1 us -> 0.87 us
    psum x1 -> x0, waiting for transfers between devices: 112 us -> none  [on_device(): total_grad = lax.psum(local_grad, ('gx', 'gy', 'gz'))]
    psum x1 -> x0, blocking collectives: 78.6 us -> none  [on_device(): flux_sum = lax.psum(gram_local, ('gx', 'gy', 'gz'))]
    pallas_call x0 -> x9, Pallas kernels: none -> 74.2 us  [the longest x1 23 us: middle_step(): pl.pallas_call(middle_kernel, grid=(NX,), out_shape=jax.ShapeDtypeStruct(...]
    dot_general x17 -> x0, matrix products: 43.8 us -> none  [the longest x6 14.2 us: backward_terms(): jnp.dot(diff_pairs[direction], back_mats[direction], preferred_element_ty...]
    convert_element_type x9 -> x0, other arithmetic: 32.7 us -> none  [the longest x3 18.9 us: neighbour_pairs(): lower_diff = (centre - lower_side.astype(jnp.float32)).astype(jnp.bfloat16)]
    all_to_all x0 -> x3, waiting for transfers between devices: none -> 32.3 us  [the longest x2 18.3 us: sum_everywhere(): lax.all_to_all(copies, ALL, split_axis=0, concat_axis=0, tiled=True)]
    all_to_all x0 -> x3, starting transfers between devices: none -> 30.6 us  [the longest x2 17.7 us: sum_everywhere(): lax.all_to_all(copies, ALL, split_axis=0, concat_axis=0, tiled=True)]
    all_to_all x0 -> x1, blocking collectives: none -> 25.5 us  [sum_everywhere(): mine = lax.all_to_all(pieces, ALL, split_axis=0, concat_axis=0, tiled=True)]
  transfers between devices with their start and end apart: 13 -> 11, of which waited for: 5 -> 3; matrix products, arithmetic and copies ran while one was open for 23% -> 0% of each run, Pallas kernels for 0% -> 21%
where the time goes in v1:
time: 188 us; the launch traced here: 187 us
  Pallas kernels  74.2 us (39%)
  starting transfers between devices  49.5 us (26%)
  waiting for transfers between devices  32.4 us (17%)
  blocking collectives  25.5 us (14%)
  local copies, waits for them, and re-layouts  4.2 us (2%)
    all_to_all x1, blocking collectives, sum_everywhere(): mine = lax.all_to_all(pieces, ALL, split_axis=0, concat_axis=0, tiled=True)  25.5 us
    pallas_call x1, Pallas kernels, middle_step(): pl.pallas_call(middle_kernel, grid=(NX,), out_shape=jax.ShapeDtypeStruct(...  23 us
    all_to_all x2, waiting for transfers between devices, sum_everywhere(): lax.all_to_all(copies, ALL, split_axis=0, concat_axis=0, tiled=True)  18.3 us
    all_to_all x2, starting transfers between devices, sum_everywhere(): lax.all_to_all(copies, ALL, split_axis=0, concat_axis=0, tiled=True)  17.7 us
    all_to_all x1, waiting for transfers between devices, sum_everywhere(): mine = lax.all_to_all(pieces, ALL, split_axis=0, concat_axis=0, tiled=True)  14 us
    all_to_all x1, starting transfers between devices, sum_everywhere(): mine = lax.all_to_all(pieces, ALL, split_axis=0, concat_axis=0, tiled=True)  12.9 us
    ppermute x4, starting transfers between devices, exchange(): results.append(lax.ppermute(hi, axis, forward))  12.4 us
    pallas_call x1, Pallas kernels, inner_step(): pl.pallas_call(inner_kernel, grid=(NX,), out_shape=(jax.ShapeDtypeStruct(...  11.1 us
  transfers between devices with their start and end apart: 11, of which 3 were waited for; matrix products, arithmetic and copies ran while one was open for 0% of the time, Pallas kernels for 21%

profile of v1, /device:TPU:1, one launch (start us, length us, event | category | flops | bytes accessed | tf_op | source)
XLA Modules:
  0.0 186.6 jit_solution(3109948078836459045)
XLA Ops:
  0.6 5.6 %faces.1 = (bf16[4,8,128,256]{3,2,1,0:T(8,128)(2,1)}, bf16[2,8,128,256]{3,2,1,0:T(8,128)(2,1)}, bf16[2,8,128,256]{3,2,1,0:T(8,128)(2,1)}, bf16[2,4,128,256]{3,2,1,0:T(8,128)(2,1)}, bf16[2,4,128,256]{3,2,1,0:T(8,128)(2,1)}) custom-call(bf16[4,8,128,256]{3,2,1,0:T(8,128)(2,1)} %state_ref.3, bf16[4,8,128,256]{3,2,1,0:T(8,128)(2,1)} %cot_ref.3, ...), custom_call_target="tpu_custom_call" | custom-call | flops 1048576 | bytes 9437184 | tf_op jit(solution)/shard_map/faces/pallas_call | solution.py:151
  6.2 4.1 %collective-permute-start = (bf16[2,8,128,256]{3,2,1,0:T(8,128)(2,1)}, bf16[2,8,128,256]{3,2,1,0:T(8,128)(2,1)S(1)}, u32[]{:S(2)}, u32[]{:S(2)}) collective-permute-start(bf16[2,8,128,256]{3,2,1,0:T(8,128)(2,1)} %get-tuple-element.16), channel_id=1, source_target_pairs={{0,16},{16,32},{32,48},{48,64},{64,80},{80,96},{96,112},{1,17},{17... | collective-permute-start | bytes 3145736 | tf_op jit(solution)/shard_map/ppermute | solution.py:479
  10.3 1.3 collective-permute-start.1
  11.6 3.9 %gram.1 = bf16[2048,128]{1,0:T(8,128)(2,1)} custom-call(bf16[2048,256]{1,0:T(8,128)(2,1)} %factors_ref.3, f32[3,2048]{1,0:T(4,128)} %speeds_ref.3, s32[3,2048]{1,0:T(4,128)} %signs_ref.3), custom_call_target="tpu_custom_call" | custom-call | flops 1610612736 | bytes 2097152 | tf_op jit(solution)/shard_map/gram/pallas_call | solution.py:83
  15.6 12.9 %all-to-all-start = ((bf16[128,16,128]{2,1,0:T(8,128)(2,1)}), bf16[128,16,128]{2,1,0:T(8,128)(2,1)S(1)}, u32[]{:S(2)}, u32[]{:S(2)}) async-start(bf16[128,16,128]{2,1,0:T(8,128)(2,1)} %bitcast.6), calls=%async_computation | async-start | bytes 1048576 | tf_op jit(solution)/shard_map/all_to_all | solution.py:102
  28.5 3.5 %collective-permute-start.2 = (bf16[2,4,128,256]{3,2,1,0:T(8,128)(2,1)}, bf16[2,4,128,256]{3,2,1,0:T(8,128)(2,1)S(1)}, u32[]{:S(2)}, u32[]{:S(2)}) collective-permute-start(bf16[2,4,128,256]{3,2,1,0:T(8,128)(2,1)} %get-tuple-element.18), channel_id=1, source_target_pairs={{0,1},{1,2},{2,3},{3,4},{4,5},{5,6},{6,7},{7,8},{8,9},{9,10},{10,1... | collective-permute-start | bytes 1572872 | tf_op jit(solution)/shard_map/ppermute | solution.py:479
  32.1 1.9 %collective-permute-start.3 = (bf16[2,4,128,256]{3,2,1,0:T(8,128)(2,1)}, bf16[2,4,128,256]{3,2,1,0:T(8,128)(2,1)}, u32[]{:S(2)}, u32[]{:S(2)}) collective-permute-start(bf16[2,4,128,256]{3,2,1,0:T(8,128)(2,1)} %get-tuple-element.19), channel_id=1, source_target_pairs={{1,0},{2,1},{3,2},{4,3},{5,4},{6,5},{7,6},{8,7},{9,8},{10,9},{11,1... | collective-permute-start | bytes 1572872 | tf_op jit(solution)/shard_map/ppermute | solution.py:480
  34.0 14.0 %all-to-all-done.parts_ref = bf16[128,16,128]{2,1,0:T(8,128)(2,1)S(1)} async-done(((bf16[128,16,128]{2,1,0:T(8,128)(2,1)}), bf16[128,16,128]{2,1,0:T(8,128)(2,1)S(1)}, u32[]{:S(2)}, u32[]{:S(2)}) %all-to-all-start) | async-done | bytes 524320 | tf_op jit(solution)/shard_map/all_to_all | solution.py:102
  48.0 0.8 copy-done
  48.8 2.0 %total.2 = bf16[128,16,128]{2,1,0:T(8,128)(2,1)} custom-call(bf16[128,16,128]{2,1,0:T(8,128)(2,1)} %copy-done), custom_call_target="tpu_custom_call" | custom-call | flops 262144 | bytes 1048576 | tf_op jit(solution)/shard_map/total/pallas_call | solution.py:103
  50.8 13.9 %all-to-all-start.1 = ((bf16[128,16,128]{2,1,0:T(8,128)(2,1)}), bf16[128,16,128]{2,1,0:T(8,128)(2,1)S(1)}, u32[]{:S(2)}, u32[]{:S(2)}) async-start(bf16[128,16,128]{2,1,0:T(8,128)(2,1)} %total.2), calls=%async_computation.1 | async-start | bytes 1048576 | tf_op jit(solution)/shard_map/all_to_all | solution.py:112
  64.7 0.0 collective-permute-done.2.ylo_hbm
  64.7 0.0 copy-start.5
  64.7 0.0 collective-permute-done.3.yhi_hbm
  64.7 14.1 %all-to-all-done.1 = bf16[128,16,128]{2,1,0:T(8,128)(2,1)S(1)} async-done(((bf16[128,16,128]{2,1,0:T(8,128)(2,1)}), bf16[128,16,128]{2,1,0:T(8,128)(2,1)S(1)}, u32[]{:S(2)}, u32[]{:S(2)}) %all-to-all-start.1) | async-done | bytes 524320 | tf_op jit(solution)/shard_map/all_to_all | solution.py:112
  78.8 0.0 collective-permute-done.xlo_hbm
  78.8 0.0 collective-permute-done.1.xhi_hbm
  78.8 0.0 copy-start.4
  78.8 0.0 copy-done.5
  78.8 0.8 copy-done.1
  79.6 0.4 copy-done.3
  80.0 0.4 copy-done.4
  80.3 11.1 %inner.1 = (bf16[4,8,128,256]{3,2,1,0:T(8,128)(2,1)}, f32[4,8,128,256]{3,2,1,0:T(8,128)}, bf16[8,128,256]{2,1,0:T(8,128)(2,1)}, bf16[8,128,256]{2,1,0:T(8,128)(2...) custom-call(bf16[2048,128]{1,0:T(8,128)(2,1)} %bitcast.4, ...), custom_call_target="tpu_custom_call" | custom-call | flops 3221225472 | bytes 14680064 | tf_op jit(solution)/shard_map/inner/pallas_call | solution.py:260
  91.4 2.5 %collective-permute-start.6 = (bf16[4,128,256]{2,1,0:T(8,128)(2,1)}, bf16[4,128,256]{2,1,0:T(8,128)(2,1)S(1)}, u32[]{:S(2)}, u32[]{:S(2)}) collective-permute-start(bf16[4,128,256]{2,1,0:T(8,128)(2,1)} %get-tuple-element.25), channel_id=1, source_target_pairs={{0,1},{1,2},{2,3},{3,4},{4,5},{5,6},{6,7},{7,8},{8,9},{9,10},{10,1... | collective-permute-start | bytes 786440 | tf_op jit(solution)/shard_map/ppermute | solution.py:479
  94.0 1.9 %collective-permute-start.7 = (bf16[4,128,256]{2,1,0:T(8,128)(2,1)}, bf16[4,128,256]{2,1,0:T(8,128)(2,1)S(1)}, u32[]{:S(2)}, u32[]{:S(2)}) collective-permute-start(bf16[4,128,256]{2,1,0:T(8,128)(2,1)} %get-tuple-element.26), channel_id=1, source_target_pairs={{1,0},{2,1},{3,2},{4,3},{5,4},{6,5},{7,6},{8,7},{9,8},{10,9},{11,1... | collective-permute-start | bytes 786440 | tf_op jit(solution)/shard_map/ppermute | solution.py:480
  95.9 2.2 %collective-permute-start.4 = (bf16[8,128,256]{2,1,0:T(8,128)(2,1)}, bf16[8,128,256]{2,1,0:T(8,128)(2,1)S(1)}, u32[]{:S(2)}, u32[]{:S(2)}) collective-permute-start(bf16[8,128,256]{2,1,0:T(8,128)(2,1)} %get-tuple-element.23), channel_id=1, source_target_pairs={{0,16},{16,32},{32,48},{48,64},{64,80},{80,96},{96,112},{1,17},{17... | collective-permute-start | bytes 1572872 | tf_op jit(solution)/shard_map/ppermute | solution.py:479
  98.1 1.3 collective-permute-start.5
  99.4 23.0 %middle.1.held_grads_ref = f32[256,1536]{1,0:T(8,128)} custom-call(bf16[1536,256]{1,0:T(8,128)(2,1)} %get-tuple-element.27.flow_ref, s32[4,8,128]{2,1,0:T(8,128)} %mask_ref.5, bf16[4,8,128,256]{3,2,1,0:T(8,128)(2,1)} %state_ref.3, bf16[4,8,128,256]{3,2,1,0:T(8,128)(2,1)} %get-tuple-element.15.held_hbm, bf16[2,8,128,256]{3,2,1,0:T(8,128)(2,1)} %copy-done.3, ...), custom_call_target="tpu_custom_call" | custom-call | flops 6442450944 | bytes 8388608 | tf_op jit(solution)/shard_map/middle/pallas_call | solution.py:319
  122.4 0.0 collective-permute-done.6.ylo_hbm
  122.5 0.0 copy-start.8
  122.5 0.0 collective-permute-done.7.yhi_hbm
  122.5 0.0 copy-start.9
  122.5 0.0 collective-permute-done.4.xlo_hbm
  122.5 0.0 copy-start.6
  122.5 0.0 collective-permute-done.5.xhi_hbm
  122.5 0.0 copy-start.7
  122.5 0.7 copy-done.8
  123.2 0.1 copy-done.9
  123.3 0.1 copy-done.6
  123.4 0.2 copy-done.7
  123.6 10.5 %grads.1 = bf16[2048,128]{1,0:T(8,128)(2,1)} custom-call(f32[256,1536]{1,0:T(8,128)} %middle.1.held_grads_ref, bf16[4,8,128,256]{3,2,1,0:T(8,128)(2,1)} %state_ref.3, bf16[4,8,128,256]{3,2,1,0:T(8,128)(2,1)} %get-tuple-element.22.hi_hbm, bf16[8,128,256]{2,1,0:T(8,128)(2,1)} %copy-done.6, bf16[8,128,256]{2,1,0:T(8,128)(2,1)} %copy-done.7, ...), custom_call_target="tpu_custom_call" | custom-call | flops 3221225472 | bytes 7340032 | tf_op jit(solution)/shard_map/grads/pallas_call | solution.py:375
  134.2 25.5 %all_to_all.20.parts_ref = bf16[128,16,128]{2,1,0:T(8,128)(2,1)} all-to-all(bf16[128,16,128]{2,1,0:T(8,128)(2,1)} %bitcast.7), channel_id=1, replica_groups=mesh['gx'=8,'gy'=8,'gz'=2] {'gx','gy','gz'}, dimensions={0} | all-to-all | bytes 1048576 | tf_op jit(solution)/shard_map/all_to_all | solution.py:102
  159.7 2.0 %total.3 = bf16[128,16,128]{2,1,0:T(8,128)(2,1)} custom-call(bf16[128,16,128]{2,1,0:T(8,128)(2,1)} %all_to_all.20.parts_ref), custom_call_target="tpu_custom_call" | custom-call | flops 262144 | bytes 1048576 | tf_op jit(solution)/shard_map/total/pallas_call | solution.py:103
  161.7 3.9 %all-to-all-start.3 = ((bf16[128,16,128]{2,1,0:T(8,128)(2,1)}), bf16[128,16,128]{2,1,0:T(8,128)(2,1)S(1)}, u32[]{:S(2)}, u32[]{:S(2)}) async-start(bf16[128,16,128]{2,1,0:T(8,128)(2,1)} %total.3), calls=%async_computation.3 | async-start | bytes 1048576 | tf_op jit(solution)/shard_map/all_to_all | solution.py:112
  165.6 10.0 %outer.1 = bf16[4,8,128,256]{3,2,1,0:T(8,128)(2,1)} custom-call(bf16[1536,256]{1,0:T(8,128)(2,1)} %get-tuple-element.20.back_ref, f32[4,8,128,256]{3,2,1,0:T(8,128)} %get-tuple-element.21.base_ref, bf16[4,8,128,256]{3,2,1,0:T(8,128)(2,1)} %get-tuple-element.22.hi_hbm, bf16[8,128,256]{2,1,0:T(8,128)(2,1)} %copy-done.6, bf16[8,128,256]{2,1,0:T(8,128)(2,1)} %copy-done.7, ...), custom_call_target="tpu_custom_call" | custom-call | flops 3221225472 | bytes 11534336 | tf_op jit(solution)/shard_map/outer/pallas_call | solution.py:412
  175.6 4.2 %all-to-all-done.3 = bf16[128,16,128]{2,1,0:T(8,128)(2,1)S(1)} async-done(((bf16[128,16,128]{2,1,0:T(8,128)(2,1)}), bf16[128,16,128]{2,1,0:T(8,128)(2,1)S(1)}, u32[]{:S(2)}, u32[]{:S(2)}) %all-to-all-start.3) | async-done | bytes 524320 | tf_op jit(solution)/shard_map/all_to_all | solution.py:112
  179.8 0.8 copy-done.2
  180.6 6.0 %final.1 = f32[2048,256]{1,0:T(8,128)} custom-call(bf16[2048,128]{1,0:T(8,128)(2,1)} %bitcast.5, bf16[2048,256]{1,0:T(8,128)(2,1)} %factors_ref.3, f32[3,2048]{1,0:T(4,128)} %speeds_ref.3, s32[3,2048]{1,0:T(4,128)} %signs_ref.3), custom_call_target="tpu_custom_call" | custom-call | flops 1610612736 | bytes 4194304 | tf_op jit(solution)/shard_map/final/pallas_call | solution.py:455
  (4 shorter events, 0.0 us)
Async XLA Ops:
  6.2 72.5 %collective-permute-start = (bf16[2,8,128,256]{3,2,1,0:T(8,128)(2,1)}, bf16[2,8,128,256]{3,2,1,0:T(8,128)(2,1)S(1)}, u32[]{:S(2)}, u32[]{:S(2)}) collective-permute-start(bf16[2,8,128,256]{3,2,1,0:T(8,128)(2,1)} %get-tuple-element.16), channel_id=1, source_target_pairs={{0,16},{16,32},{32,48},{48,64},{64,80},{80,96},{96,112},{1,17},{17... | collective-permute-start | bytes 3145736 | tf_op jit(solution)/shard_map/ppermute | solution.py:479
  10.3 68.5 %collective-permute-start.1 = (bf16[2,8,128,256]{3,2,1,0:T(8,128)(2,1)}, bf16[2,8,128,256]{3,2,1,0:T(8,128)(2,1)S(1)}, u32[]{:S(2)}, u32[]{:S(2)}) collective-permute-start(bf16[2,8,128,256]{3,2,1,0:T(8,128)(2,1)} %get-tuple-element.17), channel_id=1, source_target_pairs={{16,0},{32,16},{48,32},{64,48},{80,64},{96,80},{112,96},{17,1},{33... | collective-permute-start | bytes 3145736 | tf_op jit(solution)/shard_map/ppermute | solution.py:480
  15.6 32.4 %all-to-all-start = ((bf16[128,16,128]{2,1,0:T(8,128)(2,1)}), bf16[128,16,128]{2,1,0:T(8,128)(2,1)S(1)}, u32[]{:S(2)}, u32[]{:S(2)}) async-start(bf16[128,16,128]{2,1,0:T(8,128)(2,1)} %bitcast.6), calls=%async_computation | async-start | bytes 1048576 | tf_op jit(solution)/shard_map/all_to_all | solution.py:102
  28.5 36.1 %collective-permute-start.2 = (bf16[2,4,128,256]{3,2,1,0:T(8,128)(2,1)}, bf16[2,4,128,256]{3,2,1,0:T(8,128)(2,1)S(1)}, u32[]{:S(2)}, u32[]{:S(2)}) collective-permute-start(bf16[2,4,128,256]{3,2,1,0:T(8,128)(2,1)} %get-tuple-element.18), channel_id=1, source_target_pairs={{0,1},{1,2},{2,3},{3,4},{4,5},{5,6},{6,7},{7,8},{8,9},{9,10},{10,1... | collective-permute-start | bytes 1572872 | tf_op jit(solution)/shard_map/ppermute | solution.py:479
  32.1 32.6 %collective-permute-start.3 = (bf16[2,4,128,256]{3,2,1,0:T(8,128)(2,1)}, bf16[2,4,128,256]{3,2,1,0:T(8,128)(2,1)}, u32[]{:S(2)}, u32[]{:S(2)}) collective-permute-start(bf16[2,4,128,256]{3,2,1,0:T(8,128)(2,1)} %get-tuple-element.19), channel_id=1, source_target_pairs={{1,0},{2,1},{3,2},{4,3},{5,4},{6,5},{7,6},{8,7},{9,8},{10,9},{11,1... | collective-permute-start | bytes 1572872 | tf_op jit(solution)/shard_map/ppermute | solution.py:480
  48.0 0.8 copy-start
  50.8 28.0 %all-to-all-start.1 = ((bf16[128,16,128]{2,1,0:T(8,128)(2,1)}), bf16[128,16,128]{2,1,0:T(8,128)(2,1)S(1)}, u32[]{:S(2)}, u32[]{:S(2)}) async-start(bf16[128,16,128]{2,1,0:T(8,128)(2,1)} %total.2), calls=%async_computation.1 | async-start | bytes 1048576 | tf_op jit(solution)/shard_map/all_to_all | solution.py:112
  64.7 14.1 %copy-start.5 = (bf16[2,4,128,256]{3,2,1,0:T(8,128)(2,1)}, bf16[2,4,128,256]{3,2,1,0:T(8,128)(2,1)S(1)}, u32[]{:S(2)}) copy-start(bf16[2,4,128,256]{3,2,1,0:T(8,128)(2,1)S(1)} %collective-permute-done.2.ylo_hbm) | copy-start | bytes 1572868
  78.8 0.8 copy-start.1
  78.8 1.2 copy-start.3
  78.8 1.5 copy-start.4
  91.4 31.0 %collective-permute-start.6 = (bf16[4,128,256]{2,1,0:T(8,128)(2,1)}, bf16[4,128,256]{2,1,0:T(8,128)(2,1)S(1)}, u32[]{:S(2)}, u32[]{:S(2)}) collective-permute-start(bf16[4,128,256]{2,1,0:T(8,128)(2,1)} %get-tuple-element.25), channel_id=1, source_target_pairs={{0,1},{1,2},{2,3},{3,4},{4,5},{5,6},{6,7},{7,8},{8,9},{9,10},{10,1... | collective-permute-start | bytes 786440 | tf_op jit(solution)/shard_map/ppermute | solution.py:479
  94.0 28.5 %collective-permute-start.7 = (bf16[4,128,256]{2,1,0:T(8,128)(2,1)}, bf16[4,128,256]{2,1,0:T(8,128)(2,1)S(1)}, u32[]{:S(2)}, u32[]{:S(2)}) collective-permute-start(bf16[4,128,256]{2,1,0:T(8,128)(2,1)} %get-tuple-element.26), channel_id=1, source_target_pairs={{1,0},{2,1},{3,2},{4,3},{5,4},{6,5},{7,6},{8,7},{9,8},{10,9},{11,1... | collective-permute-start | bytes 786440 | tf_op jit(solution)/shard_map/ppermute | solution.py:480
  95.9 26.6 %collective-permute-start.4 = (bf16[8,128,256]{2,1,0:T(8,128)(2,1)}, bf16[8,128,256]{2,1,0:T(8,128)(2,1)S(1)}, u32[]{:S(2)}, u32[]{:S(2)}) collective-permute-start(bf16[8,128,256]{2,1,0:T(8,128)(2,1)} %get-tuple-element.23), channel_id=1, source_target_pairs={{0,16},{16,32},{32,48},{48,64},{64,80},{80,96},{96,112},{1,17},{17... | collective-permute-start | bytes 1572872 | tf_op jit(solution)/shard_map/ppermute | solution.py:479
  98.1 24.4 %collective-permute-start.5 = (bf16[8,128,256]{2,1,0:T(8,128)(2,1)}, bf16[8,128,256]{2,1,0:T(8,128)(2,1)S(1)}, u32[]{:S(2)}, u32[]{:S(2)}) collective-permute-start(bf16[8,128,256]{2,1,0:T(8,128)(2,1)} %get-tuple-element.24), channel_id=1, source_target_pairs={{16,0},{32,16},{48,32},{64,48},{80,64},{96,80},{112,96},{17,1},{33... | collective-permute-start | bytes 1572872 | tf_op jit(solution)/shard_map/ppermute | solution.py:480
  122.5 0.7 copy-start.8
  122.5 0.8 copy-start.9
  122.5 0.9 copy-start.6
  122.5 1.1 copy-start.7
  161.7 18.1 %all-to-all-start.3 = ((bf16[128,16,128]{2,1,0:T(8,128)(2,1)}), bf16[128,16,128]{2,1,0:T(8,128)(2,1)S(1)}, u32[]{:S(2)}, u32[]{:S(2)}) async-start(bf16[128,16,128]{2,1,0:T(8,128)(2,1)} %total.3), calls=%async_computation.3 | async-start | bytes 1048576 | tf_op jit(solution)/shard_map/all_to_all | solution.py:112
  179.8 0.8 copy-start.2

commit v2 on v0

v2 whole, which is shorter than its diff:
```python
import jax
import jax.numpy as jnp
from jax import lax
from jax.experimental import pallas as pl
from jax.experimental.pallas import tpu as pltpu
from jax.sharding import PartitionSpec as P

courant = 0.2
ALL = ("gx", "gy", "gz")
BF = jnp.bfloat16
F32 = jnp.float32
NX, NY, NZ, R = 4, 8, 128, 256
ROWS = NY * NZ
whole = pl.BlockSpec(memory_space=pltpu.VMEM)
raw = pl.BlockSpec(memory_space=pl.ANY)
hbm = pl.BlockSpec(memory_space=pltpu.HBM)


def params(mib, **kw):
    return pltpu.CompilerParams(vmem_limit_bytes=mib * 1024 * 1024, **kw)


def cost(flops, bytes_accessed):
    return pl.CostEstimate(flops=flops, bytes_accessed=bytes_accessed, transcendentals=0)


def tri_masks():
    row = lax.broadcasted_iota(jnp.int32, (128, 128), 0)
    col = lax.broadcasted_iota(jnp.int32, (128, 128), 1)
    return row, col


def store_packed(out_ref, k, a, b, d):
    row, col = tri_masks()
    out_ref[k * 256 : k * 256 + 128, :] = jnp.where(row <= col, a, d).astype(BF)
    out_ref[k * 256 + 128 : k * 256 + 256, :] = b.astype(BF)
    return jnp.sum(jnp.where(row == col, d, 0.0), axis=0, keepdims=True)


def store_diagonals(out_ref, diagonals):
    zeros = jnp.zeros((10, 128), F32)
    out_ref[1536:1552, :] = jnp.concatenate(diagonals + [zeros], axis=0).astype(BF)
    out_ref[1552:2048, :] = jnp.zeros((496, 128), BF)


def load_packed(packed_ref, k):
    row, col = tri_masks()
    t = packed_ref[k * 256 : k * 256 + 128, :].astype(F32)
    b = packed_ref[k * 256 + 128 : k * 256 + 256, :].astype(F32)
    diag = packed_ref[1536:1552, :].astype(F32)[k : k + 1, :]
    tt = t.T
    a = jnp.where(row <= col, t, tt)
    d = jnp.where(row > col, t, jnp.where(row < col, tt, jnp.broadcast_to(diag, (128, 128))))
    return a, b, b.T, d


def rate_rows(speeds_ref, signs_ref):
    rows = []
    for d in range(3):
        chosen = signs_ref[d : d + 1, :].astype(F32)
        speed = speeds_ref[d : d + 1, :]
        rows.append(speed * chosen)
        rows.append(speed * (1.0 - chosen))
    return rows


def gram_kernel(factors_ref, speeds_ref, signs_ref, out_ref, turned_ref, acc_ref):
    rows = rate_rows(speeds_ref, signs_ref)
    turned = factors_ref[...].astype(F32).T
    for k in range(6):
        turned_ref[k * 256 : k * 256 + 256, :] = (turned * rows[k]).astype(BF)
    acc_ref[...] = jnp.dot(turned_ref[...], factors_ref[...], preferred_element_type=F32)
    diagonals = []
    for k in range(6):
        g = acc_ref.at[pl.ds(k * 256, 256), :]
        diagonals.append(
            store_packed(out_ref, k, g[:128, :128], g[:128, 128:], g[128:, 128:])
        )
    store_diagonals(out_ref, diagonals)


def gram(factors, speeds, signs):
    return pl.pallas_call(
        gram_kernel,
        out_shape=jax.ShapeDtypeStruct((2048, 128), BF),
        in_specs=[whole] * 3,
        out_specs=whole,
        scratch_shapes=[pltpu.VMEM((1536, 2048), BF), pltpu.VMEM((1536, 256), F32)],
        compiler_params=params(20),
        cost_estimate=cost(2 * 2048 * 256 * 1536, 2 << 20),
        name="gram",
    )(factors, speeds, signs)


def total_kernel(parts_ref, out_ref):
    total = jnp.sum(parts_ref[...].astype(F32), axis=0).astype(BF)
    out_ref[...] = jnp.broadcast_to(total[None], (128, 16, 128))


def scatter_sum(packed):
    pieces = packed.reshape(128, 16, 128)
    mine = lax.all_to_all(pieces, ALL, split_axis=0, concat_axis=0, tiled=True)
    return pl.pallas_call(
        total_kernel,
        out_shape=jax.ShapeDtypeStruct((128, 16, 128), BF),
        in_specs=[whole],
        out_specs=whole,
        compiler_params=params(4),
        cost_estimate=cost(1 << 18, 1 << 20),
        name="total",
    )(mine)


def gather(copies):
    everything = lax.all_to_all(copies, ALL, split_axis=0, concat_axis=0, tiled=True)
    return everything.reshape(2048, 128)


GRID = (NX, NY, NZ, R)
CELLS = NX * NY


def edges_kernel(
    state_hbm, cot_hbm, mask_ref, xlo_ref, xhi_ref, ylo_ref, yhi_ref, sxlo_ref, sxhi_ref, sem
):
    copies = [
        pltpu.make_async_copy(cot_hbm.at[0], xlo_ref, sem.at[0]),
        pltpu.make_async_copy(cot_hbm.at[NX - 1], xhi_ref, sem.at[1]),
        pltpu.make_async_copy(cot_hbm.at[:, 0], ylo_ref.at[1], sem.at[2]),
        pltpu.make_async_copy(cot_hbm.at[:, NY - 1], yhi_ref.at[1], sem.at[3]),
        pltpu.make_async_copy(state_hbm.at[:, 0], ylo_ref.at[0], sem.at[4]),
        pltpu.make_async_copy(state_hbm.at[:, NY - 1], yhi_ref.at[0], sem.at[5]),
        pltpu.make_async_copy(state_hbm.at[0], sxlo_ref, sem.at[6]),
        pltpu.make_async_copy(state_hbm.at[NX - 1], sxhi_ref, sem.at[7]),
    ]
    for copy in copies:
        copy.start()
    columns = mask_ref[...].reshape(CELLS, NZ).astype(F32).T

    def gate(r):
        return jnp.broadcast_to(columns[:, r : r + 1], (NZ, R)).astype(BF)

    for copy in copies:
        copy.wait()
    for y in range(NY):
        xlo_ref[y] = xlo_ref[y] * gate(y)
        xhi_ref[y] = xhi_ref[y] * gate((NX - 1) * NY + y)
    for x in range(NX):
        ylo_ref[1, x] = ylo_ref[1, x] * gate(x * NY)
        yhi_ref[1, x] = yhi_ref[1, x] * gate(x * NY + NY - 1)


x_face = jax.ShapeDtypeStruct((NY, NZ, R), BF)
y_face = jax.ShapeDtypeStruct((NX, NZ, R), BF)
y_faces = jax.ShapeDtypeStruct((2, NX, NZ, R), BF)


def edges(state, cotangent, mask):
    return pl.pallas_call(
        edges_kernel,
        out_shape=(x_face, x_face, y_faces, y_faces, x_face, x_face),
        in_specs=[hbm, hbm, whole],
        out_specs=(whole,) * 6,
        scratch_shapes=[pltpu.SemaphoreType.DMA((8,))],
        compiler_params=params(56),
        cost_estimate=cost(1 << 20, 6 << 20),
        name="edges",
    )(state, cotangent, mask)


PADDED = (NX + 2, NY + 2, NZ, R)
field_scratch = [
    pltpu.VMEM(PADDED, BF),
    pltpu.VMEM((NX + 1, ROWS, R), BF),
    pltpu.VMEM((NX, ROWS + NZ, R), BF),
    pltpu.VMEM((NX, ROWS, R), BF),
    pltpu.VMEM((NX, ROWS, R), BF),
    pltpu.SemaphoreType.DMA((NX + 4,)),
]


def start_loads(padded, sem, centre, xlo, xhi, ylo, yhi):
    inside = pl.ds(1, NY)
    planes = pl.ds(1, NX)
    pairs = [
        (xlo, padded.at[0, inside]),
        (ylo, padded.at[planes, 0]),
        (yhi, padded.at[planes, NY + 1]),
    ]
    pairs += [(centre.at[p], padded.at[p + 1, inside]) for p in range(NX)]
    pairs.append((xhi, padded.at[NX + 1, inside]))
    copies = [pltpu.make_async_copy(a, b, sem.at[i]) for i, (a, b) in enumerate(pairs)]
    for copy in copies:
        copy.start()
    return copies


def wait_all(copies):
    for copy in copies:
        copy.wait()


GROUP = 4


def at_row(y):
    return pl.ds(pl.multiple_of(y * NZ, NZ), NZ)


def build(copies, padded, dx, dy, dzp, dzm, gates=None):
    place = lax.broadcasted_iota(jnp.int32, (NZ, R), 0)
    wait_all(copies[:3])
    for p in range(NX):
        copies[3 + p].wait()

        def some_rows(n, carry, p=p):
            y0 = n * GROUP
            below = padded[p + 1, y0]
            for j in range(GROUP):
                y = y0 + j
                centre = padded[p + 1, y + 1]
                if gates is not None:
                    centre = centre * gate_of(gates, p * NY + y).astype(BF)
                    padded[p + 1, y + 1] = centre
                dx[p, at_row(y), :] = centre - padded[p, y + 1]
                dy[p, at_row(y), :] = centre - below
                below = centre
                wide = centre.astype(F32)
                minus = wide - jnp.where(place > 0, pltpu.roll(wide, 1, 0), 0.0)
                plus = jnp.where(place < NZ - 1, pltpu.roll(minus, NZ - 1, 0), -wide)
                dzm[p, at_row(y), :] = minus.astype(BF)
                dzp[p, at_row(y), :] = plus.astype(BF)
            return carry

        lax.fori_loop(0, NY // GROUP, some_rows, 0)
        dy[p, ROWS : ROWS + NZ, :] = padded[p + 1, NY + 1] - padded[p + 1, NY]
    copies[NX + 3].wait()

    def last_plane(y, carry):
        dx[NX, at_row(y), :] = padded[NX + 1, y + 1] - padded[NX, y + 1]
        return carry

    lax.fori_loop(0, NY, last_plane, 0, unroll=4)


def pieces(p, dx, dy, dzp, dzm):
    return [
        dx[p + 1], dx[p], dy[p, NZ : NZ + ROWS, :], dy[p, 0:ROWS, :], dzp[p], dzm[p],
    ]


def times(p, differences, mats_ref):
    return jnp.dot(
        jnp.concatenate(pieces(p, *differences), axis=1), mats_ref[...],
        preferred_element_type=F32,
    )


def add_products(total, left, p, differences):
    turned = left.T
    for k, piece in enumerate(pieces(p, *differences)):
        total[:, k * 256 : k * 256 + 256] += jnp.dot(turned, piece, preferred_element_type=F32)


def fill_gates(gates, mask_ref):
    columns = mask_ref[...].reshape(CELLS, NZ).astype(F32).T
    for r in range(CELLS):
        gates[r] = jnp.broadcast_to(columns[:, r : r + 1], (NZ, 128))


def gate_of(gates, r):
    gate = gates[r]
    return jnp.concatenate([gate, gate], axis=1)


def inner_kernel(
    packed_ref, mask_ref, cot_ref, xlo_hbm, xhi_hbm, ylo_hbm, yhi_hbm,
    hi_ref, base_ref, hxlo_hbm, hxhi_hbm, hylo_hbm, hyhi_hbm, back_ref, flow_ref,
    padded, dx, dy, dzp, dzm, sem, gates, out_sem,
):
    copies = start_loads(padded, sem, cot_ref, xlo_hbm, xhi_hbm, ylo_hbm.at[1], yhi_hbm.at[1])
    fill_gates(gates, mask_ref)
    for k in range(6):
        a, b, c, e = load_packed(packed_ref, k)
        sign = 1.0 if k % 2 == 0 else -1.0
        other = k + 1 - 2 * (k % 2)
        for ref, at, s in ((back_ref, k * 256, sign), (flow_ref, other * 256, -sign)):
            ref[at : at + 128, :128] = (s * a).astype(BF)
            ref[at : at + 128, 128:] = (s * b).astype(BF)
            ref[at + 128 : at + 256, :128] = (s * c).astype(BF)
            ref[at + 128 : at + 256, 128:] = (s * e).astype(BF)
    differences = (dx, dy, dzp, dzm)
    build(copies, padded, *differences, gates=gates)

    def outs(p):
        return [
            pltpu.make_async_copy(hi_ref.at[p, 0], hylo_hbm.at[p], out_sem.at[0, p]),
            pltpu.make_async_copy(hi_ref.at[p, NY - 1], hyhi_hbm.at[p], out_sem.at[1, p]),
        ]

    first = pltpu.make_async_copy(hi_ref.at[0], hxlo_hbm, out_sem.at[2, 0])
    last = pltpu.make_async_copy(hi_ref.at[NX - 1], hxhi_hbm, out_sem.at[2, 1])

    def one_plane(p, carry):
        back = times(p, differences, back_ref)
        for y in range(NY):
            half = 0.5 * cot_ref[p, y].astype(F32)
            inner = half + (0.5 * courant) * back[y * NZ : (y + 1) * NZ, :]
            hi_ref[p, y] = (gate_of(gates, p * NY + y) * inner).astype(BF)
            base_ref[p, y] = half + inner
        for copy in outs(p):
            copy.start()

        @pl.when(p == 0)
        def _():
            first.start()

        return carry

    lax.fori_loop(0, NX, one_plane, 0)
    last.start()
    for p in range(NX):
        wait_all(outs(p))
    wait_all([first, last])


def inner_step(packed, cotangent, mask, xlo, xhi, ylo, yhi):
    return pl.pallas_call(
        inner_kernel,
        out_shape=(
            pltpu.VMEM(GRID, BF), pltpu.VMEM(GRID, F32),
            x_face, x_face, y_face, y_face, pltpu.VMEM((1536, 256), BF), pltpu.VMEM((1536, 256), BF),
        ),
        in_specs=[whole, whole, whole] + [raw] * 4,
        out_specs=(whole, whole) + (hbm,) * 4 + (whole, whole),
        scratch_shapes=field_scratch
        + [pltpu.VMEM((CELLS, NZ, 128), F32), pltpu.SemaphoreType.DMA((3, NX))],
        compiler_params=params(20),
        cost_estimate=cost(2 * 4096 * 256 * 1536, 14 << 20),
        name="inner",
    )(packed, mask, cotangent, xlo, xhi, ylo, yhi)


def middle_kernel(
    flow_ref, mask_ref, state_hbm, sxlo, sxhi, cot_hbm, hxlo, hxhi, ylo, yhi,
    grads_ref, state_pad, sdx, sdy, sdzp, sdzm, sem_s, held_pad, hdx, hdy, hdzp, hdzm, sem_h,
    gates,
):
    held_copies = start_loads(held_pad, sem_h, cot_hbm, hxlo, hxhi, ylo.at[1], yhi.at[1])
    state_copies = start_loads(state_pad, sem_s, state_hbm, sxlo, sxhi, ylo.at[0], yhi.at[0])
    fill_gates(gates, mask_ref)
    grads_ref[...] = jnp.zeros_like(grads_ref)
    states, helds = (sdx, sdy, sdzp, sdzm), (hdx, hdy, hdzp, hdzm)
    build(held_copies, held_pad, *helds, gates=gates)
    build(state_copies, state_pad, *states)

    def one_plane(p, carry):
        flow = times(p, states, flow_ref)
        rows = []
        for y in range(NY):
            own = state_pad[p + 1, y + 1].astype(F32)
            moved = courant * flow[y * NZ : (y + 1) * NZ, :]
            rows.append((own + gate_of(gates, p * NY + y) * moved).astype(BF))
        for y in range(NY):
            state_pad[p + 1, y + 1] = rows[y]
        return carry

    lax.fori_loop(0, NX, one_plane, 0)

    def products(p, carry):
        middle = state_pad[p + 1, 1 : NY + 1].reshape(ROWS, R)
        add_products(grads_ref, middle, p, helds)
        return carry

    lax.fori_loop(0, NX, products, 0)


def middle_step(flow_mats, mask, state, state_x, cotangent, held_x, y_halos):
    return pl.pallas_call(
        middle_kernel,
        out_shape=pltpu.VMEM((256, 1536), F32),
        in_specs=[whole, whole, whole, raw, raw, whole] + [raw] * 4,
        out_specs=whole,
        scratch_shapes=field_scratch * 2
        + [pltpu.VMEM((CELLS, NZ, 128), F32)],
        compiler_params=params(34),
        cost_estimate=cost(4 * 4096 * 256 * 1536, 8 << 20),
        name="middle",
    )(flow_mats, mask, state, *state_x, cotangent, *held_x, *y_halos)


def last_kernel(
    held_grads_ref, state_ref, hi_ref, back_ref, base_ref, xlo_hbm, xhi_hbm, ylo_hbm, yhi_hbm,
    packed_ref, out_hbm, padded, dx, dy, dzp, dzm, sem, total, out, out_sem,
):
    copies = start_loads(padded, sem, hi_ref, xlo_hbm, xhi_hbm, ylo_hbm, yhi_hbm)
    total[...] = 0.5 * held_grads_ref[...]
    differences = (dx, dy, dzp, dzm)
    build(copies, padded, *differences)

    def out_copy(p):
        return pltpu.make_async_copy(out.at[p], out_hbm.at[p], out_sem.at[p])

    def one_plane(p, carry):
        back = times(p, differences, back_ref)
        for y in range(NY):
            out[p, y] = (base_ref[p, y] + courant * back[y * NZ : (y + 1) * NZ, :]).astype(BF)
        out_copy(p).start()
        return carry

    lax.fori_loop(0, NX, one_plane, 0)

    def products(p, carry):
        add_products(total, state_ref[p].reshape(ROWS, R), p, differences)
        return carry

    lax.fori_loop(0, NX, products, 0)
    diagonals = []
    for k in range(6):
        scale = courant if k % 2 == 0 else -courant
        g = total.at[:, pl.ds(k * 256, 256)]
        a, b, c, d = g[:128, :128], g[:128, 128:], g[128:, :128], g[128:, 128:]
        diagonals.append(
            store_packed(packed_ref, k, scale * (a + a.T), scale * (b + c.T), scale * (d + d.T))
        )
    store_diagonals(packed_ref, diagonals)
    for p in range(NX):
        out_copy(p).wait()


def last_step(held_grads, state, hi, back_mats, base, xlo, xhi, ylo, yhi):
    return pl.pallas_call(
        last_kernel,
        out_shape=(jax.ShapeDtypeStruct((2048, 128), BF), jax.ShapeDtypeStruct(GRID, BF)),
        in_specs=[whole] * 5 + [raw] * 4,
        out_specs=(whole, hbm),
        scratch_shapes=field_scratch
        + [
            pltpu.VMEM((256, 1536), F32),
            pltpu.VMEM(GRID, BF),
            pltpu.SemaphoreType.DMA((NX,)),
        ],
        compiler_params=params(24),
        cost_estimate=cost(4 * 4096 * 256 * 1536, 5 << 20),
        name="last",
    )(held_grads, state, hi, back_mats, base, xlo, xhi, ylo, yhi)


CHUNK = 512


def weighted_kernel(factors_ref, speeds_ref, signs_ref, out_ref):
    rows = rate_rows(speeds_ref, signs_ref)
    columns = jnp.concatenate(rows + rows[:2], axis=0).T
    values = factors_ref[...].astype(F32)
    for k in range(6):
        rate = jnp.broadcast_to(columns[:, k : k + 1], (CHUNK, R))
        out_ref[:, k * 256 : k * 256 + 256] = (rate * values).astype(BF)


def weigh(factors, speeds, signs):
    rows = factors.shape[0]
    return pl.pallas_call(
        weighted_kernel,
        grid=(rows // CHUNK,),
        out_shape=jax.ShapeDtypeStruct((rows, 1536), BF),
        in_specs=[
            pl.BlockSpec((CHUNK, R), lambda i: (i, 0)),
            pl.BlockSpec((3, CHUNK), lambda i: (0, i)),
            pl.BlockSpec((3, CHUNK), lambda i: (0, i)),
        ],
        out_specs=pl.BlockSpec((CHUNK, 1536), lambda i: (i, 0)),
        compiler_params=params(56),
        cost_estimate=cost(2048 * 1536, 8 << 20),
        name="weigh",
    )(factors, speeds, signs)


def final_kernel(packed_ref, weighted_ref, out_ref, mats):
    @pl.when(pl.program_id(0) == 0)
    def _():
        for k in range(6):
            a, b, c, d = load_packed(packed_ref, k)
            at = k * 256
            mats[at : at + 128, :128] = a.astype(BF)
            mats[at : at + 128, 128:] = b.astype(BF)
            mats[at + 128 : at + 256, :128] = c.astype(BF)
            mats[at + 128 : at + 256, 128:] = d.astype(BF)

    out_ref[...] = jnp.dot(weighted_ref[...], mats[...], preferred_element_type=F32)


def constant(shape):
    return pl.BlockSpec(shape, lambda i: (0,) * len(shape), pipeline_mode=pl.Buffered(1))


def final_step(packed, weighted):
    rows = weighted.shape[0]
    return pl.pallas_call(
        final_kernel,
        grid=(rows // CHUNK,),
        out_shape=jax.ShapeDtypeStruct((rows, R), F32),
        in_specs=[constant((2048, 128)), pl.BlockSpec((CHUNK, 1536), lambda i: (i, 0))],
        out_specs=pl.BlockSpec((CHUNK, R), lambda i: (i, 0)),
        scratch_shapes=[pltpu.VMEM((1536, 256), BF)],
        compiler_params=params(56),
        cost_estimate=cost(2 * 2048 * 256 * 1536, 8 << 20),
        name="final",
    )(packed, weighted)


def shift(axis, lo, hi):
    count = lax.axis_size(axis)
    forward = [(i, i + 1) for i in range(count - 1)]
    backward = [(i + 1, i) for i in range(count - 1)]
    return lax.ppermute(hi, axis, forward), lax.ppermute(lo, axis, backward)


Y_AXES = ("gy", "gz")


def near(x):
    return pltpu.with_memory_space_constraint(x, pltpu.VMEM)


def on_device(state, cotangent, factors, speeds, signs, mask):
    hxlo, hxhi, ylo, yhi, sxlo, sxhi = edges(state, cotangent, mask)
    speeds, hxlo, hxhi = lax.optimization_barrier((speeds, hxlo, hxhi))
    held_x = shift("gx", hxlo, hxhi)
    copies = scatter_sum(gram(factors, speeds, signs))
    y_halos = shift(Y_AXES, ylo, yhi)
    copies, sxlo, sxhi = lax.optimization_barrier((copies, sxlo, sxhi))
    state_x = shift("gx", sxlo, sxhi)
    packed = gather(copies)
    hi, base, hxlo, hxhi, hylo, hyhi, back_mats, flow_mats = inner_step(
        near(packed), near(cotangent), mask, *held_x, *y_halos
    )
    hi_halos = shift("gx", hxlo, hxhi) + shift(Y_AXES, hylo, hyhi)
    held_grads = middle_step(
        near(flow_mats), mask, near(state), state_x, near(cotangent), held_x, y_halos
    )
    partial, grad_state = last_step(
        near(held_grads), near(state), near(hi), near(back_mats), near(base), *hi_halos
    )
    sums = scatter_sum(partial)
    weighted = weigh(factors, speeds, signs)
    symmetric = gather(sums)
    grad_factors = final_step(symmetric, weighted)
    return (grad_state, grad_factors)


def solution(mesh):
    placed = (
        P("gx", ("gy", "gz"), None, None),
        P("gx", ("gy", "gz"), None, None),
        P(ALL, None),
        P(None, ALL),
        P(None, ALL),
        P("gx", ("gy", "gz"), None),
    )
    return jax.shard_map(
        on_device,
        mesh=mesh,
        in_specs=placed,
        out_specs=(P("gx", ("gy", "gz"), None, None), P(ALL, None)),
        check_vma=False,
    )
```

time: 421 us -> 147 us (0.35); the launches traced: 413 us -> 147 us
  waiting for transfers between devices: 127 us -> 21.4 us
  local copies, waits for them, and re-layouts: 70 us -> 0.83 us
  blocking collectives: 78.6 us -> 24.8 us
  Pallas kernels: 0 us -> 51.1 us
  other arithmetic: 47.5 us -> 0 us
  matrix products: 43.8 us -> 0 us
  starting transfers between devices: 31.4 us -> 47.6 us
  between operations: 15.1 us -> 0.89 us
    psum x1 -> x0, waiting for transfers between devices: 112 us -> none  [on_device(): total_grad = lax.psum(local_grad, ('gx', 'gy', 'gz'))]
    psum x1 -> x0, blocking collectives: 78.6 us -> none  [on_device(): flux_sum = lax.psum(gram_local, ('gx', 'gy', 'gz'))]
    pallas_call x0 -> x9, Pallas kernels: none -> 51.1 us  [the longest x1 12.4 us: middle_step(): pl.pallas_call(middle_kernel, out_shape=pltpu.VMEM((256, 1536), F32), in_...]
    dot_general x17 -> x0, matrix products: 43.8 us -> none  [the longest x6 14.2 us: backward_terms(): jnp.dot(diff_pairs[direction], back_mats[direction], preferred_element_ty...]
    convert_element_type x9 -> x0, other arithmetic: 32.7 us -> none  [the longest x3 18.9 us: neighbour_pairs(): lower_diff = (centre - lower_side.astype(jnp.float32)).astype(jnp.bfloat16)]
    all_to_all x0 -> x1, blocking collectives: none -> 24.8 us  [scatter_sum(): mine = lax.all_to_all(pieces, ALL, split_axis=0, concat_axis=0, tiled=True)]
    all_to_all x0 -> x3, starting transfers between devices: none -> 23.5 us  [the longest x2 12 us: gather(): lax.all_to_all(copies, ALL, split_axis=0, concat_axis=0, tiled=True)]
    unnamed x126 -> x14, local copies, waits for them, and re-layouts: 23.1 us -> 0.83 us
  transfers between devices with their start and end apart: 13 -> 13, of which waited for: 5 -> 3; matrix products, arithmetic and copies ran while one was open for 23% -> 0% of each run, Pallas kernels for 0% -> 18%
where the time goes in v2:
time: 147 us
  Pallas kernels  51.1 us (35%)
  starting transfers between devices  47.6 us (32%)
  blocking collectives  24.8 us (17%)
  waiting for transfers between devices  21.4 us (15%)
    all_to_all x1, blocking collectives, scatter_sum(): mine = lax.all_to_all(pieces, ALL, split_axis=0, concat_axis=0, tiled=True)  24.8 us
    ppermute x10, starting transfers between devices, shift(): return (lax.ppermute(hi, axis, forward), lax.ppermute(lo, axis, backward))  24 us
    all_to_all x2, waiting for transfers between devices, gather(): lax.all_to_all(copies, ALL, split_axis=0, concat_axis=0, tiled=True)  17.5 us
    pallas_call x1, Pallas kernels, middle_step(): pl.pallas_call(middle_kernel, out_shape=pltpu.VMEM((256, 1536), F32), in_...  12.4 us
    all_to_all x2, starting transfers between devices, gather(): lax.all_to_all(copies, ALL, split_axis=0, concat_axis=0, tiled=True)  12 us
    all_to_all x1, starting transfers between devices, scatter_sum(): mine = lax.all_to_all(pieces, ALL, split_axis=0, concat_axis=0, tiled=True)  11.5 us
    pallas_call x1, Pallas kernels, last_step(): pl.pallas_call(last_kernel, out_shape=(jax.ShapeDtypeStruct((2048, 128),...  10.4 us
    pallas_call x1, Pallas kernels, inner_step(): pl.pallas_call(inner_kernel, out_shape=(pltpu.VMEM(GRID, BF), pltpu.VMEM(...  7.62 us
  transfers between devices with their start and end apart: 13, of which 3 were waited for; matrix products, arithmetic and copies ran while one was open for 0% of the time, Pallas kernels for 18%

profile of v2, /device:TPU:1, one launch (start us, length us, event | category | flops | bytes accessed | tf_op | source)
XLA Modules:
  0.0 146.6 jit_solution(5409146999238747692)
XLA Ops:
  0.6 0.0 copy-start.3
  0.6 0.0 copy-start.4
  0.7 0.0 copy-start.2
  0.7 4.5 %edges.1 = (bf16[8,128,256]{2,1,0:T(8,128)(2,1)}, bf16[8,128,256]{2,1,0:T(8,128)(2,1)}, bf16[2,4,128,256]{3,2,1,0:T(8,128)(2,1)}, bf16[2,4,128,256]{3,2,1,0:T(8,...) custom-call(bf16[4,8,128,256]{3,2,1,0:T(8,128)(2,1)} %state_ref.1, ...), custom_call_target="tpu_custom_call" | custom-call | flops 1048576 | bytes 6291456 | tf_op jit(solution)/shard_map/edges/pallas_call | solution.py:159
  5.1 0.0 copy-done.3
  5.1 0.0 copy-done.4
  5.1 0.0 copy-done.2
  5.2 2.7 %gram.1 = bf16[2048,128]{1,0:T(8,128)(2,1)} custom-call(bf16[2048,256]{1,0:T(8,128)(2,1)S(1)} %copy-done.2, f32[3,2048]{1,0:T(4,128)S(1)} %copy-done.3, s32[3,2048]{1,0:T(4,128)S(1)} %copy-done.4), custom_call_target="tpu_custom_call" | custom-call | flops 1610612736 | bytes 2097152 | tf_op jit(solution)/shard_map/gram/pallas_call | solution.py:83
  7.9 0.0 copy-start
  7.9 0.0 copy-start.5
  7.9 11.5 %all-to-all-start = ((bf16[128,16,128]{2,1,0:T(8,128)(2,1)}), bf16[128,16,128]{2,1,0:T(8,128)(2,1)S(1)}, u32[]{:S(2)}, u32[]{:S(2)}) async-start(bf16[128,16,128]{2,1,0:T(8,128)(2,1)} %bitcast), calls=%async_computation | async-start | bytes 1048576 | tf_op jit(solution)/shard_map/all_to_all | solution.py:102
  19.4 3.3 %collective-permute-start = (bf16[8,128,256]{2,1,0:T(8,128)(2,1)}, bf16[8,128,256]{2,1,0:T(8,128)(2,1)S(1)}, u32[]{:S(2)}, u32[]{:S(2)}) collective-permute-start(bf16[8,128,256]{2,1,0:T(8,128)(2,1)} %get-tuple-element.30), channel_id=1, source_target_pairs={{0,16},{16,32},{32,48},{48,64},{64,80},{80,96},{96,112},{1,17},{17... | collective-permute-start | bytes 1572872 | tf_op jit(solution)/shard_map/ppermute | solution.py:516
  22.7 1.3 collective-permute-start.1
  24.0 3.7 %collective-permute-start.2 = (bf16[2,4,128,256]{3,2,1,0:T(8,128)(2,1)}, bf16[2,4,128,256]{3,2,1,0:T(8,128)(2,1)}, u32[]{:S(2)}, u32[]{:S(2)}) collective-permute-start(bf16[2,4,128,256]{3,2,1,0:T(8,128)(2,1)} %get-tuple-element.32), channel_id=1, source_target_pairs={{0,1},{1,2},{2,3},{3,4},{4,5},{5,6},{6,7},{7,8},{8,9},{9,10},{10,1... | collective-permute-start | bytes 1572872 | tf_op jit(solution)/shard_map/ppermute | solution.py:516
  27.6 1.9 %collective-permute-start.3 = (bf16[2,4,128,256]{3,2,1,0:T(8,128)(2,1)}, bf16[2,4,128,256]{3,2,1,0:T(8,128)(2,1)}, u32[]{:S(2)}, u32[]{:S(2)}) collective-permute-start(bf16[2,4,128,256]{3,2,1,0:T(8,128)(2,1)} %get-tuple-element.33), channel_id=1, source_target_pairs={{1,0},{2,1},{3,2},{4,3},{5,4},{6,5},{7,6},{8,7},{9,8},{10,9},{11,1... | collective-permute-start | bytes 1572872 | tf_op jit(solution)/shard_map/ppermute | solution.py:516
  29.6 3.9 %all-to-all-done.parts_ref = bf16[128,16,128]{2,1,0:T(8,128)(2,1)S(1)} async-done(((bf16[128,16,128]{2,1,0:T(8,128)(2,1)}), bf16[128,16,128]{2,1,0:T(8,128)(2,1)S(1)}, u32[]{:S(2)}, u32[]{:S(2)}) %all-to-all-start) | async-done | bytes 524320 | tf_op jit(solution)/shard_map/all_to_all | solution.py:102
  33.5 1.0 total.2
  34.5 8.2 %all-to-all-start.1 = ((bf16[128,16,128]{2,1,0:T(8,128)(2,1)}), bf16[128,16,128]{2,1,0:T(8,128)(2,1)S(1)}, u32[]{:S(2)}, u32[]{:S(2)}) async-start(bf16[128,16,128]{2,1,0:T(8,128)(2,1)} %total.2), calls=%async_computation.1 | async-start | bytes 1048576 | tf_op jit(solution)/shard_map/all_to_all | solution.py:115
  42.6 4.1 %collective-permute-start.4 = (bf16[8,128,256]{2,1,0:T(8,128)(2,1)}, bf16[8,128,256]{2,1,0:T(8,128)(2,1)}, u32[]{:S(2)}, u32[]{:S(2)}) collective-permute-start(bf16[8,128,256]{2,1,0:T(8,128)(2,1)} %get-tuple-element.35), channel_id=1, source_target_pairs={{0,16},{16,32},{32,48},{48,64},{64,80},{80,96},{96,112},{1,17},{17... | collective-permute-start | bytes 1572872 | tf_op jit(solution)/shard_map/ppermute | solution.py:516
  46.7 0.0 collective-permute-done.xlo_hbm.hxlo
  46.7 1.3 collective-permute-start.5
  48.0 0.0 collective-permute-done.1.xhi_hbm.hxhi
  48.0 0.0 collective-permute-done.2.ylo_hbm.ylo
  48.0 0.0 collective-permute-done.3.yhi_hbm.yhi
  48.0 8.7 %all-to-all-done.1 = bf16[128,16,128]{2,1,0:T(8,128)(2,1)S(1)} async-done(((bf16[128,16,128]{2,1,0:T(8,128)(2,1)}), bf16[128,16,128]{2,1,0:T(8,128)(2,1)S(1)}, u32[]{:S(2)}, u32[]{:S(2)}) %all-to-all-start.1) | async-done | bytes 524320 | tf_op jit(solution)/shard_map/all_to_all | solution.py:115
  56.7 0.0 copy-done
  56.8 0.0 copy-done.5
  56.8 7.6 %inner.1 = (bf16[4,8,128,256]{3,2,1,0:T(8,128)(2,1)S(1)}, f32[4,8,128,256]{3,2,1,0:T(8,128)S(1)}, bf16[8,128,256]{2,1,0:T(8,128)(2,1)S(1)}, bf16[8,128,256]{2,1,...) custom-call(bf16[2048,128]{1,0:T(8,128)(2,1)S(1)} %bitcast.4, ...), custom_call_target="tpu_custom_call" | custom-call | flops 3221225472 | bytes 14680064 | tf_op jit(solution)/shard_map/inner/pallas_call | solution.py:328
  64.4 2.3 %collective-permute-start.6 = (bf16[8,128,256]{2,1,0:T(8,128)(2,1)S(1)}, bf16[8,128,256]{2,1,0:T(8,128)(2,1)S(1)}, u32[]{:S(2)}, u32[]{:S(2)}) collective-permute-start(bf16[8,128,256]{2,1,0:T(8,128)(2,1)S(1)} %get-tuple-element.40), channel_id=1, source_target_pairs={{0,16},{16,32},{32,48},{48,64},{64,80},{80,96},{96,112},{1,17},{17... | collective-permute-start | bytes 1572872 | tf_op jit(solution)/shard_map/ppermute | solution.py:516
  66.7 1.3 collective-permute-start.7
  68.0 2.9 %collective-permute-start.8 = (bf16[4,128,256]{2,1,0:T(8,128)(2,1)S(1)}, bf16[4,128,256]{2,1,0:T(8,128)(2,1)S(1)}, u32[]{:S(2)}, u32[]{:S(2)}) collective-permute-start(bf16[4,128,256]{2,1,0:T(8,128)(2,1)S(1)} %get-tuple-element.42), channel_id=1, source_target_pairs={{0,1},{1,2},{2,3},{3,4},{4,5},{5,6},{6,7},{7,8},{8,9},{9,10},{10,1... | collective-permute-start | bytes 786440 | tf_op jit(solution)/shard_map/ppermute | solution.py:516
  70.9 0.0 collective-permute-done.4.sxlo
  70.9 2.1 %collective-permute-start.9 = (bf16[4,128,256]{2,1,0:T(8,128)(2,1)S(1)}, bf16[4,128,256]{2,1,0:T(8,128)(2,1)S(1)}, u32[]{:S(2)}, u32[]{:S(2)}) collective-permute-start(bf16[4,128,256]{2,1,0:T(8,128)(2,1)S(1)} %get-tuple-element.43), channel_id=1, source_target_pairs={{1,0},{2,1},{3,2},{4,3},{5,4},{6,5},{7,6},{8,7},{9,8},{10,9},{11,1... | collective-permute-start | bytes 786440 | tf_op jit(solution)/shard_map/ppermute | solution.py:516
  73.0 0.0 collective-permute-done.5.sxhi
  73.0 0.0 copy-done.1
  73.0 12.4 %middle.1.held_grads_ref = f32[256,1536]{1,0:T(8,128)S(1)} custom-call(bf16[1536,256]{1,0:T(8,128)(2,1)S(1)} %get-tuple-element.34.flow_ref, s32[4,8,128]{2,1,0:T(8,128)S(1)} %copy-done.5, bf16[4,8,128,256]{3,2,1,0:T(8,128)(2,1)S(1)} %copy-done.1, bf16[8,128,256]{2,1,0:T(8,128)(2,1)} %collective-permute-done.4.sxlo, ...), custom_call_target="tpu_custom_call" | custom-call | flops 6442450944 | bytes 8388608 | tf_op jit(solution)/shard_map/middle/pallas_call | solution.py:379
  85.4 0.0 collective-permute-done.8.ylo_hbm
  85.4 0.0 collective-permute-done.9.yhi_hbm
  85.4 0.0 collective-permute-done.6.xlo_hbm
  85.4 0.0 collective-permute-done.7.xhi_hbm
  85.4 10.4 %last.1 = (bf16[2048,128]{1,0:T(8,128)(2,1)S(1)}, bf16[4,8,128,256]{3,2,1,0:T(8,128)(2,1)}) custom-call(f32[256,1536]{1,0:T(8,128)S(1)} %middle.1.held_grads_ref, bf16[4,8,128,256]{3,2,1,0:T(8,128)(2,1)S(1)} %copy-done.1, bf16[4,8,128,256]{3,2,1,0:T(8,128)(2,1)S(1)} %get-tuple-element.37.hi_ref, bf16[1536,256]{1,0:T(8,128)(2,1)S(1)} %get-tuple-element.38.back_ref, ...), custom_call_target="tpu_custom_call" | custom-call | flops 6442450944 | bytes 5242880 | tf_op jit(solution)/shard_map/last/pallas_call | solution.py:432
  95.8 24.8 %all_to_all.20.parts_ref = bf16[128,16,128]{2,1,0:T(8,128)(2,1)S(1)} all-to-all(bf16[128,16,128]{2,1,0:T(8,128)(2,1)S(1)} %bitcast.5), channel_id=1, replica_groups=mesh['gx'=8,'gy'=8,'gz'=2] {'gx','gy','gz'}, dimensions={0} | all-to-all | bytes 1048576 | tf_op jit(solution)/shard_map/all_to_all | solution.py:102
  120.7 1.0 total.3
  121.6 3.9 %all-to-all-start.3 = ((bf16[128,16,128]{2,1,0:T(8,128)(2,1)}), bf16[128,16,128]{2,1,0:T(8,128)(2,1)S(1)}, u32[]{:S(2)}, u32[]{:S(2)}) async-start(bf16[128,16,128]{2,1,0:T(8,128)(2,1)} %total.3), calls=%async_computation.3 | async-start | bytes 1048576 | tf_op jit(solution)/shard_map/all_to_all | solution.py:115
  125.5 5.5 %weigh.1.weighted_ref = bf16[2048,1536]{1,0:T(8,128)(2,1)} custom-call(bf16[2048,256]{1,0:T(8,128)(2,1)} %factors_ref.3, f32[3,2048]{1,0:T(4,128)} %speeds_ref.1, s32[3,2048]{1,0:T(4,128)} %signs_ref.3), custom_call_target="tpu_custom_call" | custom-call | flops 3145728 | bytes 8388608 | tf_op jit(solution)/shard_map/weigh/pallas_call | solution.py:463
  131.0 8.7 %all-to-all-done.3 = bf16[128,16,128]{2,1,0:T(8,128)(2,1)S(1)} async-done(((bf16[128,16,128]{2,1,0:T(8,128)(2,1)}), bf16[128,16,128]{2,1,0:T(8,128)(2,1)S(1)}, u32[]{:S(2)}, u32[]{:S(2)}) %all-to-all-start.3) | async-done | bytes 524320 | tf_op jit(solution)/shard_map/all_to_all | solution.py:115
  139.8 0.8 copy-done.6
  140.6 6.0 %final.1 = f32[2048,256]{1,0:T(8,128)} custom-call(bf16[2048,128]{1,0:T(8,128)(2,1)} %bitcast.6, bf16[2048,1536]{1,0:T(8,128)(2,1)} %weigh.1.weighted_ref), custom_call_target="tpu_custom_call" | custom-call | flops 1610612736 | bytes 8388608 | tf_op jit(solution)/shard_map/final/pallas_call | solution.py:499
  (2 shorter events, 0.0 us)
Async XLA Ops:
  0.6 4.5 %copy-start.3 = (f32[3,2048]{1,0:T(4,128)S(1)}, f32[3,2048]{1,0:T(4,128)}, u32[]{:S(2)}) copy-start(f32[3,2048]{1,0:T(4,128)} %speeds_ref.1) | copy-start | bytes 73732
  0.6 4.5 %copy-start.4 = (s32[3,2048]{1,0:T(4,128)S(1)}, s32[3,2048]{1,0:T(4,128)}, u32[]{:S(2)}) copy-start(s32[3,2048]{1,0:T(4,128)} %signs_ref.3) | copy-start | bytes 73732
  0.7 4.5 %copy-start.2 = (bf16[2048,256]{1,0:T(8,128)(2,1)S(1)}, bf16[2048,256]{1,0:T(8,128)(2,1)}, u32[]{:S(2)}) copy-start(bf16[2048,256]{1,0:T(8,128)(2,1)} %factors_ref.3) | copy-start | bytes 3145732
  7.9 48.9 %copy-start = (bf16[4,8,128,256]{3,2,1,0:T(8,128)(2,1)S(1)}, bf16[4,8,128,256]{3,2,1,0:T(8,128)(2,1)}, u32[]{:S(2)}) copy-start(bf16[4,8,128,256]{3,2,1,0:T(8,128)(2,1)} %cot_hbm.3) | copy-start | bytes 6291460
  7.9 48.9 %copy-start.5 = (s32[4,8,128]{2,1,0:T(8,128)S(1)}, s32[4,8,128]{2,1,0:T(8,128)}, u32[]{:S(2)}) copy-start(s32[4,8,128]{2,1,0:T(8,128)} %mask_ref.5) | copy-start | bytes 49156
  7.9 25.6 %all-to-all-start = ((bf16[128,16,128]{2,1,0:T(8,128)(2,1)}), bf16[128,16,128]{2,1,0:T(8,128)(2,1)S(1)}, u32[]{:S(2)}, u32[]{:S(2)}) async-start(bf16[128,16,128]{2,1,0:T(8,128)(2,1)} %bitcast), calls=%async_computation | async-start | bytes 1048576 | tf_op jit(solution)/shard_map/all_to_all | solution.py:102
  19.4 27.3 %collective-permute-start = (bf16[8,128,256]{2,1,0:T(8,128)(2,1)}, bf16[8,128,256]{2,1,0:T(8,128)(2,1)S(1)}, u32[]{:S(2)}, u32[]{:S(2)}) collective-permute-start(bf16[8,128,256]{2,1,0:T(8,128)(2,1)} %get-tuple-element.30), channel_id=1, source_target_pairs={{0,16},{16,32},{32,48},{48,64},{64,80},{80,96},{96,112},{1,17},{17... | collective-permute-start | bytes 1572872 | tf_op jit(solution)/shard_map/ppermute | solution.py:516
  22.7 25.3 %collective-permute-start.1 = (bf16[8,128,256]{2,1,0:T(8,128)(2,1)}, bf16[8,128,256]{2,1,0:T(8,128)(2,1)}, u32[]{:S(2)}, u32[]{:S(2)}) collective-permute-start(bf16[8,128,256]{2,1,0:T(8,128)(2,1)} %get-tuple-element.31), channel_id=1, source_target_pairs={{16,0},{32,16},{48,32},{64,48},{80,64},{96,80},{112,96},{17,1},{33... | collective-permute-start | bytes 1572872 | tf_op jit(solution)/shard_map/ppermute | solution.py:516
  24.0 24.0 %collective-permute-start.2 = (bf16[2,4,128,256]{3,2,1,0:T(8,128)(2,1)}, bf16[2,4,128,256]{3,2,1,0:T(8,128)(2,1)}, u32[]{:S(2)}, u32[]{:S(2)}) collective-permute-start(bf16[2,4,128,256]{3,2,1,0:T(8,128)(2,1)} %get-tuple-element.32), channel_id=1, source_target_pairs={{0,1},{1,2},{2,3},{3,4},{4,5},{5,6},{6,7},{7,8},{8,9},{9,10},{10,1... | collective-permute-start | bytes 1572872 | tf_op jit(solution)/shard_map/ppermute | solution.py:516
  27.6 20.4 %collective-permute-start.3 = (bf16[2,4,128,256]{3,2,1,0:T(8,128)(2,1)}, bf16[2,4,128,256]{3,2,1,0:T(8,128)(2,1)}, u32[]{:S(2)}, u32[]{:S(2)}) collective-permute-start(bf16[2,4,128,256]{3,2,1,0:T(8,128)(2,1)} %get-tuple-element.33), channel_id=1, source_target_pairs={{1,0},{2,1},{3,2},{4,3},{5,4},{6,5},{7,6},{8,7},{9,8},{10,9},{11,1... | collective-permute-start | bytes 1572872 | tf_op jit(solution)/shard_map/ppermute | solution.py:516
  34.5 22.3 %all-to-all-start.1 = ((bf16[128,16,128]{2,1,0:T(8,128)(2,1)}), bf16[128,16,128]{2,1,0:T(8,128)(2,1)S(1)}, u32[]{:S(2)}, u32[]{:S(2)}) async-start(bf16[128,16,128]{2,1,0:T(8,128)(2,1)} %total.2), calls=%async_computation.1 | async-start | bytes 1048576 | tf_op jit(solution)/shard_map/all_to_all | solution.py:115
  42.6 28.2 %collective-permute-start.4 = (bf16[8,128,256]{2,1,0:T(8,128)(2,1)}, bf16[8,128,256]{2,1,0:T(8,128)(2,1)}, u32[]{:S(2)}, u32[]{:S(2)}) collective-permute-start(bf16[8,128,256]{2,1,0:T(8,128)(2,1)} %get-tuple-element.35), channel_id=1, source_target_pairs={{0,16},{16,32},{32,48},{48,64},{64,80},{80,96},{96,112},{1,17},{17... | collective-permute-start | bytes 1572872 | tf_op jit(solution)/shard_map/ppermute | solution.py:516
  46.7 26.3 %collective-permute-start.5 = (bf16[8,128,256]{2,1,0:T(8,128)(2,1)}, bf16[8,128,256]{2,1,0:T(8,128)(2,1)}, u32[]{:S(2)}, u32[]{:S(2)}) collective-permute-start(bf16[8,128,256]{2,1,0:T(8,128)(2,1)} %get-tuple-element.36), channel_id=1, source_target_pairs={{16,0},{32,16},{48,32},{64,48},{80,64},{96,80},{112,96},{17,1},{33... | collective-permute-start | bytes 1572872 | tf_op jit(solution)/shard_map/ppermute | solution.py:516
  56.8 16.2 %copy-start.1 = (bf16[4,8,128,256]{3,2,1,0:T(8,128)(2,1)S(1)}, bf16[4,8,128,256]{3,2,1,0:T(8,128)(2,1)}, u32[]{:S(2)}) copy-start(bf16[4,8,128,256]{3,2,1,0:T(8,128)(2,1)} %state_ref.1) | copy-start | bytes 6291460
  64.4 21.0 %collective-permute-start.6 = (bf16[8,128,256]{2,1,0:T(8,128)(2,1)S(1)}, bf16[8,128,256]{2,1,0:T(8,128)(2,1)S(1)}, u32[]{:S(2)}, u32[]{:S(2)}) collective-permute-start(bf16[8,128,256]{2,1,0:T(8,128)(2,1)S(1)} %get-tuple-element.40), channel_id=1, source_target_pairs={{0,16},{16,32},{32,48},{48,64},{64,80},{80,96},{96,112},{1,17},{17... | collective-permute-start | bytes 1572872 | tf_op jit(solution)/shard_map/ppermute | solution.py:516
  66.7 18.7 %collective-permute-start.7 = (bf16[8,128,256]{2,1,0:T(8,128)(2,1)S(1)}, bf16[8,128,256]{2,1,0:T(8,128)(2,1)S(1)}, u32[]{:S(2)}, u32[]{:S(2)}) collective-permute-start(bf16[8,128,256]{2,1,0:T(8,128)(2,1)S(1)} %get-tuple-element.41), channel_id=1, source_target_pairs={{16,0},{32,16},{48,32},{64,48},{80,64},{96,80},{112,96},{17,1},{33... | collective-permute-start | bytes 1572872 | tf_op jit(solution)/shard_map/ppermute | solution.py:516
  68.0 17.4 %collective-permute-start.8 = (bf16[4,128,256]{2,1,0:T(8,128)(2,1)S(1)}, bf16[4,128,256]{2,1,0:T(8,128)(2,1)S(1)}, u32[]{:S(2)}, u32[]{:S(2)}) collective-permute-start(bf16[4,128,256]{2,1,0:T(8,128)(2,1)S(1)} %get-tuple-element.42), channel_id=1, source_target_pairs={{0,1},{1,2},{2,3},{3,4},{4,5},{5,6},{6,7},{7,8},{8,9},{9,10},{10,1... | collective-permute-start | bytes 786440 | tf_op jit(solution)/shard_map/ppermute | solution.py:516
  70.9 14.5 %collective-permute-start.9 = (bf16[4,128,256]{2,1,0:T(8,128)(2,1)S(1)}, bf16[4,128,256]{2,1,0:T(8,128)(2,1)S(1)}, u32[]{:S(2)}, u32[]{:S(2)}) collective-permute-start(bf16[4,128,256]{2,1,0:T(8,128)(2,1)S(1)} %get-tuple-element.43), channel_id=1, source_target_pairs={{1,0},{2,1},{3,2},{4,3},{5,4},{6,5},{7,6},{8,7},{9,8},{10,9},{11,1... | collective-permute-start | bytes 786440 | tf_op jit(solution)/shard_map/ppermute | solution.py:516
  121.6 18.1 %all-to-all-start.3 = ((bf16[128,16,128]{2,1,0:T(8,128)(2,1)}), bf16[128,16,128]{2,1,0:T(8,128)(2,1)S(1)}, u32[]{:S(2)}, u32[]{:S(2)}) async-start(bf16[128,16,128]{2,1,0:T(8,128)(2,1)} %total.3), calls=%async_computation.3 | async-start | bytes 1048576 | tf_op jit(solution)/shard_map/all_to_all | solution.py:115
  139.8 0.8 copy-start.6

commit v3 on v2

--- a/solution.py
+++ b/solution.py
@@ -169,14 +169,14 @@
 
 
 PADDED = (NX + 2, NY + 2, NZ, R)
-field_scratch = [
-    pltpu.VMEM(PADDED, BF),
+difference_arrays = [
     pltpu.VMEM((NX + 1, ROWS, R), BF),
     pltpu.VMEM((NX, ROWS + NZ, R), BF),
     pltpu.VMEM((NX, ROWS, R), BF),
     pltpu.VMEM((NX, ROWS, R), BF),
-    pltpu.SemaphoreType.DMA((NX + 4,)),
 ]
+load_sems = pltpu.SemaphoreType.DMA((NX + 4,))
+field_scratch = [pltpu.VMEM(PADDED, BF)] + difference_arrays + [load_sems]
 
 
 def start_loads(padded, sem, centre, xlo, xhi, ylo, yhi):
@@ -276,7 +276,7 @@
 def inner_kernel(
     packed_ref, mask_ref, cot_ref, xlo_hbm, xhi_hbm, ylo_hbm, yhi_hbm,
     hi_ref, base_ref, hxlo_hbm, hxhi_hbm, hylo_hbm, hyhi_hbm, back_ref, flow_ref,
-    padded, dx, dy, dzp, dzm, sem, gates, out_sem,
+    dx, dy, dzp, dzm, padded, sem, gates, out_sem,
 ):
     copies = start_loads(padded, sem, cot_ref, xlo_hbm, xhi_hbm, ylo_hbm.at[1], yhi_hbm.at[1])
     fill_gates(gates, mask_ref)
@@ -330,11 +330,15 @@
         out_shape=(
             pltpu.VMEM(GRID, BF), pltpu.VMEM(GRID, F32),
             x_face, x_face, y_face, y_face, pltpu.VMEM((1536, 256), BF), pltpu.VMEM((1536, 256), BF),
-        ),
+        ) + tuple(difference_arrays),
         in_specs=[whole, whole, whole] + [raw] * 4,
-        out_specs=(whole, whole) + (hbm,) * 4 + (whole, whole),
-        scratch_shapes=field_scratch
-        + [pltpu.VMEM((CELLS, NZ, 128), F32), pltpu.SemaphoreType.DMA((3, NX))],
+        out_specs=(whole, whole) + (hbm,) * 4 + (whole,) * 6,
+        scratch_shapes=[
+            pltpu.VMEM(PADDED, BF),
+            load_sems,
+            pltpu.VMEM((CELLS, NZ, 128), F32),
+            pltpu.SemaphoreType.DMA((3, NX)),
+        ],
         compiler_params=params(20),
         cost_estimate=cost(2 * 4096 * 256 * 1536, 14 << 20),
         name="inner",
@@ -342,16 +346,13 @@
 
 
 def middle_kernel(
-    flow_ref, mask_ref, state_hbm, sxlo, sxhi, cot_hbm, hxlo, hxhi, ylo, yhi,
-    grads_ref, state_pad, sdx, sdy, sdzp, sdzm, sem_s, held_pad, hdx, hdy, hdzp, hdzm, sem_h,
-    gates,
+    flow_ref, mask_ref, state_ref, sxlo, sxhi, ylo, yhi, hdx, hdy, hdzp, hdzm,
+    grads_ref, state_pad, sdx, sdy, sdzp, sdzm, sem_s, gates,
 ):
-    held_copies = start_loads(held_pad, sem_h, cot_hbm, hxlo, hxhi, ylo.at[1], yhi.at[1])
-    state_copies = start_loads(state_pad, sem_s, state_hbm, sxlo, sxhi, ylo.at[0], yhi.at[0])
+    state_copies = start_loads(state_pad, sem_s, state_ref, sxlo, sxhi, ylo.at[0], yhi.at[0])
     fill_gates(gates, mask_ref)
     grads_ref[...] = jnp.zeros_like(grads_ref)
     states, helds = (sdx, sdy, sdzp, sdzm), (hdx, hdy, hdzp, hdzm)
-    build(held_copies, held_pad, *helds, gates=gates)
     build(state_copies, state_pad, *states)
 
     def one_plane(p, carry):
@@ -375,18 +376,17 @@
     lax.fori_loop(0, NX, products, 0)
 
 
-def middle_step(flow_mats, mask, state, state_x, cotangent, held_x, y_halos):
+def middle_step(flow_mats, mask, state, state_x, y_halos, held_differences):
     return pl.pallas_call(
         middle_kernel,
         out_shape=pltpu.VMEM((256, 1536), F32),
-        in_specs=[whole, whole, whole, raw, raw, whole] + [raw] * 4,
+        in_specs=[whole] * 3 + [raw] * 4 + [whole] * 4,
         out_specs=whole,
-        scratch_shapes=field_scratch * 2
-        + [pltpu.VMEM((CELLS, NZ, 128), F32)],
-        compiler_params=params(34),
-        cost_estimate=cost(4 * 4096 * 256 * 1536, 8 << 20),
+        scratch_shapes=field_scratch + [pltpu.VMEM((CELLS, NZ, 128), F32)],
+        compiler_params=params(22),
+        cost_estimate=cost(4 * 4096 * 256 * 1536, 4 << 20),
         name="middle",
-    )(flow_mats, mask, state, *state_x, cotangent, *held_x, *y_halos)
+    )(flow_mats, mask, state, *state_x, *y_halos, *held_differences)
 
 
 def last_kernel(
@@ -476,33 +476,44 @@
     )(factors, speeds, signs)
 
 
-def final_kernel(packed_ref, weighted_ref, out_ref, mats):
-    @pl.when(pl.program_id(0) == 0)
-    def _():
-        for k in range(6):
-            a, b, c, d = load_packed(packed_ref, k)
-            at = k * 256
-            mats[at : at + 128, :128] = a.astype(BF)
-            mats[at : at + 128, 128:] = b.astype(BF)
-            mats[at + 128 : at + 256, :128] = c.astype(BF)
-            mats[at + 128 : at + 256, 128:] = d.astype(BF)
-
-    out_ref[...] = jnp.dot(weighted_ref[...], mats[...], preferred_element_type=F32)
-
-
-def constant(shape):
-    return pl.BlockSpec(shape, lambda i: (0,) * len(shape), pipeline_mode=pl.Buffered(1))
+def final_kernel(packed_ref, weighted_hbm, out_hbm, mats, weighted, out, sem, out_sem):
+    chunks = weighted.shape[0] // CHUNK
+    loads, stores = [], []
+    for i in range(chunks):
+        at = pl.ds(i * CHUNK, CHUNK)
+        loads.append(pltpu.make_async_copy(weighted_hbm.at[at], weighted.at[at], sem.at[i]))
+        stores.append(pltpu.make_async_copy(out.at[at], out_hbm.at[at], out_sem.at[i]))
+        loads[-1].start()
+    for k in range(6):
+        a, b, c, d = load_packed(packed_ref, k)
+        at = k * 256
+        mats[at : at + 128, :128] = a.astype(BF)
+        mats[at : at + 128, 128:] = b.astype(BF)
+        mats[at + 128 : at + 256, :128] = c.astype(BF)
+        mats[at + 128 : at + 256, 128:] = d.astype(BF)
+    for i in range(chunks):
+        rows = slice(i * CHUNK, (i + 1) * CHUNK)
+        loads[i].wait()
+        out[rows, :] = jnp.dot(weighted[rows, :], mats[...], preferred_element_type=F32)
+        stores[i].start()
+    for store in stores:
+        store.wait()
 
 
 def final_step(packed, weighted):
     rows = weighted.shape[0]
     return pl.pallas_call(
         final_kernel,
-        grid=(rows // CHUNK,),
         out_shape=jax.ShapeDtypeStruct((rows, R), F32),
-        in_specs=[constant((2048, 128)), pl.BlockSpec((CHUNK, 1536), lambda i: (i, 0))],
-        out_specs=pl.BlockSpec((CHUNK, R), lambda i: (i, 0)),
-        scratch_shapes=[pltpu.VMEM((1536, 256), BF)],
+        in_specs=[whole, hbm],
+        out_specs=hbm,
+        scratch_shapes=[
+            pltpu.VMEM((1536, 256), BF),
+            pltpu.VMEM((rows, 1536), BF),
+            pltpu.VMEM((rows, R), F32),
+            pltpu.SemaphoreType.DMA((rows // CHUNK,)),
+            pltpu.SemaphoreType.DMA((rows // CHUNK,)),
+        ],
         compiler_params=params(56),
         cost_estimate=cost(2 * 2048 * 256 * 1536, 8 << 20),
         name="final",
@@ -527,17 +538,18 @@
     hxlo, hxhi, ylo, yhi, sxlo, sxhi = edges(state, cotangent, mask)
     speeds, hxlo, hxhi = lax.optimization_barrier((speeds, hxlo, hxhi))
     held_x = shift("gx", hxlo, hxhi)
-    copies = scatter_sum(gram(factors, speeds, signs))
+    packed = gram(factors, speeds, signs)
+    copies = scatter_sum(packed)
     y_halos = shift(Y_AXES, ylo, yhi)
     copies, sxlo, sxhi = lax.optimization_barrier((copies, sxlo, sxhi))
     state_x = shift("gx", sxlo, sxhi)
     packed = gather(copies)
-    hi, base, hxlo, hxhi, hylo, hyhi, back_mats, flow_mats = inner_step(
+    hi, base, hxlo, hxhi, hylo, hyhi, back_mats, flow_mats, *held_differences = inner_step(
         near(packed), near(cotangent), mask, *held_x, *y_halos
     )
     hi_halos = shift("gx", hxlo, hxhi) + shift(Y_AXES, hylo, hyhi)
     held_grads = middle_step(
-        near(flow_mats), mask, near(state), state_x, near(cotangent), held_x, y_halos
+        near(flow_mats), mask, near(state), state_x, y_halos, [near(d) for d in held_differences]
     )
     partial, grad_state = last_step(
         near(held_grads), near(state), near(hi), near(back_mats), near(base), *hi_halos

time: 147 us -> 147 us (level)
    pallas_call x1, Pallas kernels: 12.4 us -> 10.7 us  [middle_step(): pl.pallas_call(middle_kernel, out_shape=pltpu.VMEM((256, 1536), F32), in_...]
  transfers between devices with their start and end apart: 13 -> 13, of which waited for: 3 -> 3; matrix products, arithmetic and copies ran while one was open for 0% -> 0% of each run, Pallas kernels for 18% -> 17%
where the time goes in v3:
time: 147 us; the launch traced here: 146 us
  Pallas kernels  50.6 us (34%)
  starting transfers between devices  48.3 us (33%)
  blocking collectives  24.8 us (17%)
  waiting for transfers between devices  20.7 us (14%)
    all_to_all x1, blocking collectives, scatter_sum(): mine = lax.all_to_all(pieces, ALL, split_axis=0, concat_axis=0, tiled=True)  24.8 us
    ppermute x10, starting transfers between devices, shift(): return (lax.ppermute(hi, axis, forward), lax.ppermute(lo, axis, backward))  24.8 us
    all_to_all x2, waiting for transfers between devices, gather(): lax.all_to_all(copies, ALL, split_axis=0, concat_axis=0, tiled=True)  17.4 us
    all_to_all x2, starting transfers between devices, gather(): lax.all_to_all(copies, ALL, split_axis=0, concat_axis=0, tiled=True)  12 us
    all_to_all x1, starting transfers between devices, scatter_sum(): mine = lax.all_to_all(pieces, ALL, split_axis=0, concat_axis=0, tiled=True)  11.5 us
    pallas_call x1, Pallas kernels, middle_step(): pl.pallas_call(middle_kernel, out_shape=pltpu.VMEM((256, 1536), F32), in_...  10.7 us
    pallas_call x1, Pallas kernels, last_step(): pl.pallas_call(last_kernel, out_shape=(jax.ShapeDtypeStruct((2048, 128),...  10.4 us
    pallas_call x1, Pallas kernels, inner_step(): pl.pallas_call(inner_kernel, out_shape=(pltpu.VMEM(GRID, BF), pltpu.VMEM(...  7.69 us
  transfers between devices with their start and end apart: 13, of which 3 were waited for; matrix products, arithmetic and copies ran while one was open for 0% of the time, Pallas kernels for 17%

profile of v3, /device:TPU:1, one launch (start us, length us, event | category | flops | bytes accessed | tf_op | source)
XLA Modules:
  0.0 146.3 jit_solution(1200304772499510285)
XLA Ops:
  0.6 0.0 copy-start.3
  0.6 0.0 copy-start.4
  0.7 0.0 copy-start.2
  0.7 4.5 %edges.1 = (bf16[8,128,256]{2,1,0:T(8,128)(2,1)}, bf16[8,128,256]{2,1,0:T(8,128)(2,1)}, bf16[2,4,128,256]{3,2,1,0:T(8,128)(2,1)}, bf16[2,4,128,256]{3,2,1,0:T(8,...) custom-call(bf16[4,8,128,256]{3,2,1,0:T(8,128)(2,1)} %state_ref.3, ...), custom_call_target="tpu_custom_call" | custom-call | flops 1048576 | bytes 6291456 | tf_op jit(solution)/shard_map/edges/pallas_call | solution.py:159
  5.1 0.0 copy-done.3
  5.1 0.0 copy-done.4
  5.1 0.0 copy-done.2
  5.2 2.7 %gram.1 = bf16[2048,128]{1,0:T(8,128)(2,1)} custom-call(bf16[2048,256]{1,0:T(8,128)(2,1)S(1)} %copy-done.2, f32[3,2048]{1,0:T(4,128)S(1)} %copy-done.3, s32[3,2048]{1,0:T(4,128)S(1)} %copy-done.4), custom_call_target="tpu_custom_call" | custom-call | flops 1610612736 | bytes 2097152 | tf_op jit(solution)/shard_map/gram/pallas_call | solution.py:83
  7.9 0.0 copy-start
  7.9 0.0 copy-start.5
  7.9 11.5 %all-to-all-start = ((bf16[128,16,128]{2,1,0:T(8,128)(2,1)}), bf16[128,16,128]{2,1,0:T(8,128)(2,1)S(1)}, u32[]{:S(2)}, u32[]{:S(2)}) async-start(bf16[128,16,128]{2,1,0:T(8,128)(2,1)} %bitcast), calls=%async_computation | async-start | bytes 1048576 | tf_op jit(solution)/shard_map/all_to_all | solution.py:102
  19.4 4.1 %collective-permute-start = (bf16[8,128,256]{2,1,0:T(8,128)(2,1)}, bf16[8,128,256]{2,1,0:T(8,128)(2,1)}, u32[]{:S(2)}, u32[]{:S(2)}) collective-permute-start(bf16[8,128,256]{2,1,0:T(8,128)(2,1)} %get-tuple-element.34), channel_id=1, source_target_pairs={{0,16},{16,32},{32,48},{48,64},{64,80},{80,96},{96,112},{1,17},{17... | collective-permute-start | bytes 1572872 | tf_op jit(solution)/shard_map/ppermute | solution.py:527
  23.4 1.3 collective-permute-start.1
  24.7 3.7 %collective-permute-start.2 = (bf16[2,4,128,256]{3,2,1,0:T(8,128)(2,1)}, bf16[2,4,128,256]{3,2,1,0:T(8,128)(2,1)S(1)}, u32[]{:S(2)}, u32[]{:S(2)}) collective-permute-start(bf16[2,4,128,256]{3,2,1,0:T(8,128)(2,1)} %get-tuple-element.36), channel_id=1, source_target_pairs={{0,1},{1,2},{2,3},{3,4},{4,5},{5,6},{6,7},{7,8},{8,9},{9,10},{10,1... | collective-permute-start | bytes 1572872 | tf_op jit(solution)/shard_map/ppermute | solution.py:527
  28.4 1.9 %collective-permute-start.3 = (bf16[2,4,128,256]{3,2,1,0:T(8,128)(2,1)}, bf16[2,4,128,256]{3,2,1,0:T(8,128)(2,1)}, u32[]{:S(2)}, u32[]{:S(2)}) collective-permute-start(bf16[2,4,128,256]{3,2,1,0:T(8,128)(2,1)} %get-tuple-element.37), channel_id=1, source_target_pairs={{1,0},{2,1},{3,2},{4,3},{5,4},{6,5},{7,6},{8,7},{9,8},{10,9},{11,1... | collective-permute-start | bytes 1572872 | tf_op jit(solution)/shard_map/ppermute | solution.py:527
  30.3 3.2 %all-to-all-done.parts_ref = bf16[128,16,128]{2,1,0:T(8,128)(2,1)S(1)} async-done(((bf16[128,16,128]{2,1,0:T(8,128)(2,1)}), bf16[128,16,128]{2,1,0:T(8,128)(2,1)S(1)}, u32[]{:S(2)}, u32[]{:S(2)}) %all-to-all-start) | async-done | bytes 524320 | tf_op jit(solution)/shard_map/all_to_all | solution.py:102
  33.5 1.0 total.2
  34.5 8.2 %all-to-all-start.1 = ((bf16[128,16,128]{2,1,0:T(8,128)(2,1)}), bf16[128,16,128]{2,1,0:T(8,128)(2,1)S(1)}, u32[]{:S(2)}, u32[]{:S(2)}) async-start(bf16[128,16,128]{2,1,0:T(8,128)(2,1)} %total.2), calls=%async_computation.1 | async-start | bytes 1048576 | tf_op jit(solution)/shard_map/all_to_all | solution.py:115
  42.6 4.1 %collective-permute-start.4 = (bf16[8,128,256]{2,1,0:T(8,128)(2,1)}, bf16[8,128,256]{2,1,0:T(8,128)(2,1)}, u32[]{:S(2)}, u32[]{:S(2)}) collective-permute-start(bf16[8,128,256]{2,1,0:T(8,128)(2,1)} %get-tuple-element.39), channel_id=1, source_target_pairs={{0,16},{16,32},{32,48},{48,64},{64,80},{80,96},{96,112},{1,17},{17... | collective-permute-start | bytes 1572872 | tf_op jit(solution)/shard_map/ppermute | solution.py:527
  46.7 0.0 collective-permute-done.xlo_hbm
  46.7 1.3 collective-permute-start.5
  48.0 0.0 collective-permute-done.1.xhi_hbm
  48.0 0.0 collective-permute-done.2.ylo_hbm.ylo
  48.0 0.0 collective-permute-done.3.yhi_hbm.yhi
  48.0 8.7 %all-to-all-done.1 = bf16[128,16,128]{2,1,0:T(8,128)(2,1)S(1)} async-done(((bf16[128,16,128]{2,1,0:T(8,128)(2,1)}), bf16[128,16,128]{2,1,0:T(8,128)(2,1)S(1)}, u32[]{:S(2)}, u32[]{:S(2)}) %all-to-all-start.1) | async-done | bytes 524320 | tf_op jit(solution)/shard_map/all_to_all | solution.py:115
  56.7 0.0 copy-done
  56.8 0.0 copy-done.5
  56.8 7.7 %inner.1 = (bf16[4,8,128,256]{3,2,1,0:T(8,128)(2,1)S(1)}, f32[4,8,128,256]{3,2,1,0:T(8,128)S(1)}, bf16[8,128,256]{2,1,0:T(8,128)(2,1)S(1)}, bf16[8,128,256]{2,1,...) custom-call(bf16[2048,128]{1,0:T(8,128)(2,1)S(1)} %bitcast.4, ...), custom_call_target="tpu_custom_call" | custom-call | flops 3221225472 | bytes 14680064 | tf_op jit(solution)/shard_map/inner/pallas_call | solution.py:328
  64.5 2.3 %collective-permute-start.6 = (bf16[8,128,256]{2,1,0:T(8,128)(2,1)S(1)}, bf16[8,128,256]{2,1,0:T(8,128)(2,1)S(1)}, u32[]{:S(2)}, u32[]{:S(2)}) collective-permute-start(bf16[8,128,256]{2,1,0:T(8,128)(2,1)S(1)} %get-tuple-element.48), channel_id=1, source_target_pairs={{0,16},{16,32},{32,48},{48,64},{64,80},{80,96},{96,112},{1,17},{17... | collective-permute-start | bytes 1572872 | tf_op jit(solution)/shard_map/ppermute | solution.py:527
  66.7 1.3 collective-permute-start.7
  68.0 2.9 %collective-permute-start.8 = (bf16[4,128,256]{2,1,0:T(8,128)(2,1)S(1)}, bf16[4,128,256]{2,1,0:T(8,128)(2,1)S(1)}, u32[]{:S(2)}, u32[]{:S(2)}) collective-permute-start(bf16[4,128,256]{2,1,0:T(8,128)(2,1)S(1)} %get-tuple-element.50), channel_id=1, source_target_pairs={{0,1},{1,2},{2,3},{3,4},{4,5},{5,6},{6,7},{7,8},{8,9},{9,10},{10,1... | collective-permute-start | bytes 786440 | tf_op jit(solution)/shard_map/ppermute | solution.py:527
  70.9 0.0 collective-permute-done.4.sxlo
  70.9 2.1 %collective-permute-start.9 = (bf16[4,128,256]{2,1,0:T(8,128)(2,1)S(1)}, bf16[4,128,256]{2,1,0:T(8,128)(2,1)S(1)}, u32[]{:S(2)}, u32[]{:S(2)}) collective-permute-start(bf16[4,128,256]{2,1,0:T(8,128)(2,1)S(1)} %get-tuple-element.51), channel_id=1, source_target_pairs={{1,0},{2,1},{3,2},{4,3},{5,4},{6,5},{7,6},{8,7},{9,8},{10,9},{11,1... | collective-permute-start | bytes 786440 | tf_op jit(solution)/shard_map/ppermute | solution.py:527
  73.0 0.0 collective-permute-done.5.sxhi
  73.1 0.0 copy-done.1
  73.1 10.7 %middle.1.held_grads_ref = f32[256,1536]{1,0:T(8,128)S(1)} custom-call(bf16[1536,256]{1,0:T(8,128)(2,1)S(1)} %get-tuple-element.38.flow_ref, s32[4,8,128]{2,1,0:T(8,128)S(1)} %copy-done.5, bf16[4,8,128,256]{3,2,1,0:T(8,128)(2,1)S(1)} %copy-done.1, bf16[8,128,256]{2,1,0:T(8,128)(2,1)} %collective-permute-done.4.sxlo, ...), custom_call_target="tpu_custom_call" | custom-call | flops 6442450944 | bytes 4194304 | tf_op jit(solution)/shard_map/middle/pallas_call | solution.py:380
  83.8 0.0 collective-permute-done.8.ylo_hbm
  83.8 0.0 collective-permute-done.9.yhi_hbm
  83.8 0.0 collective-permute-done.6.xlo_hbm
  83.8 0.0 collective-permute-done.7.xhi_hbm
  83.8 10.4 %last.1 = (bf16[2048,128]{1,0:T(8,128)(2,1)S(1)}, bf16[4,8,128,256]{3,2,1,0:T(8,128)(2,1)}) custom-call(f32[256,1536]{1,0:T(8,128)S(1)} %middle.1.held_grads_ref, bf16[4,8,128,256]{3,2,1,0:T(8,128)(2,1)S(1)} %copy-done.1, bf16[4,8,128,256]{3,2,1,0:T(8,128)(2,1)S(1)} %get-tuple-element.45.hi_ref, bf16[1536,256]{1,0:T(8,128)(2,1)S(1)} %get-tuple-element.46.back_ref, ...), custom_call_target="tpu_custom_call" | custom-call | flops 6442450944 | bytes 5242880 | tf_op jit(solution)/shard_map/last/pallas_call | solution.py:432
  94.2 24.8 %all_to_all.20.parts_ref = bf16[128,16,128]{2,1,0:T(8,128)(2,1)S(1)} all-to-all(bf16[128,16,128]{2,1,0:T(8,128)(2,1)S(1)} %bitcast.5), channel_id=1, replica_groups=mesh['gx'=8,'gy'=8,'gz'=2] {'gx','gy','gz'}, dimensions={0} | all-to-all | bytes 1048576 | tf_op jit(solution)/shard_map/all_to_all | solution.py:102
  119.1 1.0 total.3
  120.1 3.9 %all-to-all-start.3 = ((bf16[128,16,128]{2,1,0:T(8,128)(2,1)}), bf16[128,16,128]{2,1,0:T(8,128)(2,1)S(1)}, u32[]{:S(2)}, u32[]{:S(2)}) async-start(bf16[128,16,128]{2,1,0:T(8,128)(2,1)} %total.3), calls=%async_computation.3 | async-start | bytes 1048576 | tf_op jit(solution)/shard_map/all_to_all | solution.py:115
  123.9 5.5 %weigh.1.weighted_hbm = bf16[2048,1536]{1,0:T(8,128)(2,1)} custom-call(bf16[2048,256]{1,0:T(8,128)(2,1)} %factors_ref.3, f32[3,2048]{1,0:T(4,128)} %speeds_ref.1, s32[3,2048]{1,0:T(4,128)} %signs_ref.3), custom_call_target="tpu_custom_call" | custom-call | flops 3145728 | bytes 8388608 | tf_op jit(solution)/shard_map/weigh/pallas_call | solution.py:463
  129.5 8.7 %all-to-all-done.3 = bf16[128,16,128]{2,1,0:T(8,128)(2,1)S(1)} async-done(((bf16[128,16,128]{2,1,0:T(8,128)(2,1)}), bf16[128,16,128]{2,1,0:T(8,128)(2,1)S(1)}, u32[]{:S(2)}, u32[]{:S(2)}) %all-to-all-start.3) | async-done | bytes 524320 | tf_op jit(solution)/shard_map/all_to_all | solution.py:115
  138.2 0.8 copy-done.6
  139.0 7.2 %final.1 = f32[2048,256]{1,0:T(8,128)} custom-call(bf16[2048,128]{1,0:T(8,128)(2,1)} %bitcast.6, bf16[2048,1536]{1,0:T(8,128)(2,1)} %weigh.1.weighted_hbm), custom_call_target="tpu_custom_call" | custom-call | flops 1610612736 | bytes 8388608 | tf_op jit(solution)/shard_map/final/pallas_call | solution.py:505
  (2 shorter events, 0.0 us)
Async XLA Ops:
  0.6 4.5 %copy-start.3 = (f32[3,2048]{1,0:T(4,128)S(1)}, f32[3,2048]{1,0:T(4,128)}, u32[]{:S(2)}) copy-start(f32[3,2048]{1,0:T(4,128)} %speeds_ref.1) | copy-start | bytes 73732
  0.6 4.5 %copy-start.4 = (s32[3,2048]{1,0:T(4,128)S(1)}, s32[3,2048]{1,0:T(4,128)}, u32[]{:S(2)}) copy-start(s32[3,2048]{1,0:T(4,128)} %signs_ref.3) | copy-start | bytes 73732
  0.7 4.5 %copy-start.2 = (bf16[2048,256]{1,0:T(8,128)(2,1)S(1)}, bf16[2048,256]{1,0:T(8,128)(2,1)}, u32[]{:S(2)}) copy-start(bf16[2048,256]{1,0:T(8,128)(2,1)} %factors_ref.3) | copy-start | bytes 3145732
  7.9 48.9 %copy-start = (bf16[4,8,128,256]{3,2,1,0:T(8,128)(2,1)S(1)}, bf16[4,8,128,256]{3,2,1,0:T(8,128)(2,1)}, u32[]{:S(2)}) copy-start(bf16[4,8,128,256]{3,2,1,0:T(8,128)(2,1)} %cot_ref.1) | copy-start | bytes 6291460
  7.9 48.9 %copy-start.5 = (s32[4,8,128]{2,1,0:T(8,128)S(1)}, s32[4,8,128]{2,1,0:T(8,128)}, u32[]{:S(2)}) copy-start(s32[4,8,128]{2,1,0:T(8,128)} %mask_ref.5) | copy-start | bytes 49156
  7.9 25.6 %all-to-all-start = ((bf16[128,16,128]{2,1,0:T(8,128)(2,1)}), bf16[128,16,128]{2,1,0:T(8,128)(2,1)S(1)}, u32[]{:S(2)}, u32[]{:S(2)}) async-start(bf16[128,16,128]{2,1,0:T(8,128)(2,1)} %bitcast), calls=%async_computation | async-start | bytes 1048576 | tf_op jit(solution)/shard_map/all_to_all | solution.py:102
  19.4 27.3 %collective-permute-start = (bf16[8,128,256]{2,1,0:T(8,128)(2,1)}, bf16[8,128,256]{2,1,0:T(8,128)(2,1)}, u32[]{:S(2)}, u32[]{:S(2)}) collective-permute-start(bf16[8,128,256]{2,1,0:T(8,128)(2,1)} %get-tuple-element.34), channel_id=1, source_target_pairs={{0,16},{16,32},{32,48},{48,64},{64,80},{80,96},{96,112},{1,17},{17... | collective-permute-start | bytes 1572872 | tf_op jit(solution)/shard_map/ppermute | solution.py:527
  23.4 24.6 %collective-permute-start.1 = (bf16[8,128,256]{2,1,0:T(8,128)(2,1)}, bf16[8,128,256]{2,1,0:T(8,128)(2,1)}, u32[]{:S(2)}, u32[]{:S(2)}) collective-permute-start(bf16[8,128,256]{2,1,0:T(8,128)(2,1)} %get-tuple-element.35), channel_id=1, source_target_pairs={{16,0},{32,16},{48,32},{64,48},{80,64},{96,80},{112,96},{17,1},{33... | collective-permute-start | bytes 1572872 | tf_op jit(solution)/shard_map/ppermute | solution.py:527
  24.7 23.3 %collective-permute-start.2 = (bf16[2,4,128,256]{3,2,1,0:T(8,128)(2,1)}, bf16[2,4,128,256]{3,2,1,0:T(8,128)(2,1)S(1)}, u32[]{:S(2)}, u32[]{:S(2)}) collective-permute-start(bf16[2,4,128,256]{3,2,1,0:T(8,128)(2,1)} %get-tuple-element.36), channel_id=1, source_target_pairs={{0,1},{1,2},{2,3},{3,4},{4,5},{5,6},{6,7},{7,8},{8,9},{9,10},{10,1... | collective-permute-start | bytes 1572872 | tf_op jit(solution)/shard_map/ppermute | solution.py:527
  28.4 19.6 %collective-permute-start.3 = (bf16[2,4,128,256]{3,2,1,0:T(8,128)(2,1)}, bf16[2,4,128,256]{3,2,1,0:T(8,128)(2,1)}, u32[]{:S(2)}, u32[]{:S(2)}) collective-permute-start(bf16[2,4,128,256]{3,2,1,0:T(8,128)(2,1)} %get-tuple-element.37), channel_id=1, source_target_pairs={{1,0},{2,1},{3,2},{4,3},{5,4},{6,5},{7,6},{8,7},{9,8},{10,9},{11,1... | collective-permute-start | bytes 1572872 | tf_op jit(solution)/shard_map/ppermute | solution.py:527
  34.5 22.3 %all-to-all-start.1 = ((bf16[128,16,128]{2,1,0:T(8,128)(2,1)}), bf16[128,16,128]{2,1,0:T(8,128)(2,1)S(1)}, u32[]{:S(2)}, u32[]{:S(2)}) async-start(bf16[128,16,128]{2,1,0:T(8,128)(2,1)} %total.2), calls=%async_computation.1 | async-start | bytes 1048576 | tf_op jit(solution)/shard_map/all_to_all | solution.py:115
  42.6 28.3 %collective-permute-start.4 = (bf16[8,128,256]{2,1,0:T(8,128)(2,1)}, bf16[8,128,256]{2,1,0:T(8,128)(2,1)}, u32[]{:S(2)}, u32[]{:S(2)}) collective-permute-start(bf16[8,128,256]{2,1,0:T(8,128)(2,1)} %get-tuple-element.39), channel_id=1, source_target_pairs={{0,16},{16,32},{32,48},{48,64},{64,80},{80,96},{96,112},{1,17},{17... | collective-permute-start | bytes 1572872 | tf_op jit(solution)/shard_map/ppermute | solution.py:527
  46.7 26.4 %collective-permute-start.5 = (bf16[8,128,256]{2,1,0:T(8,128)(2,1)}, bf16[8,128,256]{2,1,0:T(8,128)(2,1)}, u32[]{:S(2)}, u32[]{:S(2)}) collective-permute-start(bf16[8,128,256]{2,1,0:T(8,128)(2,1)} %get-tuple-element.40), channel_id=1, source_target_pairs={{16,0},{32,16},{48,32},{64,48},{80,64},{96,80},{112,96},{17,1},{33... | collective-permute-start | bytes 1572872 | tf_op jit(solution)/shard_map/ppermute | solution.py:527
  56.8 16.3 %copy-start.1 = (bf16[4,8,128,256]{3,2,1,0:T(8,128)(2,1)S(1)}, bf16[4,8,128,256]{3,2,1,0:T(8,128)(2,1)}, u32[]{:S(2)}) copy-start(bf16[4,8,128,256]{3,2,1,0:T(8,128)(2,1)} %state_ref.3) | copy-start | bytes 6291460
  64.5 19.4 %collective-permute-start.6 = (bf16[8,128,256]{2,1,0:T(8,128)(2,1)S(1)}, bf16[8,128,256]{2,1,0:T(8,128)(2,1)S(1)}, u32[]{:S(2)}, u32[]{:S(2)}) collective-permute-start(bf16[8,128,256]{2,1,0:T(8,128)(2,1)S(1)} %get-tuple-element.48), channel_id=1, source_target_pairs={{0,16},{16,32},{32,48},{48,64},{64,80},{80,96},{96,112},{1,17},{17... | collective-permute-start | bytes 1572872 | tf_op jit(solution)/shard_map/ppermute | solution.py:527
  66.7 17.1 %collective-permute-start.7 = (bf16[8,128,256]{2,1,0:T(8,128)(2,1)S(1)}, bf16[8,128,256]{2,1,0:T(8,128)(2,1)S(1)}, u32[]{:S(2)}, u32[]{:S(2)}) collective-permute-start(bf16[8,128,256]{2,1,0:T(8,128)(2,1)S(1)} %get-tuple-element.49), channel_id=1, source_target_pairs={{16,0},{32,16},{48,32},{64,48},{80,64},{96,80},{112,96},{17,1},{33... | collective-permute-start | bytes 1572872 | tf_op jit(solution)/shard_map/ppermute | solution.py:527
  68.0 15.8 %collective-permute-start.8 = (bf16[4,128,256]{2,1,0:T(8,128)(2,1)S(1)}, bf16[4,128,256]{2,1,0:T(8,128)(2,1)S(1)}, u32[]{:S(2)}, u32[]{:S(2)}) collective-permute-start(bf16[4,128,256]{2,1,0:T(8,128)(2,1)S(1)} %get-tuple-element.50), channel_id=1, source_target_pairs={{0,1},{1,2},{2,3},{3,4},{4,5},{5,6},{6,7},{7,8},{8,9},{9,10},{10,1... | collective-permute-start | bytes 786440 | tf_op jit(solution)/shard_map/ppermute | solution.py:527
  70.9 12.9 %collective-permute-start.9 = (bf16[4,128,256]{2,1,0:T(8,128)(2,1)S(1)}, bf16[4,128,256]{2,1,0:T(8,128)(2,1)S(1)}, u32[]{:S(2)}, u32[]{:S(2)}) collective-permute-start(bf16[4,128,256]{2,1,0:T(8,128)(2,1)S(1)} %get-tuple-element.51), channel_id=1, source_target_pairs={{1,0},{2,1},{3,2},{4,3},{5,4},{6,5},{7,6},{8,7},{9,8},{10,9},{11,1... | collective-permute-start | bytes 786440 | tf_op jit(solution)/shard_map/ppermute | solution.py:527
  120.1 18.1 %all-to-all-start.3 = ((bf16[128,16,128]{2,1,0:T(8,128)(2,1)}), bf16[128,16,128]{2,1,0:T(8,128)(2,1)S(1)}, u32[]{:S(2)}, u32[]{:S(2)}) async-start(bf16[128,16,128]{2,1,0:T(8,128)(2,1)} %total.3), calls=%async_computation.3 | async-start | bytes 1048576 | tf_op jit(solution)/shard_map/all_to_all | solution.py:115
  138.2 0.8 copy-start.6

commit v4 on v2

--- a/solution.py
+++ b/solution.py
@@ -169,14 +169,14 @@
 
 
 PADDED = (NX + 2, NY + 2, NZ, R)
-field_scratch = [
-    pltpu.VMEM(PADDED, BF),
+difference_arrays = [
     pltpu.VMEM((NX + 1, ROWS, R), BF),
     pltpu.VMEM((NX, ROWS + NZ, R), BF),
     pltpu.VMEM((NX, ROWS, R), BF),
     pltpu.VMEM((NX, ROWS, R), BF),
-    pltpu.SemaphoreType.DMA((NX + 4,)),
 ]
+load_sems = pltpu.SemaphoreType.DMA((NX + 4,))
+field_scratch = [pltpu.VMEM(PADDED, BF)] + difference_arrays + [load_sems]
 
 
 def start_loads(padded, sem, centre, xlo, xhi, ylo, yhi):
@@ -276,7 +276,7 @@
 def inner_kernel(
     packed_ref, mask_ref, cot_ref, xlo_hbm, xhi_hbm, ylo_hbm, yhi_hbm,
     hi_ref, base_ref, hxlo_hbm, hxhi_hbm, hylo_hbm, hyhi_hbm, back_ref, flow_ref,
-    padded, dx, dy, dzp, dzm, sem, gates, out_sem,
+    dx, dy, dzp, dzm, padded, sem, gates, out_sem,
 ):
     copies = start_loads(padded, sem, cot_ref, xlo_hbm, xhi_hbm, ylo_hbm.at[1], yhi_hbm.at[1])
     fill_gates(gates, mask_ref)
@@ -330,11 +330,15 @@
         out_shape=(
             pltpu.VMEM(GRID, BF), pltpu.VMEM(GRID, F32),
             x_face, x_face, y_face, y_face, pltpu.VMEM((1536, 256), BF), pltpu.VMEM((1536, 256), BF),
-        ),
+        ) + tuple(difference_arrays),
         in_specs=[whole, whole, whole] + [raw] * 4,
-        out_specs=(whole, whole) + (hbm,) * 4 + (whole, whole),
-        scratch_shapes=field_scratch
-        + [pltpu.VMEM((CELLS, NZ, 128), F32), pltpu.SemaphoreType.DMA((3, NX))],
+        out_specs=(whole, whole) + (hbm,) * 4 + (whole,) * 6,
+        scratch_shapes=[
+            pltpu.VMEM(PADDED, BF),
+            load_sems,
+            pltpu.VMEM((CELLS, NZ, 128), F32),
+            pltpu.SemaphoreType.DMA((3, NX)),
+        ],
         compiler_params=params(20),
         cost_estimate=cost(2 * 4096 * 256 * 1536, 14 << 20),
         name="inner",
@@ -342,16 +346,13 @@
 
 
 def middle_kernel(
-    flow_ref, mask_ref, state_hbm, sxlo, sxhi, cot_hbm, hxlo, hxhi, ylo, yhi,
-    grads_ref, state_pad, sdx, sdy, sdzp, sdzm, sem_s, held_pad, hdx, hdy, hdzp, hdzm, sem_h,
-    gates,
+    flow_ref, mask_ref, state_ref, sxlo, sxhi, ylo, yhi, hdx, hdy, hdzp, hdzm,
+    grads_ref, state_pad, sdx, sdy, sdzp, sdzm, sem_s, gates,
 ):
-    held_copies = start_loads(held_pad, sem_h, cot_hbm, hxlo, hxhi, ylo.at[1], yhi.at[1])
-    state_copies = start_loads(state_pad, sem_s, state_hbm, sxlo, sxhi, ylo.at[0], yhi.at[0])
+    state_copies = start_loads(state_pad, sem_s, state_ref, sxlo, sxhi, ylo.at[0], yhi.at[0])
     fill_gates(gates, mask_ref)
     grads_ref[...] = jnp.zeros_like(grads_ref)
     states, helds = (sdx, sdy, sdzp, sdzm), (hdx, hdy, hdzp, hdzm)
-    build(held_copies, held_pad, *helds, gates=gates)
     build(state_copies, state_pad, *states)
 
     def one_plane(p, carry):
@@ -375,18 +376,17 @@
     lax.fori_loop(0, NX, products, 0)
 
 
-def middle_step(flow_mats, mask, state, state_x, cotangent, held_x, y_halos):
+def middle_step(flow_mats, mask, state, state_x, y_halos, held_differences):
     return pl.pallas_call(
         middle_kernel,
         out_shape=pltpu.VMEM((256, 1536), F32),
-        in_specs=[whole, whole, whole, raw, raw, whole] + [raw] * 4,
+        in_specs=[whole] * 3 + [raw] * 4 + [whole] * 4,
         out_specs=whole,
-        scratch_shapes=field_scratch * 2
-        + [pltpu.VMEM((CELLS, NZ, 128), F32)],
-        compiler_params=params(34),
-        cost_estimate=cost(4 * 4096 * 256 * 1536, 8 << 20),
+        scratch_shapes=field_scratch + [pltpu.VMEM((CELLS, NZ, 128), F32)],
+        compiler_params=params(22),
+        cost_estimate=cost(4 * 4096 * 256 * 1536, 4 << 20),
         name="middle",
-    )(flow_mats, mask, state, *state_x, cotangent, *held_x, *y_halos)
+    )(flow_mats, mask, state, *state_x, *y_halos, *held_differences)
 
 
 def last_kernel(
@@ -513,7 +513,9 @@
     count = lax.axis_size(axis)
     forward = [(i, i + 1) for i in range(count - 1)]
     backward = [(i + 1, i) for i in range(count - 1)]
-    return lax.ppermute(hi, axis, forward), lax.ppermute(lo, axis, backward)
+    from_below = lax.ppermute(hi, axis, forward)
+    from_above = lax.ppermute(lo, axis, backward)
+    return from_below, from_above
 
 
 Y_AXES = ("gy", "gz")
@@ -532,12 +534,12 @@
     copies, sxlo, sxhi = lax.optimization_barrier((copies, sxlo, sxhi))
     state_x = shift("gx", sxlo, sxhi)
     packed = gather(copies)
-    hi, base, hxlo, hxhi, hylo, hyhi, back_mats, flow_mats = inner_step(
+    hi, base, hxlo, hxhi, hylo, hyhi, back_mats, flow_mats, *held_differences = inner_step(
         near(packed), near(cotangent), mask, *held_x, *y_halos
     )
     hi_halos = shift("gx", hxlo, hxhi) + shift(Y_AXES, hylo, hyhi)
     held_grads = middle_step(
-        near(flow_mats), mask, near(state), state_x, near(cotangent), held_x, y_halos
+        near(flow_mats), mask, near(state), state_x, y_halos, [near(d) for d in held_differences]
     )
     partial, grad_state = last_step(
         near(held_grads), near(state), near(hi), near(back_mats), near(base), *hi_halos
@@ -558,6 +560,7 @@
         P(None, ALL),
         P("gx", ("gy", "gz"), None),
     )
+
     return jax.shard_map(
         on_device,
         mesh=mesh,

time: 147 us -> 146 us (level)
  Pallas kernels: 51.1 us -> 49.5 us
    pallas_call x1, Pallas kernels: 12.4 us -> 10.7 us  [middle_step(): pl.pallas_call(middle_kernel, out_shape=pltpu.VMEM((256, 1536), F32), in_...]
  transfers between devices with their start and end apart: 13 -> 13, of which waited for: 3 -> 3; matrix products, arithmetic and copies ran while one was open for 0% -> 0% of each run, Pallas kernels for 18% -> 17%
where the time goes in v4:
time: 146 us; the launch traced here: 145 us
  Pallas kernels  49.5 us (34%)
  starting transfers between devices  48.3 us (33%)
  blocking collectives  24.8 us (17%)
  waiting for transfers between devices  20.7 us (14%)
    all_to_all x1, blocking collectives, scatter_sum(): mine = lax.all_to_all(pieces, ALL, split_axis=0, concat_axis=0, tiled=True)  24.8 us
    all_to_all x2, waiting for transfers between devices, gather(): lax.all_to_all(copies, ALL, split_axis=0, concat_axis=0, tiled=True)  17.4 us
    ppermute x5, starting transfers between devices, shift(): from_below = lax.ppermute(hi, axis, forward)  16.9 us
    all_to_all x2, starting transfers between devices, gather(): lax.all_to_all(copies, ALL, split_axis=0, concat_axis=0, tiled=True)  12 us
    all_to_all x1, starting transfers between devices, scatter_sum(): mine = lax.all_to_all(pieces, ALL, split_axis=0, concat_axis=0, tiled=True)  11.5 us
    pallas_call x1, Pallas kernels, middle_step(): pl.pallas_call(middle_kernel, out_shape=pltpu.VMEM((256, 1536), F32), in_...  10.7 us
    pallas_call x1, Pallas kernels, last_step(): pl.pallas_call(last_kernel, out_shape=(jax.ShapeDtypeStruct((2048, 128),...  10.4 us
    ppermute x5, starting transfers between devices, shift(): from_above = lax.ppermute(lo, axis, backward)  7.88 us
  transfers between devices with their start and end apart: 13, of which 3 were waited for; matrix products, arithmetic and copies ran while one was open for 0% of the time, Pallas kernels for 17%

profile of v4, /device:TPU:1, one launch (start us, length us, event | category | flops | bytes accessed | tf_op | source)
XLA Modules:
  0.0 145.0 jit_solution(1743054954611777696)
XLA Ops:
  0.6 0.0 copy-start.3
  0.6 0.0 copy-start.4
  0.7 0.0 copy-start.2
  0.7 4.5 %edges.1 = (bf16[8,128,256]{2,1,0:T(8,128)(2,1)}, bf16[8,128,256]{2,1,0:T(8,128)(2,1)}, bf16[2,4,128,256]{3,2,1,0:T(8,128)(2,1)}, bf16[2,4,128,256]{3,2,1,0:T(8,...) custom-call(bf16[4,8,128,256]{3,2,1,0:T(8,128)(2,1)} %state_ref.3, ...), custom_call_target="tpu_custom_call" | custom-call | flops 1048576 | bytes 6291456 | tf_op jit(solution)/shard_map/edges/pallas_call | solution.py:159
  5.1 0.0 copy-done.3
  5.1 0.0 copy-done.4
  5.1 0.0 copy-done.2
  5.2 2.7 %gram.1 = bf16[2048,128]{1,0:T(8,128)(2,1)} custom-call(bf16[2048,256]{1,0:T(8,128)(2,1)S(1)} %copy-done.2, f32[3,2048]{1,0:T(4,128)S(1)} %copy-done.3, s32[3,2048]{1,0:T(4,128)S(1)} %copy-done.4), custom_call_target="tpu_custom_call" | custom-call | flops 1610612736 | bytes 2097152 | tf_op jit(solution)/shard_map/gram/pallas_call | solution.py:83
  7.9 0.0 copy-start
  7.9 0.0 copy-start.5
  7.9 11.5 %all-to-all-start = ((bf16[128,16,128]{2,1,0:T(8,128)(2,1)}), bf16[128,16,128]{2,1,0:T(8,128)(2,1)S(1)}, u32[]{:S(2)}, u32[]{:S(2)}) async-start(bf16[128,16,128]{2,1,0:T(8,128)(2,1)} %bitcast), calls=%async_computation | async-start | bytes 1048576 | tf_op jit(solution)/shard_map/all_to_all | solution.py:102
  19.4 4.1 %collective-permute-start = (bf16[8,128,256]{2,1,0:T(8,128)(2,1)}, bf16[8,128,256]{2,1,0:T(8,128)(2,1)}, u32[]{:S(2)}, u32[]{:S(2)}) collective-permute-start(bf16[8,128,256]{2,1,0:T(8,128)(2,1)} %get-tuple-element.34), channel_id=1, source_target_pairs={{0,16},{16,32},{32,48},{48,64},{64,80},{80,96},{96,112},{1,17},{17... | collective-permute-start | bytes 1572872 | tf_op jit(solution)/shard_map/ppermute | solution.py:516
  23.4 1.3 collective-permute-start.1
  24.7 3.7 %collective-permute-start.2 = (bf16[2,4,128,256]{3,2,1,0:T(8,128)(2,1)}, bf16[2,4,128,256]{3,2,1,0:T(8,128)(2,1)S(1)}, u32[]{:S(2)}, u32[]{:S(2)}) collective-permute-start(bf16[2,4,128,256]{3,2,1,0:T(8,128)(2,1)} %get-tuple-element.36), channel_id=1, source_target_pairs={{0,1},{1,2},{2,3},{3,4},{4,5},{5,6},{6,7},{7,8},{8,9},{9,10},{10,1... | collective-permute-start | bytes 1572872 | tf_op jit(solution)/shard_map/ppermute | solution.py:516
  28.4 1.9 %collective-permute-start.3 = (bf16[2,4,128,256]{3,2,1,0:T(8,128)(2,1)}, bf16[2,4,128,256]{3,2,1,0:T(8,128)(2,1)}, u32[]{:S(2)}, u32[]{:S(2)}) collective-permute-start(bf16[2,4,128,256]{3,2,1,0:T(8,128)(2,1)} %get-tuple-element.37), channel_id=1, source_target_pairs={{1,0},{2,1},{3,2},{4,3},{5,4},{6,5},{7,6},{8,7},{9,8},{10,9},{11,1... | collective-permute-start | bytes 1572872 | tf_op jit(solution)/shard_map/ppermute | solution.py:517
  30.3 3.2 %all-to-all-done.parts_ref = bf16[128,16,128]{2,1,0:T(8,128)(2,1)S(1)} async-done(((bf16[128,16,128]{2,1,0:T(8,128)(2,1)}), bf16[128,16,128]{2,1,0:T(8,128)(2,1)S(1)}, u32[]{:S(2)}, u32[]{:S(2)}) %all-to-all-start) | async-done | bytes 524320 | tf_op jit(solution)/shard_map/all_to_all | solution.py:102
  33.5 1.0 total.2
  34.5 8.2 %all-to-all-start.1 = ((bf16[128,16,128]{2,1,0:T(8,128)(2,1)}), bf16[128,16,128]{2,1,0:T(8,128)(2,1)S(1)}, u32[]{:S(2)}, u32[]{:S(2)}) async-start(bf16[128,16,128]{2,1,0:T(8,128)(2,1)} %total.2), calls=%async_computation.1 | async-start | bytes 1048576 | tf_op jit(solution)/shard_map/all_to_all | solution.py:115
  42.6 4.1 %collective-permute-start.4 = (bf16[8,128,256]{2,1,0:T(8,128)(2,1)}, bf16[8,128,256]{2,1,0:T(8,128)(2,1)}, u32[]{:S(2)}, u32[]{:S(2)}) collective-permute-start(bf16[8,128,256]{2,1,0:T(8,128)(2,1)} %get-tuple-element.39), channel_id=1, source_target_pairs={{0,16},{16,32},{32,48},{48,64},{64,80},{80,96},{96,112},{1,17},{17... | collective-permute-start | bytes 1572872 | tf_op jit(solution)/shard_map/ppermute | solution.py:516
  46.7 0.0 collective-permute-done.xlo_hbm
  46.7 1.3 collective-permute-start.5
  48.0 0.0 collective-permute-done.1.xhi_hbm
  48.0 0.0 collective-permute-done.2.ylo_hbm.ylo
  48.0 0.0 collective-permute-done.3.yhi_hbm.yhi
  48.0 8.7 %all-to-all-done.1 = bf16[128,16,128]{2,1,0:T(8,128)(2,1)S(1)} async-done(((bf16[128,16,128]{2,1,0:T(8,128)(2,1)}), bf16[128,16,128]{2,1,0:T(8,128)(2,1)S(1)}, u32[]{:S(2)}, u32[]{:S(2)}) %all-to-all-start.1) | async-done | bytes 524320 | tf_op jit(solution)/shard_map/all_to_all | solution.py:115
  56.7 0.0 copy-done
  56.8 0.0 copy-done.5
  56.8 7.7 %inner.1 = (bf16[4,8,128,256]{3,2,1,0:T(8,128)(2,1)S(1)}, f32[4,8,128,256]{3,2,1,0:T(8,128)S(1)}, bf16[8,128,256]{2,1,0:T(8,128)(2,1)S(1)}, bf16[8,128,256]{2,1,...) custom-call(bf16[2048,128]{1,0:T(8,128)(2,1)S(1)} %bitcast.4, ...), custom_call_target="tpu_custom_call" | custom-call | flops 3221225472 | bytes 14680064 | tf_op jit(solution)/shard_map/inner/pallas_call | solution.py:328
  64.5 2.3 %collective-permute-start.6 = (bf16[8,128,256]{2,1,0:T(8,128)(2,1)S(1)}, bf16[8,128,256]{2,1,0:T(8,128)(2,1)S(1)}, u32[]{:S(2)}, u32[]{:S(2)}) collective-permute-start(bf16[8,128,256]{2,1,0:T(8,128)(2,1)S(1)} %get-tuple-element.48), channel_id=1, source_target_pairs={{0,16},{16,32},{32,48},{48,64},{64,80},{80,96},{96,112},{1,17},{17... | collective-permute-start | bytes 1572872 | tf_op jit(solution)/shard_map/ppermute | solution.py:516
  66.7 1.3 collective-permute-start.7
  68.0 2.9 %collective-permute-start.8 = (bf16[4,128,256]{2,1,0:T(8,128)(2,1)S(1)}, bf16[4,128,256]{2,1,0:T(8,128)(2,1)S(1)}, u32[]{:S(2)}, u32[]{:S(2)}) collective-permute-start(bf16[4,128,256]{2,1,0:T(8,128)(2,1)S(1)} %get-tuple-element.50), channel_id=1, source_target_pairs={{0,1},{1,2},{2,3},{3,4},{4,5},{5,6},{6,7},{7,8},{8,9},{9,10},{10,1... | collective-permute-start | bytes 786440 | tf_op jit(solution)/shard_map/ppermute | solution.py:516
  70.9 0.0 collective-permute-done.4.sxlo
  70.9 2.1 %collective-permute-start.9 = (bf16[4,128,256]{2,1,0:T(8,128)(2,1)S(1)}, bf16[4,128,256]{2,1,0:T(8,128)(2,1)S(1)}, u32[]{:S(2)}, u32[]{:S(2)}) collective-permute-start(bf16[4,128,256]{2,1,0:T(8,128)(2,1)S(1)} %get-tuple-element.51), channel_id=1, source_target_pairs={{1,0},{2,1},{3,2},{4,3},{5,4},{6,5},{7,6},{8,7},{9,8},{10,9},{11,1... | collective-permute-start | bytes 786440 | tf_op jit(solution)/shard_map/ppermute | solution.py:517
  73.0 0.0 collective-permute-done.5.sxhi
  73.1 0.0 copy-done.1
  73.1 10.7 %middle.1.held_grads_ref = f32[256,1536]{1,0:T(8,128)S(1)} custom-call(bf16[1536,256]{1,0:T(8,128)(2,1)S(1)} %get-tuple-element.38.flow_ref, s32[4,8,128]{2,1,0:T(8,128)S(1)} %copy-done.5, bf16[4,8,128,256]{3,2,1,0:T(8,128)(2,1)S(1)} %copy-done.1, bf16[8,128,256]{2,1,0:T(8,128)(2,1)} %collective-permute-done.4.sxlo, ...), custom_call_target="tpu_custom_call" | custom-call | flops 6442450944 | bytes 4194304 | tf_op jit(solution)/shard_map/middle/pallas_call | solution.py:380
  83.8 0.0 collective-permute-done.8.ylo_hbm
  83.8 0.0 collective-permute-done.9.yhi_hbm
  83.8 0.0 collective-permute-done.6.xlo_hbm
  83.8 0.0 collective-permute-done.7.xhi_hbm
  83.8 10.4 %last.1 = (bf16[2048,128]{1,0:T(8,128)(2,1)S(1)}, bf16[4,8,128,256]{3,2,1,0:T(8,128)(2,1)}) custom-call(f32[256,1536]{1,0:T(8,128)S(1)} %middle.1.held_grads_ref, bf16[4,8,128,256]{3,2,1,0:T(8,128)(2,1)S(1)} %copy-done.1, bf16[4,8,128,256]{3,2,1,0:T(8,128)(2,1)S(1)} %get-tuple-element.45.hi_ref, bf16[1536,256]{1,0:T(8,128)(2,1)S(1)} %get-tuple-element.46.back_ref, ...), custom_call_target="tpu_custom_call" | custom-call | flops 6442450944 | bytes 5242880 | tf_op jit(solution)/shard_map/last/pallas_call | solution.py:432
  94.2 24.8 %all_to_all.20.parts_ref = bf16[128,16,128]{2,1,0:T(8,128)(2,1)S(1)} all-to-all(bf16[128,16,128]{2,1,0:T(8,128)(2,1)S(1)} %bitcast.5), channel_id=1, replica_groups=mesh['gx'=8,'gy'=8,'gz'=2] {'gx','gy','gz'}, dimensions={0} | all-to-all | bytes 1048576 | tf_op jit(solution)/shard_map/all_to_all | solution.py:102
  119.1 1.0 total.3
  120.1 3.9 %all-to-all-start.3 = ((bf16[128,16,128]{2,1,0:T(8,128)(2,1)}), bf16[128,16,128]{2,1,0:T(8,128)(2,1)S(1)}, u32[]{:S(2)}, u32[]{:S(2)}) async-start(bf16[128,16,128]{2,1,0:T(8,128)(2,1)} %total.3), calls=%async_computation.3 | async-start | bytes 1048576 | tf_op jit(solution)/shard_map/all_to_all | solution.py:115
  123.9 5.5 %weigh.1.weighted_ref = bf16[2048,1536]{1,0:T(8,128)(2,1)} custom-call(bf16[2048,256]{1,0:T(8,128)(2,1)} %factors_ref.3, f32[3,2048]{1,0:T(4,128)} %speeds_ref.1, s32[3,2048]{1,0:T(4,128)} %signs_ref.3), custom_call_target="tpu_custom_call" | custom-call | flops 3145728 | bytes 8388608 | tf_op jit(solution)/shard_map/weigh/pallas_call | solution.py:463
  129.5 8.7 %all-to-all-done.3 = bf16[128,16,128]{2,1,0:T(8,128)(2,1)S(1)} async-done(((bf16[128,16,128]{2,1,0:T(8,128)(2,1)}), bf16[128,16,128]{2,1,0:T(8,128)(2,1)S(1)}, u32[]{:S(2)}, u32[]{:S(2)}) %all-to-all-start.3) | async-done | bytes 524320 | tf_op jit(solution)/shard_map/all_to_all | solution.py:115
  138.2 0.8 copy-done.6
  139.0 6.0 %final.1 = f32[2048,256]{1,0:T(8,128)} custom-call(bf16[2048,128]{1,0:T(8,128)(2,1)} %bitcast.6, bf16[2048,1536]{1,0:T(8,128)(2,1)} %weigh.1.weighted_ref), custom_call_target="tpu_custom_call" | custom-call | flops 1610612736 | bytes 8388608 | tf_op jit(solution)/shard_map/final/pallas_call | solution.py:499
  (2 shorter events, 0.0 us)
Async XLA Ops:
  0.6 4.5 %copy-start.3 = (f32[3,2048]{1,0:T(4,128)S(1)}, f32[3,2048]{1,0:T(4,128)}, u32[]{:S(2)}) copy-start(f32[3,2048]{1,0:T(4,128)} %speeds_ref.1) | copy-start | bytes 73732
  0.6 4.5 %copy-start.4 = (s32[3,2048]{1,0:T(4,128)S(1)}, s32[3,2048]{1,0:T(4,128)}, u32[]{:S(2)}) copy-start(s32[3,2048]{1,0:T(4,128)} %signs_ref.3) | copy-start | bytes 73732
  0.7 4.5 %copy-start.2 = (bf16[2048,256]{1,0:T(8,128)(2,1)S(1)}, bf16[2048,256]{1,0:T(8,128)(2,1)}, u32[]{:S(2)}) copy-start(bf16[2048,256]{1,0:T(8,128)(2,1)} %factors_ref.3) | copy-start | bytes 3145732
  7.9 48.9 %copy-start = (bf16[4,8,128,256]{3,2,1,0:T(8,128)(2,1)S(1)}, bf16[4,8,128,256]{3,2,1,0:T(8,128)(2,1)}, u32[]{:S(2)}) copy-start(bf16[4,8,128,256]{3,2,1,0:T(8,128)(2,1)} %cot_ref.1) | copy-start | bytes 6291460
  7.9 48.9 %copy-start.5 = (s32[4,8,128]{2,1,0:T(8,128)S(1)}, s32[4,8,128]{2,1,0:T(8,128)}, u32[]{:S(2)}) copy-start(s32[4,8,128]{2,1,0:T(8,128)} %mask_ref.5) | copy-start | bytes 49156
  7.9 25.6 %all-to-all-start = ((bf16[128,16,128]{2,1,0:T(8,128)(2,1)}), bf16[128,16,128]{2,1,0:T(8,128)(2,1)S(1)}, u32[]{:S(2)}, u32[]{:S(2)}) async-start(bf16[128,16,128]{2,1,0:T(8,128)(2,1)} %bitcast), calls=%async_computation | async-start | bytes 1048576 | tf_op jit(solution)/shard_map/all_to_all | solution.py:102
  19.4 27.3 %collective-permute-start = (bf16[8,128,256]{2,1,0:T(8,128)(2,1)}, bf16[8,128,256]{2,1,0:T(8,128)(2,1)}, u32[]{:S(2)}, u32[]{:S(2)}) collective-permute-start(bf16[8,128,256]{2,1,0:T(8,128)(2,1)} %get-tuple-element.34), channel_id=1, source_target_pairs={{0,16},{16,32},{32,48},{48,64},{64,80},{80,96},{96,112},{1,17},{17... | collective-permute-start | bytes 1572872 | tf_op jit(solution)/shard_map/ppermute | solution.py:516
  23.4 24.6 %collective-permute-start.1 = (bf16[8,128,256]{2,1,0:T(8,128)(2,1)}, bf16[8,128,256]{2,1,0:T(8,128)(2,1)}, u32[]{:S(2)}, u32[]{:S(2)}) collective-permute-start(bf16[8,128,256]{2,1,0:T(8,128)(2,1)} %get-tuple-element.35), channel_id=1, source_target_pairs={{16,0},{32,16},{48,32},{64,48},{80,64},{96,80},{112,96},{17,1},{33... | collective-permute-start | bytes 1572872 | tf_op jit(solution)/shard_map/ppermute | solution.py:517
  24.7 23.3 %collective-permute-start.2 = (bf16[2,4,128,256]{3,2,1,0:T(8,128)(2,1)}, bf16[2,4,128,256]{3,2,1,0:T(8,128)(2,1)S(1)}, u32[]{:S(2)}, u32[]{:S(2)}) collective-permute-start(bf16[2,4,128,256]{3,2,1,0:T(8,128)(2,1)} %get-tuple-element.36), channel_id=1, source_target_pairs={{0,1},{1,2},{2,3},{3,4},{4,5},{5,6},{6,7},{7,8},{8,9},{9,10},{10,1... | collective-permute-start | bytes 1572872 | tf_op jit(solution)/shard_map/ppermute | solution.py:516
  28.4 19.6 %collective-permute-start.3 = (bf16[2,4,128,256]{3,2,1,0:T(8,128)(2,1)}, bf16[2,4,128,256]{3,2,1,0:T(8,128)(2,1)}, u32[]{:S(2)}, u32[]{:S(2)}) collective-permute-start(bf16[2,4,128,256]{3,2,1,0:T(8,128)(2,1)} %get-tuple-element.37), channel_id=1, source_target_pairs={{1,0},{2,1},{3,2},{4,3},{5,4},{6,5},{7,6},{8,7},{9,8},{10,9},{11,1... | collective-permute-start | bytes 1572872 | tf_op jit(solution)/shard_map/ppermute | solution.py:517
  34.5 22.3 %all-to-all-start.1 = ((bf16[128,16,128]{2,1,0:T(8,128)(2,1)}), bf16[128,16,128]{2,1,0:T(8,128)(2,1)S(1)}, u32[]{:S(2)}, u32[]{:S(2)}) async-start(bf16[128,16,128]{2,1,0:T(8,128)(2,1)} %total.2), calls=%async_computation.1 | async-start | bytes 1048576 | tf_op jit(solution)/shard_map/all_to_all | solution.py:115
  42.6 28.3 %collective-permute-start.4 = (bf16[8,128,256]{2,1,0:T(8,128)(2,1)}, bf16[8,128,256]{2,1,0:T(8,128)(2,1)}, u32[]{:S(2)}, u32[]{:S(2)}) collective-permute-start(bf16[8,128,256]{2,1,0:T(8,128)(2,1)} %get-tuple-element.39), channel_id=1, source_target_pairs={{0,16},{16,32},{32,48},{48,64},{64,80},{80,96},{96,112},{1,17},{17... | collective-permute-start | bytes 1572872 | tf_op jit(solution)/shard_map/ppermute | solution.py:516
  46.7 26.4 %collective-permute-start.5 = (bf16[8,128,256]{2,1,0:T(8,128)(2,1)}, bf16[8,128,256]{2,1,0:T(8,128)(2,1)}, u32[]{:S(2)}, u32[]{:S(2)}) collective-permute-start(bf16[8,128,256]{2,1,0:T(8,128)(2,1)} %get-tuple-element.40), channel_id=1, source_target_pairs={{16,0},{32,16},{48,32},{64,48},{80,64},{96,80},{112,96},{17,1},{33... | collective-permute-start | bytes 1572872 | tf_op jit(solution)/shard_map/ppermute | solution.py:517
  56.8 16.3 %copy-start.1 = (bf16[4,8,128,256]{3,2,1,0:T(8,128)(2,1)S(1)}, bf16[4,8,128,256]{3,2,1,0:T(8,128)(2,1)}, u32[]{:S(2)}) copy-start(bf16[4,8,128,256]{3,2,1,0:T(8,128)(2,1)} %state_ref.3) | copy-start | bytes 6291460
  64.5 19.4 %collective-permute-start.6 = (bf16[8,128,256]{2,1,0:T(8,128)(2,1)S(1)}, bf16[8,128,256]{2,1,0:T(8,128)(2,1)S(1)}, u32[]{:S(2)}, u32[]{:S(2)}) collective-permute-start(bf16[8,128,256]{2,1,0:T(8,128)(2,1)S(1)} %get-tuple-element.48), channel_id=1, source_target_pairs={{0,16},{16,32},{32,48},{48,64},{64,80},{80,96},{96,112},{1,17},{17... | collective-permute-start | bytes 1572872 | tf_op jit(solution)/shard_map/ppermute | solution.py:516
  66.7 17.1 %collective-permute-start.7 = (bf16[8,128,256]{2,1,0:T(8,128)(2,1)S(1)}, bf16[8,128,256]{2,1,0:T(8,128)(2,1)S(1)}, u32[]{:S(2)}, u32[]{:S(2)}) collective-permute-start(bf16[8,128,256]{2,1,0:T(8,128)(2,1)S(1)} %get-tuple-element.49), channel_id=1, source_target_pairs={{16,0},{32,16},{48,32},{64,48},{80,64},{96,80},{112,96},{17,1},{33... | collective-permute-start | bytes 1572872 | tf_op jit(solution)/shard_map/ppermute | solution.py:517
  68.0 15.8 %collective-permute-start.8 = (bf16[4,128,256]{2,1,0:T(8,128)(2,1)S(1)}, bf16[4,128,256]{2,1,0:T(8,128)(2,1)S(1)}, u32[]{:S(2)}, u32[]{:S(2)}) collective-permute-start(bf16[4,128,256]{2,1,0:T(8,128)(2,1)S(1)} %get-tuple-element.50), channel_id=1, source_target_pairs={{0,1},{1,2},{2,3},{3,4},{4,5},{5,6},{6,7},{7,8},{8,9},{9,10},{10,1... | collective-permute-start | bytes 786440 | tf_op jit(solution)/shard_map/ppermute | solution.py:516
  70.9 12.9 %collective-permute-start.9 = (bf16[4,128,256]{2,1,0:T(8,128)(2,1)S(1)}, bf16[4,128,256]{2,1,0:T(8,128)(2,1)S(1)}, u32[]{:S(2)}, u32[]{:S(2)}) collective-permute-start(bf16[4,128,256]{2,1,0:T(8,128)(2,1)S(1)} %get-tuple-element.51), channel_id=1, source_target_pairs={{1,0},{2,1},{3,2},{4,3},{5,4},{6,5},{7,6},{8,7},{9,8},{10,9},{11,1... | collective-permute-start | bytes 786440 | tf_op jit(solution)/shard_map/ppermute | solution.py:517
  120.1 18.1 %all-to-all-start.3 = ((bf16[128,16,128]{2,1,0:T(8,128)(2,1)}), bf16[128,16,128]{2,1,0:T(8,128)(2,1)S(1)}, u32[]{:S(2)}, u32[]{:S(2)}) async-start(bf16[128,16,128]{2,1,0:T(8,128)(2,1)} %total.3), calls=%async_computation.3 | async-start | bytes 1048576 | tf_op jit(solution)/shard_map/all_to_all | solution.py:115
  138.2 0.8 copy-start.6

commit v5 on v4

--- a/solution.py
+++ b/solution.py
@@ -120,51 +120,93 @@
 CELLS = NX * NY
 
 
-def edges_kernel(
-    state_hbm, cot_hbm, mask_ref, xlo_ref, xhi_ref, ylo_ref, yhi_ref, sxlo_ref, sxhi_ref, sem
+def mask_gate(mask_ref):
+    columns = mask_ref[...].reshape(CELLS, NZ).astype(F32).T
+    return lambda r: jnp.broadcast_to(columns[:, r : r + 1], (NZ, R)).astype(BF)
+
+
+def held_x_kernel(cot_hbm, mask_ref, xlo_hbm, xhi_hbm, xlo, xhi, sem, out_sem):
+    ins = [
+        pltpu.make_async_copy(cot_hbm.at[0], xlo, sem.at[0]),
+        pltpu.make_async_copy(cot_hbm.at[NX - 1], xhi, sem.at[1]),
+    ]
+    outs = [
+        pltpu.make_async_copy(xlo, xlo_hbm, out_sem.at[0]),
+        pltpu.make_async_copy(xhi, xhi_hbm, out_sem.at[1]),
+    ]
+    for copy in ins:
+        copy.start()
+    gate = mask_gate(mask_ref)
+    for i, face in enumerate((xlo, xhi)):
+        ins[i].wait()
+        for y in range(NY):
+            face[y] = face[y] * gate(i * (NX - 1) * NY + y)
+        outs[i].start()
+    for copy in outs:
+        copy.wait()
+
+
+def other_faces_kernel(
+    state_hbm, cot_hbm, mask_ref, ylo_hbm, yhi_hbm, sxlo_hbm, sxhi_hbm,
+    ylo, yhi, sxlo, sxhi, sem, out_sem,
 ):
-    copies = [
-        pltpu.make_async_copy(cot_hbm.at[0], xlo_ref, sem.at[0]),
-        pltpu.make_async_copy(cot_hbm.at[NX - 1], xhi_ref, sem.at[1]),
-        pltpu.make_async_copy(cot_hbm.at[:, 0], ylo_ref.at[1], sem.at[2]),
-        pltpu.make_async_copy(cot_hbm.at[:, NY - 1], yhi_ref.at[1], sem.at[3]),
-        pltpu.make_async_copy(state_hbm.at[:, 0], ylo_ref.at[0], sem.at[4]),
-        pltpu.make_async_copy(state_hbm.at[:, NY - 1], yhi_ref.at[0], sem.at[5]),
-        pltpu.make_async_copy(state_hbm.at[0], sxlo_ref, sem.at[6]),
-        pltpu.make_async_copy(state_hbm.at[NX - 1], sxhi_ref, sem.at[7]),
-    ]
-    for copy in copies:
+    ins, outs = [], []
+    for i, (y, face) in enumerate(((0, ylo), (NY - 1, yhi))):
+        ins.append(pltpu.make_async_copy(cot_hbm.at[:, y], face.at[1], sem.at[2 * i]))
+        ins.append(pltpu.make_async_copy(state_hbm.at[:, y], face.at[0], sem.at[2 * i + 1]))
+        outs.append(pltpu.make_async_copy(face, (ylo_hbm, yhi_hbm)[i], out_sem.at[i]))
+    for i, (x, face) in enumerate(((0, sxlo), (NX - 1, sxhi))):
+        ins.append(pltpu.make_async_copy(state_hbm.at[x], face, sem.at[4 + i]))
+        outs.append(pltpu.make_async_copy(face, (sxlo_hbm, sxhi_hbm)[i], out_sem.at[2 + i]))
+    for copy in ins:
         copy.start()
-    columns = mask_ref[...].reshape(CELLS, NZ).astype(F32).T
-
-    def gate(r):
-        return jnp.broadcast_to(columns[:, r : r + 1], (NZ, R)).astype(BF)
-
-    for copy in copies:
+    gate = mask_gate(mask_ref)
+    for i, face in enumerate((ylo, yhi)):
+        ins[2 * i].wait()
+        ins[2 * i + 1].wait()
+        for x in range(NX):
+            face[1, x] = face[1, x] * gate(x * NY + i * (NY - 1))
+        outs[i].start()
+    for i in range(2):
+        ins[4 + i].wait()
+        outs[2 + i].start()
+    for copy in outs:
         copy.wait()
-    for y in range(NY):
-        xlo_ref[y] = xlo_ref[y] * gate(y)
-        xhi_ref[y] = xhi_ref[y] * gate((NX - 1) * NY + y)
-    for x in range(NX):
-        ylo_ref[1, x] = ylo_ref[1, x] * gate(x * NY)
-        yhi_ref[1, x] = yhi_ref[1, x] * gate(x * NY + NY - 1)
 
 
 x_face = jax.ShapeDtypeStruct((NY, NZ, R), BF)
 y_face = jax.ShapeDtypeStruct((NX, NZ, R), BF)
-y_faces = jax.ShapeDtypeStruct((2, NX, NZ, R), BF)
-
-
-def edges(state, cotangent, mask):
-    return pl.pallas_call(
-        edges_kernel,
-        out_shape=(x_face, x_face, y_faces, y_faces, x_face, x_face),
+two_y_faces = jax.ShapeDtypeStruct((2, NX, NZ, R), BF)
+
+
+def held_x_faces(cotangent, mask):
+    face = pltpu.VMEM((NY, NZ, R), BF)
+    sems = pltpu.SemaphoreType.DMA((2,))
+    return pl.pallas_call(
+        held_x_kernel,
+        out_shape=(x_face, x_face),
+        in_specs=[hbm, whole],
+        out_specs=(hbm, hbm),
+        scratch_shapes=[face, face, sems, sems],
+        compiler_params=params(56),
+        cost_estimate=cost(1 << 20, 2 << 20),
+        name="held_x_faces",
+    )(cotangent, mask)
+
+
+def other_faces(state, cotangent, mask):
+    x, y = pltpu.VMEM((NY, NZ, R), BF), pltpu.VMEM((2, NX, NZ, R), BF)
+    return pl.pallas_call(
+        other_faces_kernel,
+        out_shape=(two_y_faces, two_y_faces, x_face, x_face),
         in_specs=[hbm, hbm, whole],
-        out_specs=(whole,) * 6,
-        scratch_shapes=[pltpu.SemaphoreType.DMA((8,))],
+        out_specs=(hbm,) * 4,
+        scratch_shapes=[
+            y, y, x, x, pltpu.SemaphoreType.DMA((6,)), pltpu.SemaphoreType.DMA((4,)),
+        ],
         compiler_params=params(56),
-        cost_estimate=cost(1 << 20, 6 << 20),
-        name="edges",
+        cost_estimate=cost(1 << 20, 4 << 20),
+        name="other_faces",
     )(state, cotangent, mask)
 
 
@@ -503,7 +545,7 @@
         in_specs=[constant((2048, 128)), pl.BlockSpec((CHUNK, 1536), lambda i: (i, 0))],
         out_specs=pl.BlockSpec((CHUNK, R), lambda i: (i, 0)),
         scratch_shapes=[pltpu.VMEM((1536, 256), BF)],
-        compiler_params=params(56),
+        compiler_params=params(58),
         cost_estimate=cost(2 * 2048 * 256 * 1536, 8 << 20),
         name="final",
     )(packed, weighted)
@@ -526,10 +568,10 @@
 
 
 def on_device(state, cotangent, factors, speeds, signs, mask):
-    hxlo, hxhi, ylo, yhi, sxlo, sxhi = edges(state, cotangent, mask)
-    speeds, hxlo, hxhi = lax.optimization_barrier((speeds, hxlo, hxhi))
+    hxlo, hxhi = held_x_faces(cotangent, mask)
     held_x = shift("gx", hxlo, hxhi)
     copies = scatter_sum(gram(factors, speeds, signs))
+    ylo, yhi, sxlo, sxhi = other_faces(state, cotangent, mask)
     y_halos = shift(Y_AXES, ylo, yhi)
     copies, sxlo, sxhi = lax.optimization_barrier((copies, sxlo, sxhi))
     state_x = shift("gx", sxlo, sxhi)
@@ -547,7 +589,7 @@
     sums = scatter_sum(partial)
     weighted = weigh(factors, speeds, signs)
     symmetric = gather(sums)
-    grad_factors = final_step(symmetric, weighted)
+    grad_factors = final_step(near(symmetric), weighted)
     return (grad_state, grad_factors)
 
 

time: 146 us -> 150 us (1.027)
  starting transfers between devices: 48.3 us -> 51.6 us
  waiting for transfers between devices: 20.7 us -> 17.5 us
  local copies, waits for them, and re-layouts: 0.83 us -> 2.75 us
  Pallas kernels: 49.5 us -> 51.1 us
    all_to_all x2, starting transfers between devices: 12 us -> 15.5 us  [gather(): lax.all_to_all(copies, ALL, split_axis=0, concat_axis=0, tiled=True)]
    all_to_all x1, waiting for transfers between devices: 3.19 us -> 0.01 us  [scatter_sum(): mine = lax.all_to_all(pieces, ALL, split_axis=0, concat_axis=0, tiled=True)]
    unnamed x14 -> x12, local copies, waits for them, and re-layouts: 0.83 us -> 2.75 us
    pallas_call x1 -> x2, Pallas kernels: 4.45 us -> 6.17 us  [the longest x1 3.27 us: other_faces(): pl.pallas_call(other_faces_kernel, out_shape=(two_y_faces, two_y_faces, x...]
  transfers between devices with their start and end apart: 13 -> 13, of which waited for: 3 -> 2; matrix products, arithmetic and copies ran while one was open for 0% -> 0% of each run, Pallas kernels for 17% -> 21%
where the time goes in v5:
time: 150 us; the launch traced here: 149 us
  starting transfers between devices  51.6 us (34%)
  Pallas kernels  51.1 us (34%)
  blocking collectives  24.9 us (17%)
  waiting for transfers between devices  17.5 us (12%)
  local copies, waits for them, and re-layouts  2.75 us (2%)
    all_to_all x1, blocking collectives, scatter_sum(): mine = lax.all_to_all(pieces, ALL, split_axis=0, concat_axis=0, tiled=True)  24.9 us
    all_to_all x2, waiting for transfers between devices, gather(): lax.all_to_all(copies, ALL, split_axis=0, concat_axis=0, tiled=True)  17.4 us
    ppermute x5, starting transfers between devices, shift(): from_below = lax.ppermute(hi, axis, forward)  16.6 us
    all_to_all x2, starting transfers between devices, gather(): lax.all_to_all(copies, ALL, split_axis=0, concat_axis=0, tiled=True)  15.5 us
    all_to_all x1, starting transfers between devices, scatter_sum(): mine = lax.all_to_all(pieces, ALL, split_axis=0, concat_axis=0, tiled=True)  11.5 us
    pallas_call x1, Pallas kernels, middle_step(): pl.pallas_call(middle_kernel, out_shape=pltpu.VMEM((256, 1536), F32), in_...  10.7 us
    pallas_call x1, Pallas kernels, last_step(): pl.pallas_call(last_kernel, out_shape=(jax.ShapeDtypeStruct((2048, 128),...  10.4 us
    ppermute x5, starting transfers between devices, shift(): from_above = lax.ppermute(lo, axis, backward)  8.01 us
  transfers between devices with their start and end apart: 13, of which 2 were waited for; matrix products, arithmetic and copies ran while one was open for 0% of the time, Pallas kernels for 21%

profile of v5, /device:TPU:1, one launch (start us, length us, event | category | flops | bytes accessed | tf_op | source)
XLA Modules:
  0.0 148.7 jit_solution(1881857090741254873)
XLA Ops:
  0.6 0.0 copy-start.2
  0.6 1.2 copy-done.2
  1.9 0.0 copy-start.4
  1.9 0.8 copy-done.4
  2.6 0.0 copy-start.5
  2.6 0.8 copy-done.5
  3.4 2.7 %gram.1 = bf16[2048,128]{1,0:T(8,128)(2,1)} custom-call(bf16[2048,256]{1,0:T(8,128)(2,1)S(1)} %copy-done.2, f32[3,2048]{1,0:T(4,128)S(1)} %copy-done.4, s32[3,2048]{1,0:T(4,128)S(1)} %copy-done.5), custom_call_target="tpu_custom_call" | custom-call | flops 1610612736 | bytes 2097152 | tf_op jit(solution)/shard_map/gram/pallas_call | solution.py:83
  6.1 11.5 %all-to-all-start = ((bf16[128,16,128]{2,1,0:T(8,128)(2,1)}), bf16[128,16,128]{2,1,0:T(8,128)(2,1)S(1)}, u32[]{:S(2)}, u32[]{:S(2)}) async-start(bf16[128,16,128]{2,1,0:T(8,128)(2,1)} %bitcast), calls=%async_computation | async-start | bytes 1048576 | tf_op jit(solution)/shard_map/all_to_all | solution.py:102
  17.6 3.3 %other_faces.1 = (bf16[2,4,128,256]{3,2,1,0:T(8,128)(2,1)}, bf16[2,4,128,256]{3,2,1,0:T(8,128)(2,1)}, bf16[8,128,256]{2,1,0:T(8,128)(2,1)}, bf16[8,128,256]{2,1,0:T(8,128)(2,1)}) custom-call(bf16[4,8,128,256]{3,2,1,0:T(8,128)(2,1)} %state_ref.3, bf16[4,8,128,256]{3,2,1,0:T(8,128)(2,1)} %cot_ref.1, s32[4,8,128]{2,1,0:T(8,128)} %mask_ref.7), custom_call_target="tpu_custom_call" | custom-call | flops 1048576 | bytes 4194304 | tf_op jit(solution)/shard_map/other_faces/pallas_call | solution.py:199
  20.9 3.5 %collective-permute-start.2 = (bf16[2,4,128,256]{3,2,1,0:T(8,128)(2,1)}, bf16[2,4,128,256]{3,2,1,0:T(8,128)(2,1)S(1)}, u32[]{:S(2)}, u32[]{:S(2)}) collective-permute-start(bf16[2,4,128,256]{3,2,1,0:T(8,128)(2,1)} %get-tuple-element.30), channel_id=1, source_target_pairs={{0,1},{1,2},{2,3},{3,4},{4,5},{5,6},{6,7},{7,8},{8,9},{9,10},{10,1... | collective-permute-start | bytes 1572872 | tf_op jit(solution)/shard_map/ppermute | solution.py:558
  24.4 0.0 copy-start
  24.4 0.0 copy-start.3
  24.4 2.1 %collective-permute-start.3 = (bf16[2,4,128,256]{3,2,1,0:T(8,128)(2,1)}, bf16[2,4,128,256]{3,2,1,0:T(8,128)(2,1)}, u32[]{:S(2)}, u32[]{:S(2)}) collective-permute-start(bf16[2,4,128,256]{3,2,1,0:T(8,128)(2,1)} %get-tuple-element.31), channel_id=1, source_target_pairs={{1,0},{2,1},{3,2},{4,3},{5,4},{6,5},{7,6},{8,7},{9,8},{10,9},{11,1... | collective-permute-start | bytes 1572872 | tf_op jit(solution)/shard_map/ppermute | solution.py:559
  26.5 2.9 %held_x_faces.1 = (bf16[8,128,256]{2,1,0:T(8,128)(2,1)}, bf16[8,128,256]{2,1,0:T(8,128)(2,1)}) custom-call(bf16[4,8,128,256]{3,2,1,0:T(8,128)(2,1)} %cot_ref.1, s32[4,8,128]{2,1,0:T(8,128)} %mask_ref.7), custom_call_target="tpu_custom_call" | custom-call | flops 1048576 | bytes 2097152 | tf_op jit(solution)/shard_map/held_x_faces/pallas_call | solution.py:185
  29.4 3.9 %collective-permute-start = (bf16[8,128,256]{2,1,0:T(8,128)(2,1)}, bf16[8,128,256]{2,1,0:T(8,128)(2,1)}, u32[]{:S(2)}, u32[]{:S(2)}) collective-permute-start(bf16[8,128,256]{2,1,0:T(8,128)(2,1)} %get-tuple-element.28), channel_id=1, source_target_pairs={{0,16},{16,32},{32,48},{48,64},{64,80},{80,96},{96,112},{1,17},{17... | collective-permute-start | bytes 1572872 | tf_op jit(solution)/shard_map/ppermute | solution.py:558
  33.3 1.3 collective-permute-start.1
  34.6 0.0 all-to-all-done.parts_ref
  34.6 1.0 total.2
  35.5 11.6 %all-to-all-start.1 = ((bf16[128,16,128]{2,1,0:T(8,128)(2,1)}), bf16[128,16,128]{2,1,0:T(8,128)(2,1)S(1)}, u32[]{:S(2)}, u32[]{:S(2)}) async-start(bf16[128,16,128]{2,1,0:T(8,128)(2,1)} %total.2), calls=%async_computation.1 | async-start | bytes 1048576 | tf_op jit(solution)/shard_map/all_to_all | solution.py:115
  47.2 4.1 %collective-permute-start.4 = (bf16[8,128,256]{2,1,0:T(8,128)(2,1)}, bf16[8,128,256]{2,1,0:T(8,128)(2,1)}, u32[]{:S(2)}, u32[]{:S(2)}) collective-permute-start(bf16[8,128,256]{2,1,0:T(8,128)(2,1)} %get-tuple-element.33), channel_id=1, source_target_pairs={{0,16},{16,32},{32,48},{48,64},{64,80},{80,96},{96,112},{1,17},{17... | collective-permute-start | bytes 1572872 | tf_op jit(solution)/shard_map/ppermute | solution.py:558
  51.2 0.0 collective-permute-done.2.ylo_hbm.ylo
  51.2 1.3 collective-permute-start.5
  52.5 0.0 collective-permute-done.3.yhi_hbm.yhi
  52.5 0.0 collective-permute-done.xlo_hbm
  52.6 0.0 collective-permute-done.1.xhi_hbm
  52.6 8.7 %all-to-all-done.1 = bf16[128,16,128]{2,1,0:T(8,128)(2,1)S(1)} async-done(((bf16[128,16,128]{2,1,0:T(8,128)(2,1)}), bf16[128,16,128]{2,1,0:T(8,128)(2,1)S(1)}, u32[]{:S(2)}, u32[]{:S(2)}) %all-to-all-start.1) | async-done | bytes 524320 | tf_op jit(solution)/shard_map/all_to_all | solution.py:115
  61.3 0.0 copy-done
  61.3 0.0 copy-done.3
  61.3 7.7 %inner.1 = (bf16[4,8,128,256]{3,2,1,0:T(8,128)(2,1)S(1)}, f32[4,8,128,256]{3,2,1,0:T(8,128)S(1)}, bf16[8,128,256]{2,1,0:T(8,128)(2,1)S(1)}, bf16[8,128,256]{2,1,...) custom-call(bf16[2048,128]{1,0:T(8,128)(2,1)S(1)} %bitcast.5, ...), custom_call_target="tpu_custom_call" | custom-call | flops 3221225472 | bytes 14680064 | tf_op jit(solution)/shard_map/inner/pallas_call | solution.py:370
  69.0 2.3 %collective-permute-start.6 = (bf16[8,128,256]{2,1,0:T(8,128)(2,1)S(1)}, bf16[8,128,256]{2,1,0:T(8,128)(2,1)S(1)}, u32[]{:S(2)}, u32[]{:S(2)}) collective-permute-start(bf16[8,128,256]{2,1,0:T(8,128)(2,1)S(1)} %get-tuple-element.42), channel_id=1, source_target_pairs={{0,16},{16,32},{32,48},{48,64},{64,80},{80,96},{96,112},{1,17},{17... | collective-permute-start | bytes 1572872 | tf_op jit(solution)/shard_map/ppermute | solution.py:558
  71.3 1.3 collective-permute-start.7
  72.6 2.9 %collective-permute-start.8 = (bf16[4,128,256]{2,1,0:T(8,128)(2,1)S(1)}, bf16[4,128,256]{2,1,0:T(8,128)(2,1)S(1)}, u32[]{:S(2)}, u32[]{:S(2)}) collective-permute-start(bf16[4,128,256]{2,1,0:T(8,128)(2,1)S(1)} %get-tuple-element.44), channel_id=1, source_target_pairs={{0,1},{1,2},{2,3},{3,4},{4,5},{5,6},{6,7},{7,8},{8,9},{9,10},{10,1... | collective-permute-start | bytes 786440 | tf_op jit(solution)/shard_map/ppermute | solution.py:558
  75.5 0.0 collective-permute-done.4.sxlo
  75.5 2.1 %collective-permute-start.9 = (bf16[4,128,256]{2,1,0:T(8,128)(2,1)S(1)}, bf16[4,128,256]{2,1,0:T(8,128)(2,1)S(1)}, u32[]{:S(2)}, u32[]{:S(2)}) collective-permute-start(bf16[4,128,256]{2,1,0:T(8,128)(2,1)S(1)} %get-tuple-element.45), channel_id=1, source_target_pairs={{1,0},{2,1},{3,2},{4,3},{5,4},{6,5},{7,6},{8,7},{9,8},{10,9},{11,1... | collective-permute-start | bytes 786440 | tf_op jit(solution)/shard_map/ppermute | solution.py:559
  77.6 0.0 collective-permute-done.5.sxhi
  77.6 0.0 copy-done.1
  77.6 10.7 %middle.1.held_grads_ref = f32[256,1536]{1,0:T(8,128)S(1)} custom-call(bf16[1536,256]{1,0:T(8,128)(2,1)S(1)} %get-tuple-element.32.flow_ref, s32[4,8,128]{2,1,0:T(8,128)S(1)} %copy-done.3, bf16[4,8,128,256]{3,2,1,0:T(8,128)(2,1)S(1)} %copy-done.1, bf16[8,128,256]{2,1,0:T(8,128)(2,1)} %collective-permute-done.4.sxlo, ...), custom_call_target="tpu_custom_call" | custom-call | flops 6442450944 | bytes 4194304 | tf_op jit(solution)/shard_map/middle/pallas_call | solution.py:422
  88.4 0.0 collective-permute-done.8.ylo_hbm
  88.4 0.0 collective-permute-done.9.yhi_hbm
  88.4 0.0 collective-permute-done.6.xlo_hbm
  88.4 0.0 collective-permute-done.7.xhi_hbm
  88.4 10.4 %last.1 = (bf16[2048,128]{1,0:T(8,128)(2,1)S(1)}, bf16[4,8,128,256]{3,2,1,0:T(8,128)(2,1)}) custom-call(f32[256,1536]{1,0:T(8,128)S(1)} %middle.1.held_grads_ref, bf16[4,8,128,256]{3,2,1,0:T(8,128)(2,1)S(1)} %copy-done.1, bf16[4,8,128,256]{3,2,1,0:T(8,128)(2,1)S(1)} %get-tuple-element.39.hi_ref, bf16[1536,256]{1,0:T(8,128)(2,1)S(1)} %get-tuple-element.40.back_ref, ...), custom_call_target="tpu_custom_call" | custom-call | flops 6442450944 | bytes 5242880 | tf_op jit(solution)/shard_map/last/pallas_call | solution.py:474
  98.8 24.9 %all_to_all.20.parts_ref = bf16[128,16,128]{2,1,0:T(8,128)(2,1)S(1)} all-to-all(bf16[128,16,128]{2,1,0:T(8,128)(2,1)S(1)} %bitcast.6), channel_id=1, replica_groups=mesh['gx'=8,'gy'=8,'gz'=2] {'gx','gy','gz'}, dimensions={0} | all-to-all | bytes 1048576 | tf_op jit(solution)/shard_map/all_to_all | solution.py:102
  123.6 1.0 total.3
  124.6 3.9 %all-to-all-start.3 = ((bf16[128,16,128]{2,1,0:T(8,128)(2,1)}), bf16[128,16,128]{2,1,0:T(8,128)(2,1)S(1)}, u32[]{:S(2)}, u32[]{:S(2)}) async-start(bf16[128,16,128]{2,1,0:T(8,128)(2,1)} %total.3), calls=%async_computation.3 | async-start | bytes 1048576 | tf_op jit(solution)/shard_map/all_to_all | solution.py:115
  128.5 5.5 %weigh.1.weighted_ref = bf16[2048,1536]{1,0:T(8,128)(2,1)} custom-call(bf16[2048,256]{1,0:T(8,128)(2,1)} %factors_ref.3, f32[3,2048]{1,0:T(4,128)} %speeds_ref.3, s32[3,2048]{1,0:T(4,128)} %signs_ref.3), custom_call_target="tpu_custom_call" | custom-call | flops 3145728 | bytes 8388608 | tf_op jit(solution)/shard_map/weigh/pallas_call | solution.py:505
  134.0 8.7 %all-to-all-done.3 = bf16[128,16,128]{2,1,0:T(8,128)(2,1)S(1)} async-done(((bf16[128,16,128]{2,1,0:T(8,128)(2,1)}), bf16[128,16,128]{2,1,0:T(8,128)(2,1)S(1)}, u32[]{:S(2)}, u32[]{:S(2)}) %all-to-all-start.3) | async-done | bytes 524320 | tf_op jit(solution)/shard_map/all_to_all | solution.py:115
  142.7 5.9 %final.1 = f32[2048,256]{1,0:T(8,128)} custom-call(bf16[2048,128]{1,0:T(8,128)(2,1)S(1)} %bitcast.4, bf16[2048,1536]{1,0:T(8,128)(2,1)} %weigh.1.weighted_ref), custom_call_target="tpu_custom_call" | custom-call | flops 1610612736 | bytes 8388608 | tf_op jit(solution)/shard_map/final/pallas_call | solution.py:541
  (1 shorter events, 0.0 us)
Async XLA Ops:
  0.6 1.2 copy-start.2
  1.9 0.8 copy-start.4
  2.6 0.8 copy-start.5
  6.1 28.5 %all-to-all-start = ((bf16[128,16,128]{2,1,0:T(8,128)(2,1)}), bf16[128,16,128]{2,1,0:T(8,128)(2,1)S(1)}, u32[]{:S(2)}, u32[]{:S(2)}) async-start(bf16[128,16,128]{2,1,0:T(8,128)(2,1)} %bitcast), calls=%async_computation | async-start | bytes 1048576 | tf_op jit(solution)/shard_map/all_to_all | solution.py:102
  20.9 30.4 %collective-permute-start.2 = (bf16[2,4,128,256]{3,2,1,0:T(8,128)(2,1)}, bf16[2,4,128,256]{3,2,1,0:T(8,128)(2,1)S(1)}, u32[]{:S(2)}, u32[]{:S(2)}) collective-permute-start(bf16[2,4,128,256]{3,2,1,0:T(8,128)(2,1)} %get-tuple-element.30), channel_id=1, source_target_pairs={{0,1},{1,2},{2,3},{3,4},{4,5},{5,6},{6,7},{7,8},{8,9},{9,10},{10,1... | collective-permute-start | bytes 1572872 | tf_op jit(solution)/shard_map/ppermute | solution.py:558
  24.4 36.9 %copy-start = (bf16[4,8,128,256]{3,2,1,0:T(8,128)(2,1)S(1)}, bf16[4,8,128,256]{3,2,1,0:T(8,128)(2,1)}, u32[]{:S(2)}) copy-start(bf16[4,8,128,256]{3,2,1,0:T(8,128)(2,1)} %cot_ref.1) | copy-start | bytes 6291460
  24.4 36.9 %copy-start.3 = (s32[4,8,128]{2,1,0:T(8,128)S(1)}, s32[4,8,128]{2,1,0:T(8,128)}, u32[]{:S(2)}) copy-start(s32[4,8,128]{2,1,0:T(8,128)} %mask_ref.7) | copy-start | bytes 49156
  24.4 28.1 %collective-permute-start.3 = (bf16[2,4,128,256]{3,2,1,0:T(8,128)(2,1)}, bf16[2,4,128,256]{3,2,1,0:T(8,128)(2,1)}, u32[]{:S(2)}, u32[]{:S(2)}) collective-permute-start(bf16[2,4,128,256]{3,2,1,0:T(8,128)(2,1)} %get-tuple-element.31), channel_id=1, source_target_pairs={{1,0},{2,1},{3,2},{4,3},{5,4},{6,5},{7,6},{8,7},{9,8},{10,9},{11,1... | collective-permute-start | bytes 1572872 | tf_op jit(solution)/shard_map/ppermute | solution.py:559
  29.4 23.1 %collective-permute-start = (bf16[8,128,256]{2,1,0:T(8,128)(2,1)}, bf16[8,128,256]{2,1,0:T(8,128)(2,1)}, u32[]{:S(2)}, u32[]{:S(2)}) collective-permute-start(bf16[8,128,256]{2,1,0:T(8,128)(2,1)} %get-tuple-element.28), channel_id=1, source_target_pairs={{0,16},{16,32},{32,48},{48,64},{64,80},{80,96},{96,112},{1,17},{17... | collective-permute-start | bytes 1572872 | tf_op jit(solution)/shard_map/ppermute | solution.py:558
  33.3 19.3 %collective-permute-start.1 = (bf16[8,128,256]{2,1,0:T(8,128)(2,1)}, bf16[8,128,256]{2,1,0:T(8,128)(2,1)}, u32[]{:S(2)}, u32[]{:S(2)}) collective-permute-start(bf16[8,128,256]{2,1,0:T(8,128)(2,1)} %get-tuple-element.29), channel_id=1, source_target_pairs={{16,0},{32,16},{48,32},{64,48},{80,64},{96,80},{112,96},{17,1},{33... | collective-permute-start | bytes 1572872 | tf_op jit(solution)/shard_map/ppermute | solution.py:559
  35.5 25.8 %all-to-all-start.1 = ((bf16[128,16,128]{2,1,0:T(8,128)(2,1)}), bf16[128,16,128]{2,1,0:T(8,128)(2,1)S(1)}, u32[]{:S(2)}, u32[]{:S(2)}) async-start(bf16[128,16,128]{2,1,0:T(8,128)(2,1)} %total.2), calls=%async_computation.1 | async-start | bytes 1048576 | tf_op jit(solution)/shard_map/all_to_all | solution.py:115
  47.2 28.3 %collective-permute-start.4 = (bf16[8,128,256]{2,1,0:T(8,128)(2,1)}, bf16[8,128,256]{2,1,0:T(8,128)(2,1)}, u32[]{:S(2)}, u32[]{:S(2)}) collective-permute-start(bf16[8,128,256]{2,1,0:T(8,128)(2,1)} %get-tuple-element.33), channel_id=1, source_target_pairs={{0,16},{16,32},{32,48},{48,64},{64,80},{80,96},{96,112},{1,17},{17... | collective-permute-start | bytes 1572872 | tf_op jit(solution)/shard_map/ppermute | solution.py:558
  51.2 26.4 %collective-permute-start.5 = (bf16[8,128,256]{2,1,0:T(8,128)(2,1)}, bf16[8,128,256]{2,1,0:T(8,128)(2,1)}, u32[]{:S(2)}, u32[]{:S(2)}) collective-permute-start(bf16[8,128,256]{2,1,0:T(8,128)(2,1)} %get-tuple-element.34), channel_id=1, source_target_pairs={{16,0},{32,16},{48,32},{64,48},{80,64},{96,80},{112,96},{17,1},{33... | collective-permute-start | bytes 1572872 | tf_op jit(solution)/shard_map/ppermute | solution.py:559
  61.3 16.3 %copy-start.1 = (bf16[4,8,128,256]{3,2,1,0:T(8,128)(2,1)S(1)}, bf16[4,8,128,256]{3,2,1,0:T(8,128)(2,1)}, u32[]{:S(2)}) copy-start(bf16[4,8,128,256]{3,2,1,0:T(8,128)(2,1)} %state_ref.3) | copy-start | bytes 6291460
  69.0 19.4 %collective-permute-start.6 = (bf16[8,128,256]{2,1,0:T(8,128)(2,1)S(1)}, bf16[8,128,256]{2,1,0:T(8,128)(2,1)S(1)}, u32[]{:S(2)}, u32[]{:S(2)}) collective-permute-start(bf16[8,128,256]{2,1,0:T(8,128)(2,1)S(1)} %get-tuple-element.42), channel_id=1, source_target_pairs={{0,16},{16,32},{32,48},{48,64},{64,80},{80,96},{96,112},{1,17},{17... | collective-permute-start | bytes 1572872 | tf_op jit(solution)/shard_map/ppermute | solution.py:558
  71.3 17.1 %collective-permute-start.7 = (bf16[8,128,256]{2,1,0:T(8,128)(2,1)S(1)}, bf16[8,128,256]{2,1,0:T(8,128)(2,1)S(1)}, u32[]{:S(2)}, u32[]{:S(2)}) collective-permute-start(bf16[8,128,256]{2,1,0:T(8,128)(2,1)S(1)} %get-tuple-element.43), channel_id=1, source_target_pairs={{16,0},{32,16},{48,32},{64,48},{80,64},{96,80},{112,96},{17,1},{33... | collective-permute-start | bytes 1572872 | tf_op jit(solution)/shard_map/ppermute | solution.py:559
  72.6 15.8 %collective-permute-start.8 = (bf16[4,128,256]{2,1,0:T(8,128)(2,1)S(1)}, bf16[4,128,256]{2,1,0:T(8,128)(2,1)S(1)}, u32[]{:S(2)}, u32[]{:S(2)}) collective-permute-start(bf16[4,128,256]{2,1,0:T(8,128)(2,1)S(1)} %get-tuple-element.44), channel_id=1, source_target_pairs={{0,1},{1,2},{2,3},{3,4},{4,5},{5,6},{6,7},{7,8},{8,9},{9,10},{10,1... | collective-permute-start | bytes 786440 | tf_op jit(solution)/shard_map/ppermute | solution.py:558
  75.5 12.9 %collective-permute-start.9 = (bf16[4,128,256]{2,1,0:T(8,128)(2,1)S(1)}, bf16[4,128,256]{2,1,0:T(8,128)(2,1)S(1)}, u32[]{:S(2)}, u32[]{:S(2)}) collective-permute-start(bf16[4,128,256]{2,1,0:T(8,128)(2,1)S(1)} %get-tuple-element.45), channel_id=1, source_target_pairs={{1,0},{2,1},{3,2},{4,3},{5,4},{6,5},{7,6},{8,7},{9,8},{10,9},{11,1... | collective-permute-start | bytes 786440 | tf_op jit(solution)/shard_map/ppermute | solution.py:559
  124.6 18.1 %all-to-all-start.3 = ((bf16[128,16,128]{2,1,0:T(8,128)(2,1)}), bf16[128,16,128]{2,1,0:T(8,128)(2,1)S(1)}, u32[]{:S(2)}, u32[]{:S(2)}) async-start(bf16[128,16,128]{2,1,0:T(8,128)(2,1)} %total.3), calls=%async_computation.3 | async-start | bytes 1048576 | tf_op jit(solution)/shard_map/all_to_all | solution.py:115
